TPU v7x, 32 devices: a whole 2x2x4 slice. The times are simulated.
32 devices in a mesh: enc: 2 (over core), dp: 16 (over z, y, x).
Axes of the slice: x: 2, y: 2, z: 4, core: 2. Of those that a mesh axis runs over, the one named last changes fastest.
Arguments:
- text_in: bfloat16 [16384, 768], P(('enc', 'dp')), may hold values from -6 to 6
- text_lengths: int32 [32, 5], P(('enc', 'dp')), may hold values from 1 to 256, 512 in all within a row
- region_feats: bfloat16 [4096, 2048], P(('enc', 'dp')), may hold values from -6 to 6
- region_boxes: float32 [4, 4096], P(None, ('enc', 'dp')), may hold values from 0 to 1
- region_dest: int32 [4096, 1], P(('enc', 'dp')), may hold values from 0 to 15; in each aligned block of 128 rows (0 to 127, 128 to 255, ...) at most 16 rows name the same one
- region_seq: int32 [4096], P(('enc', 'dp')), may hold values from 0 to 4
- w_region: bfloat16 [2048, 768], replicated, may hold values from -0.125 to 0.125
- w_box: float32 [4, 768], replicated, may hold values from -3 to 3
- type_embed: float32 [768], replicated, may hold values from -3 to 3
- region_gain: float32 [768], replicated, may hold values from 0.5 to 1.5
- region_shift: float32 [768], replicated, may hold values from -1.2 to 1.2
- w_qkv: bfloat16 [768, 2304], replicated, may hold values from -0.21875 to 0.21875
- q_bias: float32 [768], replicated, may hold values from -3 to 3
- v_bias: float32 [768], replicated, may hold values from -1.8 to 1.8
- w_out: bfloat16 [768, 768], replicated, may hold values from -0.875 to 0.875
- out_bias: float32 [768], replicated, may hold values from -1.2 to 1.2
- attn_gain: float32 [768], replicated, may hold values from 0.5 to 1.5
- attn_shift: float32 [768], replicated, may hold values from -1.2 to 1.2
- w_up: bfloat16 [768, 3072], replicated, may hold values from -0.21875 to 0.21875
- up_bias: float32 [3072], replicated, may hold values from -1.8 to 1.8
- w_down: bfloat16 [3072, 768], replicated, may hold values from -0.109375 to 0.109375
- down_bias: float32 [768], replicated, may hold values from -1.2 to 1.2
- ffn_gain: float32 [768], replicated, may hold values from 0.5 to 1.5
- ffn_shift: float32 [768], replicated, may hold values from -1.2 to 1.2
- cot_text: bfloat16 [16384, 768], P(('enc', 'dp')), may hold values from -6 to 6
- cot_region: bfloat16 [4096, 768], P(('enc', 'dp')), may hold values from -6 to 6
Outputs:
- text_out: bfloat16 [16384, 768], P(('enc', 'dp'))
- region_out: bfloat16 [4096, 768], P(('enc', 'dp'))
- text_grad: bfloat16 [16384, 768], P(('enc', 'dp'))
- feats_grad: bfloat16 [4096, 2048], P(('enc', 'dp'))
- w_region_grad: float32 [2048, 768], P(None, ('enc', 'dp'))
- w_box_grad: float32 [4, 768], P(None, ('enc', 'dp'))
- type_grad: float32 [768], P(('enc', 'dp'))
- region_gain_grad: float32 [768], P(('enc', 'dp'))
- region_shift_grad: float32 [768], P(('enc', 'dp'))
- w_qkv_grad: float32 [768, 2304], P(('enc', 'dp'))
- q_bias_grad: float32 [768], P(('enc', 'dp'))
- v_bias_grad: float32 [768], P(('enc', 'dp'))
- w_out_grad: float32 [768, 768], P(('enc', 'dp'))
- out_bias_grad: float32 [768], P(('enc', 'dp'))
- attn_gain_grad: float32 [768], P(('enc', 'dp'))
- attn_shift_grad: float32 [768], P(('enc', 'dp'))
- w_up_grad: float32 [768, 3072], P(('enc', 'dp'))
- up_bias_grad: float32 [3072], P(('enc', 'dp'))
- w_down_grad: float32 [3072, 768], P(('enc', 'dp'))
- down_bias_grad: float32 [768], P(('enc', 'dp'))
- ffn_gain_grad: float32 [768], P(('enc', 'dp'))
- ffn_shift_grad: float32 [768], P(('enc', 'dp'))
Inputs may be any that keep to these rules, and one draw needn't show every extreme that they name: `text_lengths`: each row lists the text lengths of one device's 5 sequences and sums to 512. `region_dest`: A destination in the source's own enc group; of the 128 rows of one device at most 16 name the same destination.
All inputs are finite; a program needn't handle non-finite values.
Results may differ from a plain program's by a relative error of at most 0.017.
Values may be sent and summed in bfloat16 or wider, within the bound.
No kernel may reach another device: no remote copies, remote signals or barrier semaphores. Data moves between devices by JAX's collectives and lax.ppermute only.
A program may use at most 256 MiB of HBM per device.

v0:
```python
import functools
import math

import jax
import jax.numpy as jnp
from jax import lax
from jax.experimental import pallas as pl
from jax.experimental.pallas import tpu as pltpu
from jax.sharding import PartitionSpec as P

D = 768
HEADS = 12
HDIM = 64
PAIR = 2 * HDIM
PAIRS = HEADS // 2
TAGS = 128
VECS = 128

F32 = jnp.float32
BF16 = jnp.bfloat16
eps = 1e-05
SCALE = HDIM ** (-0.5)

TAIL_RATE = 0.3275911 * 0.7071067811865476
TAIL = (0.254829592, -0.284496736, 1.421413741, -1.453152027, 1.061405429)


def dot_nn(left, right):
    return lax.dot_general(left, right, (((1,), (0,)), ((), ())), preferred_element_type=F32)


def dot_nt(left, right):
    return lax.dot_general(left, right, (((1,), (1,)), ((), ())), preferred_element_type=F32)


def dot_tn(left, right):
    return lax.dot_general(left, right, (((0,), (0,)), ((), ())), preferred_element_type=F32)


def standardize(inputs):
    row_mean = jnp.mean(inputs, axis=-1, keepdims=True)
    centred = inputs - row_mean
    spread = jnp.mean(centred * centred, axis=-1, keepdims=True)
    inv = lax.rsqrt(spread + eps)
    return centred * inv, inv


def standardize_back(grad, norm, inv):
    first = jnp.mean(grad, axis=-1, keepdims=True)
    second = jnp.mean(grad * norm, axis=-1, keepdims=True)
    return (grad - first - norm * second) * inv


def row_of(ref):
    return ref[...].reshape(1, D)


def column_sum(inputs):
    return jnp.sum(inputs, axis=0, keepdims=True)


def whole(shape):
    return pl.BlockSpec(shape, lambda *_: (0,) * len(shape), pipeline_mode=pl.Buffered(1))


def struct(shape, dtype):
    return jax.ShapeDtypeStruct(shape, dtype)


def cost(flops, moved, exps=0):
    return pl.CostEstimate(flops=int(flops), bytes_accessed=int(moved), transcendentals=int(exps))


def region_body(
    capacity,
    feats_ref,
    w_ref,
    boxes_ref,
    dest_ref,
    seq_ref,
    w_box_ref,
    type_ref,
    gain_ref,
    shift_ref,
    cot_ref,
    out_ref,
    cot_out_ref,
    hot_ref,
    norm_ref,
    inv_ref,
):
    rows = feats_ref.shape[0]
    slots = out_ref.shape[0]
    dest_row = jnp.broadcast_to(dest_ref[...].astype(F32), (rows, rows))
    dest_col = dest_row.T
    row_io = lax.broadcasted_iota(jnp.int32, (rows, rows), 0)
    col_io = lax.broadcasted_iota(jnp.int32, (rows, rows), 1)
    earlier = jnp.where((dest_col == dest_row) & (row_io < col_io), 1.0, 0.0)
    slot = dest_row[0:1, :] * capacity + column_sum(earlier)
    slot_io = lax.broadcasted_iota(jnp.int32, (slots, rows), 0).astype(F32)
    hot = jnp.where(slot_io == slot, 1.0, 0.0)
    hot_low = hot.astype(BF16)
    hot_ref[...] = hot_low
    cot_out_ref[...] = dot_nn(hot_low, cot_ref[...]).astype(BF16)
    tags = jnp.sum(hot * (seq_ref[...].astype(F32) + 1.0), axis=1, keepdims=True)
    projection = dot_nn(feats_ref[...], w_ref[...])
    boxes = jnp.concatenate([boxes_ref[...], jnp.zeros((4, rows), F32)], axis=0).T
    spatial = boxes[:, 0:1] * w_box_ref[0:1, :]
    for side in range(1, 4):
        spatial = spatial + boxes[:, side : side + 1] * w_box_ref[side : side + 1, :]
    norm, inv = standardize(projection + spatial + row_of(type_ref))
    norm_ref[...] = norm
    inv_ref[...] = inv
    low_rows = (norm * row_of(gain_ref) + row_of(shift_ref)).astype(BF16)
    out_ref[:, :D] = dot_nn(hot_low, low_rows).astype(BF16)
    out_ref[:, D:] = jnp.broadcast_to(tags, (slots, TAGS)).astype(BF16)


def region_forward(capacity, slots, feats, w_region, *others):
    rows, width = feats.shape
    return pl.pallas_call(
        functools.partial(region_body, capacity),
        out_shape=(
            struct((slots, D + TAGS), BF16),
            struct((slots, D), BF16),
            struct((slots, rows), BF16),
            struct((rows, D), F32),
            struct((rows, 1), F32),
        ),
        cost_estimate=cost(2 * rows * width * D, 2 * (rows + D) * width),
        name="region_forward",
    )(feats, w_region, *others)


def head_mask(head):
    lane = lax.broadcasted_iota(jnp.int32, (1, PAIR), 1)
    return (lane >= head * HDIM) & (lane < (head + 1) * HDIM)


def join(*refs):
    return jnp.concatenate([ref[...] for ref in refs], axis=0)


def thirds(rows):
    return [pl.BlockSpec((rows, PAIR), lambda p, *_, part=part: (0, part * PAIRS + p)) for part in range(3)]


def attend_body(
    lengths_ref,
    tag_ref,
    text_q_ref,
    text_k_ref,
    text_v_ref,
    region_q_ref,
    region_k_ref,
    region_v_ref,
    ctx_ref,
    chance_ref,
    inv_ref,
    bias_ref,
):
    text_count, slots = text_q_ref.shape[0], region_q_ref.shape[0]
    count = text_count + slots
    sequences = lengths_ref.shape[1]

    @pl.when(pl.program_id(0) == 0)
    def _():
        place = lax.broadcasted_iota(jnp.int32, (text_count, 1), 0)
        text_seg = jnp.zeros((text_count, 1), F32)
        end = jnp.int32(0)
        for index in range(sequences):
            end = end + lengths_ref[0, index]
            text_seg = text_seg + jnp.where(place >= end, 1.0, 0.0)
        region_seg = tag_ref[:, 0:1].astype(F32) - 1.0
        region_seg = jnp.where(region_seg < 0.0, float(sequences), region_seg)
        seg_col = jnp.concatenate([text_seg, region_seg], axis=0)
        seg_row = jnp.broadcast_to(seg_col, (count, 128)).T[0:1, :]
        bias_ref[...] = jnp.where(seg_col == seg_row, 0.0, -1e30)

    queries = join(text_q_ref, region_q_ref) * jnp.asarray(SCALE, BF16)
    key_rows = join(text_k_ref, region_k_ref)
    values = join(text_v_ref, region_v_ref)
    step = 256
    first = head_mask(0)
    for start in range(0, count, step):
        stop = start + step
        outs, invs = [], []
        for head in range(2):
            q_part = jnp.where(head_mask(head), queries[start:stop], jnp.zeros((), BF16))
            scores = dot_nt(q_part, key_rows) + bias_ref[start:stop, :]
            exp_terms = jnp.exp(scores - jnp.max(scores, axis=1, keepdims=True))
            inv = 1.0 / jnp.sum(exp_terms, axis=1, keepdims=True)
            low_terms = exp_terms.astype(BF16)
            chance_ref[head, start:stop, :] = low_terms
            outs.append(dot_nn(low_terms, values) * inv)
            invs.append(inv)
        ctx_ref[start:stop, :] = jnp.where(first, outs[0], outs[1]).astype(BF16)
        inv_ref[start:stop, :] = jnp.where(first, invs[0], invs[1])


def attend(lengths, arrived, qkv_text, qkv_region):
    text_count, slots = qkv_text.shape[0], qkv_region.shape[0]
    count = text_count + slots
    return pl.pallas_call(
        attend_body,
        grid_spec=pltpu.PrefetchScalarGridSpec(
            num_scalar_prefetch=1,
            grid=(PAIRS,),
            in_specs=[pl.BlockSpec((slots, TAGS), lambda p, *_: (0, D // TAGS))] + thirds(text_count) + thirds(slots),
            out_specs=[
                pl.BlockSpec((count, PAIR), lambda p, *_: (0, p)),
                pl.BlockSpec((2, count, count), lambda p, *_: (p, 0, 0)),
                pl.BlockSpec((count, PAIR), lambda p, *_: (0, p)),
            ],
            scratch_shapes=[pltpu.VMEM((count, count), F32)],
        ),
        out_shape=(
            struct((count, D), BF16),
            struct((HEADS, count, count), BF16),
            struct((count, D), F32),
        ),
        cost_estimate=cost(4 * count * count * D * 4, HEADS * count * count * 2, HEADS * count * count),
        name="attend",
    )(lengths, arrived, *(qkv_text,) * 3, *(qkv_region,) * 3)


def attend_back_body(
    text_q_ref,
    text_k_ref,
    text_v_ref,
    region_q_ref,
    region_k_ref,
    region_v_ref,
    w_q_ref,
    w_k_ref,
    w_v_ref,
    chance_ref,
    inv_ref,
    ctx_ref,
    dctx_ref,
    d_mid_ref,
    rows_turned_ref,
    keep_ref,
    send_ref,
    sum_ref,
    text_grad_ref,
    region_grad_ref,
    total_ref,
    grad_ref,
):
    count = ctx_ref.shape[0]
    text_count = text_q_ref.shape[0]
    queries = join(text_q_ref, region_q_ref) * jnp.asarray(SCALE, BF16)
    key_rows = join(text_k_ref, region_k_ref)
    values = join(text_v_ref, region_v_ref)
    scaled = dctx_ref[...].astype(F32) * inv_ref[...]
    product = scaled * ctx_ref[...].astype(F32)
    scaled_low = scaled.astype(BF16)
    scaled_turned = scaled.T.astype(BF16)
    q_turned = queries.astype(F32).T.astype(BF16)
    step = 256
    first = head_mask(0)
    keys_turned, values_turned = [None, None], [None, None]
    for start in range(0, count, step):
        stop = start + step
        ques = []
        for head in range(2):
            mask = head_mask(head)
            low, high = head * HDIM, (head + 1) * HDIM
            low_terms = chance_ref[head, start:stop, :]
            delta = jnp.sum(jnp.where(mask, product[start:stop], 0.0), axis=1, keepdims=True)
            d_part = jnp.where(mask, scaled_low[start:stop], jnp.zeros((), BF16))
            d_chance = dot_nt(d_part, values)
            d_scores = (low_terms.astype(F32) * (d_chance - delta)).astype(BF16)
            ques.append(dot_nn(d_scores, key_rows))
            v_add = dot_nn(scaled_turned[low:high, start:stop], low_terms)
            k_add = dot_nn(q_turned[low:high, start:stop], d_scores)
            values_turned[head] = v_add if start == 0 else values_turned[head] + v_add
            keys_turned[head] = k_add if start == 0 else keys_turned[head] + k_add
        d_ques = (jnp.where(first, ques[0], ques[1]) * SCALE).astype(BF16)
        grad_ref[start:stop, :PAIR] = d_ques
    grad_ref[:, PAIR : 2 * PAIR] = jnp.concatenate(keys_turned, axis=0).T.astype(BF16)
    d_values = jnp.concatenate(values_turned, axis=0).T.astype(BF16)
    grad_ref[:, 2 * PAIR :] = d_values
    sum_ref[...] = column_sum(grad_ref[...].astype(F32))

    @pl.when(pl.program_id(0) == 0)
    def _():
        total_ref[...] = d_mid_ref[...]

    w_part = jnp.concatenate([w_q_ref[...], w_k_ref[...], w_v_ref[...]], axis=1)
    total_ref[...] += dot_nt(grad_ref[...], w_part)
    half = keep_ref.shape[0]
    keep_ref[...] = dot_nn(rows_turned_ref[:half, :], grad_ref[...]).astype(BF16)
    send_ref[...] = dot_nn(rows_turned_ref[half:, :], grad_ref[...]).astype(BF16)

    @pl.when(pl.program_id(0) == pl.num_programs(0) - 1)
    def _():
        text_grad_ref[...] = total_ref[:text_count, :].astype(BF16)
        region_grad_ref[...] = total_ref[text_count:, :].astype(BF16)


def attend_back(qkv_text, qkv_region, w_qkv, chance, inv, ctx, d_ctx, d_mid, rows_turned):
    text_count, slots = qkv_text.shape[0], qkv_region.shape[0]
    count = text_count + slots
    return pl.pallas_call(
        attend_back_body,
        grid=(PAIRS,),
        in_specs=thirds(text_count)
        + thirds(slots)
        + thirds(D)
        + [
            pl.BlockSpec((2, count, count), lambda p: (p, 0, 0)),
            pl.BlockSpec((count, PAIR), lambda p: (0, p)),
            pl.BlockSpec((count, PAIR), lambda p: (0, p)),
            pl.BlockSpec((count, PAIR), lambda p: (0, p)),
            whole((count, D)),
            whole((D, count)),
        ],
        out_specs=[
            pl.BlockSpec((D // 2, 3 * PAIR), lambda p: (0, p)),
            pl.BlockSpec((D // 2, 3 * PAIR), lambda p: (0, p)),
            pl.BlockSpec((1, 3 * PAIR), lambda p: (0, p)),
            whole((text_count, D)),
            whole((slots, D)),
        ],
        out_shape=(
            struct((D // 2, 3 * D), BF16),
            struct((D // 2, 3 * D), BF16),
            struct((1, 3 * D), F32),
            struct((text_count, D), BF16),
            struct((slots, D), BF16),
        ),
        scratch_shapes=[pltpu.VMEM((count, D), F32), pltpu.VMEM((count, 3 * PAIR), BF16)],
        cost_estimate=cost(8 * count * count * D * 4 + 12 * count * D * D, HEADS * count * count * 2),
        name="attend_back",
    )(*(qkv_text,) * 3, *(qkv_region,) * 3, *(w_qkv,) * 3, chance, inv, ctx, d_ctx, d_mid, rows_turned)


def gelu_parts(inputs):
    weight = jnp.exp(inputs * inputs * (-0.5))
    place = 1.0 / (1.0 + jnp.abs(inputs) * TAIL_RATE)
    poly = TAIL[4]
    for factor in TAIL[3::-1]:
        poly = poly * place + factor
    tail = (0.5 * weight) * (poly * place)
    phi_sum = jnp.where(inputs >= 0.0, 1.0 - tail, tail)
    return inputs * phi_sum, phi_sum + inputs * (weight * 0.3989422804014327)


def feed_body(
    ctx_ref,
    w_out_ref,
    text_ref,
    region_ref,
    perm_ref,
    out_bias_ref,
    attn_gain_ref,
    attn_shift_ref,
    down_bias_ref,
    ffn_gain_ref,
    ffn_shift_ref,
    w_up_ref,
    up_bias_ref,
    w_down_ref,
    cot_text_ref,
    cot_region_ref,
    hidden_ref,
    slope_ref,
    norm_ref,
    inv_ref,
    rows_turned_ref,
    ctx_turned_ref,
    low_turned_ref,
    text_out_ref,
    region_out_ref,
    d_second_ref,
    d_down_ref,
    stats_ref,
    normed_ref,
    low_ref,
    total_ref,
):
    step = pl.program_id(0)
    text_count = text_ref.shape[0]
    count = ctx_ref.shape[0]
    parts = [(start, start + 256) for start in range(0, count, 256)]

    def each(body):
        @pl.loop(0, text_count // 256)
        def _(part):
            rows = pl.ds(pl.multiple_of(part * 256, 256), 256)
            body(rows, 0, rows)

        for start in range(text_count, count, 256):
            body(pl.ds(start, 256), 1, pl.ds(start - text_count, 256))

    @pl.when(step == 0)
    def _():
        def first(rows, side, own):
            inputs = (text_ref, region_ref)[side][own, :]
            ctx = ctx_ref[rows, :]
            attn_out = dot_nn(ctx, w_out_ref[...]) + row_of(out_bias_ref)
            norm, inv = standardize(inputs.astype(F32) + attn_out)
            normed = norm * row_of(attn_gain_ref) + row_of(attn_shift_ref)
            low = normed.astype(BF16)
            norm_ref[rows, :] = norm
            inv_ref[rows, :] = inv
            normed_ref[rows, :] = normed
            low_ref[rows, :] = low
            total_ref[rows, :] = normed + row_of(down_bias_ref)
            rows_turned_ref[:, rows] = dot_nt(perm_ref[...], inputs).astype(BF16)
            ctx_turned_ref[:, rows] = dot_nt(perm_ref[...], ctx).astype(BF16)
            low_turned_ref[:, rows] = dot_nt(perm_ref[...], low).astype(BF16)

        each(first)

    for start, stop in parts:
        up_sum = dot_nn(low_ref[start:stop, :], w_up_ref[...]) + up_bias_ref[...]
        value, slope = gelu_parts(up_sum)
        hidden = value.astype(BF16)
        hidden_ref[start:stop, :] = hidden
        slope_ref[start:stop, :] = slope.astype(BF16)
        total_ref[start:stop, :] += dot_nn(hidden, w_down_ref[...])

    @pl.when(step == pl.num_programs(0) - 1)
    def _():
        stats_ref[...] = jnp.zeros(stats_ref.shape, F32)

        def last(rows, side, own):
            norm, inv = standardize(total_ref[rows, :])
            out_ref = (text_out_ref, region_out_ref)[side]
            out_ref[own, :] = (norm * row_of(ffn_gain_ref) + row_of(ffn_shift_ref)).astype(BF16)
            upstream = (cot_text_ref, cot_region_ref)[side][own, :].astype(F32)
            d_second = standardize_back(upstream * row_of(ffn_gain_ref), norm, inv)
            d_down = d_second.astype(BF16)
            d_second_ref[rows, :] = d_second
            d_down_ref[rows, :] = d_down
            stats_ref[0:1, :] += column_sum(upstream * norm)
            stats_ref[1:2, :] += column_sum(upstream)
            stats_ref[2:3, :] += column_sum(d_down.astype(F32))

        each(last)


def feed_forward(ctx, w_out, text, arrived, perm, vecs, w_up, up_bias, w_down, cot_text, cot_region):
    count, text_count = ctx.shape[0], text.shape[0]
    slots = count - text_count
    units = w_up.shape[1]
    chunk = 512
    half = D // 2
    return pl.pallas_call(
        feed_body,
        grid=(units // chunk,),
        in_specs=[
            whole((count, D)),
            whole((D, D)),
            whole((text_count, D)),
            whole((slots, D)),
            whole((D, D)),
        ]
        + [whole((D,))] * len(vecs)
        + [
            pl.BlockSpec((D, chunk), lambda j: (0, j)),
            pl.BlockSpec((1, chunk), lambda j: (0, j)),
            pl.BlockSpec((chunk, D), lambda j: (j, 0)),
            whole((text_count, D)),
            whole((slots, D)),
        ],
        out_specs=[
            pl.BlockSpec((count, chunk), lambda j: (0, j)),
            pl.BlockSpec((count, chunk), lambda j: (0, j)),
            whole((count, D)),
            whole((count, 1)),
            whole((D, count)),
            whole((D, count)),
            whole((D, count)),
            whole((text_count, D)),
            whole((slots, D)),
            whole((count, D)),
            whole((count, D)),
            whole((8, D)),
        ],
        out_shape=(
            struct((count, units), BF16),
            struct((count, units), BF16),
            struct((count, D), F32),
            struct((count, 1), F32),
            struct((D, count), BF16),
            struct((D, count), BF16),
            struct((D, count), BF16),
            struct((text_count, D), BF16),
            struct((slots, D), BF16),
            struct((count, D), F32),
            struct((count, D), BF16),
            struct((8, D), F32),
        ),
        scratch_shapes=[
            pltpu.VMEM((count, D), F32),
            pltpu.VMEM((count, D), BF16),
            pltpu.VMEM((count, D), F32),
        ],
        cost_estimate=cost(4 * count * D * units + 8 * count * D * D, 4 * D * units + 4 * count * units, count * units),
        name="feed_forward",
    )(ctx, w_out, text, arrived, perm, *vecs, w_up, up_bias, w_down, cot_text, cot_region)


def feed_back_body(
    d_down_ref,
    slope_ref,
    w_down_ref,
    w_up_ref,
    d_second_ref,
    norm_ref,
    inv_ref,
    gain_ref,
    w_out_ref,
    low_turned_ref,
    ctx_turned_ref,
    up_keep_ref,
    up_send_ref,
    out_keep_ref,
    out_send_ref,
    up_sum_ref,
    d_mid_ref,
    d_ctx_ref,
    stats_ref,
    total_ref,
    d_up_ref,
    d_attn_ref,
):
    step = pl.program_id(0)
    count = d_down_ref.shape[0]
    parts = [(start, start + 256) for start in range(0, count, 256)]

    @pl.when(step == 0)
    def _():
        total_ref[...] = d_second_ref[...]

    up_total = jnp.zeros(up_sum_ref.shape, F32)
    for start, stop in parts:
        d_hidden = dot_nt(d_down_ref[start:stop, :], w_down_ref[...])
        d_up = (d_hidden * slope_ref[start:stop, :].astype(F32)).astype(BF16)
        d_up_ref[start:stop, :] = d_up
        up_total = up_total + column_sum(d_up.astype(F32))
        total_ref[start:stop, :] += dot_nt(d_up, w_up_ref[...])
    up_sum_ref[...] = up_total
    half = up_keep_ref.shape[0]
    up_keep_ref[...] = dot_nn(low_turned_ref[:half, :], d_up_ref[...]).astype(BF16)
    up_send_ref[...] = dot_nn(low_turned_ref[half:, :], d_up_ref[...]).astype(BF16)

    @pl.when(step == pl.num_programs(0) - 1)
    def _():
        stats_ref[...] = jnp.zeros(stats_ref.shape, F32)

        @pl.loop(0, len(parts))
        def _(part):
            rows = pl.ds(pl.multiple_of(part * 256, 256), 256)
            d_first = total_ref[rows, :]
            norm = norm_ref[rows, :]
            d_mid = standardize_back(d_first * row_of(gain_ref), norm, inv_ref[rows, :])
            d_attn = d_mid.astype(BF16)
            d_mid_ref[rows, :] = d_mid
            d_attn_ref[rows, :] = d_attn
            d_ctx_ref[rows, :] = dot_nt(d_attn, w_out_ref[...]).astype(BF16)
            stats_ref[0:1, :] += column_sum(d_first * norm)
            stats_ref[1:2, :] += column_sum(d_first)
            stats_ref[2:3, :] += column_sum(d_attn.astype(F32))

        out_keep_ref[...] = dot_nn(ctx_turned_ref[:half, :], d_attn_ref[...]).astype(BF16)
        out_send_ref[...] = dot_nn(ctx_turned_ref[half:, :], d_attn_ref[...]).astype(BF16)


def feed_back(d_down, slope, w_down, w_up, d_second, norm, inv, gain, w_out, low_turned, ctx_turned):
    count, units = slope.shape
    chunk = 512
    return pl.pallas_call(
        feed_back_body,
        grid=(units // chunk,),
        in_specs=[
            whole((count, D)),
            pl.BlockSpec((count, chunk), lambda j: (0, j)),
            pl.BlockSpec((chunk, D), lambda j: (j, 0)),
            pl.BlockSpec((D, chunk), lambda j: (0, j)),
            whole((count, D)),
            whole((count, D)),
            whole((count, 1)),
            whole((D,)),
            whole((D, D)),
            whole((D, count)),
            whole((D, count)),
        ],
        out_specs=[
            pl.BlockSpec((D // 2, chunk), lambda j: (0, j)),
            pl.BlockSpec((D // 2, chunk), lambda j: (0, j)),
            whole((D // 2, D)),
            whole((D // 2, D)),
            pl.BlockSpec((1, chunk), lambda j: (0, j)),
            whole((count, D)),
            whole((count, D)),
            whole((8, D)),
        ],
        out_shape=(
            struct((D // 2, units), BF16),
            struct((D // 2, units), BF16),
            struct((D // 2, D), BF16),
            struct((D // 2, D), BF16),
            struct((1, units), F32),
            struct((count, D), F32),
            struct((count, D), BF16),
            struct((8, D), F32),
        ),
        scratch_shapes=[
            pltpu.VMEM((count, D), F32),
            pltpu.VMEM((count, chunk), BF16),
            pltpu.VMEM((count, D), BF16),
        ],
        cost_estimate=cost(6 * count * D * units + 4 * count * D * D, 4 * D * units + 4 * count * units),
        name="feed_back",
    )(d_down, slope, w_down, w_up, d_second, norm, inv, gain, w_out, low_turned, ctx_turned)


def region_back_body(
    back_ref,
    hot_ref,
    norm_ref,
    inv_ref,
    gain_ref,
    boxes_ref,
    qkv_ref,
    attn_ref,
    ffn_ref,
    up_ref,
    perm_ref,
    d_proj_ref,
    *piece_refs,
):
    rows = norm_ref.shape[0]
    d_region = dot_tn(hot_ref[...], back_ref[...])
    norm = norm_ref[...]
    d_pre = standardize_back(d_region * row_of(gain_ref), norm, inv_ref[...])
    d_proj = d_pre.astype(BF16)
    d_proj_ref[...] = d_proj
    boxes = jnp.concatenate([boxes_ref[...], jnp.zeros((4, rows), F32)], axis=0).T
    vectors = [column_sum(d_pre), column_sum(d_region * norm), column_sum(d_region)]
    vectors += [column_sum(boxes[:, side : side + 1] * d_pre) for side in range(4)]
    for part in (0, 2):
        starts = [(3 * pair + part) * PAIR for pair in range(PAIRS)]
        vectors.append(jnp.concatenate([qkv_ref[:, start : start + PAIR] for start in starts], axis=1))
    for ref in (attn_ref, ffn_ref):
        vectors += [ref[2:3, :], ref[0:2, :]]
    vectors.append(up_ref[...])
    filled = sum(vector.shape[0] for vector in vectors)
    vectors.append(jnp.zeros((VECS - filled, D), F32))
    low_vectors = jnp.concatenate(vectors, axis=0).astype(BF16)
    turned = dot_nt(perm_ref[...], jnp.concatenate([d_proj, low_vectors], axis=0)).astype(BF16)
    size = D // len(piece_refs)
    for index, piece_ref in enumerate(piece_refs):
        piece_ref[...] = turned[index * size : (index + 1) * size]


def region_back(back, hot, norm, *others):
    rows = norm.shape[0]
    return pl.pallas_call(
        region_back_body,
        out_shape=(struct((rows, D), BF16),) + (struct((D // 4, rows + VECS), BF16),) * 4,
        cost_estimate=cost(0, 0),
        name="region_back",
    )(back, hot, norm, *others)


def swap_cores(sent):
    return lax.ppermute(sent, "enc", [(0, 1), (1, 0)])


def swap_chips(sent, offset, peers):
    return lax.ppermute(sent, "dp", [(peer, peer ^ offset) for peer in range(peers)])


MASKS = (0, 1, 3, 2)


def reverse(value, width):
    result = value & 0
    for bit in range(width):
        result = result | (((value >> bit) & 1) << (width - 1 - bit))
    return result


def after(first, *others):
    if not others:
        return first
    return lax.optimization_barrier((first,) + others)[0]


def swap_cores(sent):
    return [lax.ppermute(array, "enc", [(0, 1), (1, 0)]) for array in sent]


def swap_chips(sent, mask, peers):
    return lax.ppermute(sent, "dp", [(peer, peer ^ mask) for peer in range(peers)])


def combine_body(plans, counts, *refs):
    refs, out_refs = refs[:counts], refs[counts:]
    for out_ref, (unit, segments) in zip(out_refs, plans):

        def add(start, size, segments=segments, out_ref=out_ref):
            for place, at, terms in segments:
                sums = [refs[index][pl.ds(start, size), left:right].astype(F32) for index, left, right in terms]
                value = functools.reduce(jnp.add, sums).astype(out_ref.dtype)
                out_ref[pl.ds(place + start, size), at : at + value.shape[1]] = value

        if unit % 32 or unit < 64:
            add(0, unit)
        else:

            @pl.loop(0, unit // 32)
            def _(step, add=add):
                add(pl.multiple_of(step * 32, 32), 32)


def segments_of(terms, columns):
    edges = set()
    for array, _, first in terms:
        edges |= {first, first + array.shape[1]}
    for left, right in columns:
        inside = sorted({left, right} | {edge for edge in edges if left < edge < right})
        yield from zip(inside, inside[1:])


def combine_plain(terms, start, stop, columns, dtype):
    sums = []
    for left, right in segments_of(terms, columns):
        blocks = [
            array[row + start : row + stop, left - first : right - first].astype(F32)
            for array, row, first in terms
            if first <= left and right <= first + array.shape[1]
        ]
        sums.append(functools.reduce(jnp.add, blocks))
    return jnp.concatenate(sums, axis=1).astype(dtype)


def combine(wanted, name):
    plans, operands, specs, shapes, known = [], [], [], [], {}
    for terms, start, stop, columns, dtype in wanted:
        unit = functools.reduce(math.gcd, [value for _, row, _ in terms for value in (row + start, row + stop)])
        if unit % 8:
            return [combine_plain(*each) for each in wanted]
        segments = []
        for place in range(0, stop - start, unit):
            at = 0
            for left, right in segments_of(terms, columns):
                sources = []
                for array, row, first in terms:
                    if first <= left and right <= first + array.shape[1]:
                        block = (row + start + place) // unit
                        key = (id(array), unit, block)
                        if key not in known:
                            known[key] = len(operands)
                            operands.append(array)
                            specs.append(pl.BlockSpec((unit, array.shape[1]), lambda j, block=block: (block, 0)))
                        sources.append((known[key], left - first, right - first))
                segments.append((place, at, sources))
                at += right - left
        plans.append((unit, segments))
        shapes.append(struct((stop - start, at), dtype))
    return pl.pallas_call(
        functools.partial(combine_body, plans, len(operands)),
        grid=(1,),
        in_specs=specs,
        out_specs=[pl.BlockSpec(shape.shape, lambda j: (0, 0)) for shape in shapes],
        out_shape=tuple(shapes),
        cost_estimate=cost(0, 0),
        name=name,
    )(*operands)


def side_by_side(*arrays):
    terms, first = [], 0
    for array in arrays:
        terms.append((array, 0, first))
        first += array.shape[1]
    return terms


class Pair:
    def __init__(self, terms, rows, middle, width, peers):
        self.terms, self.size, self.middle, self.width, self.peers = terms, rows // 4, middle, width, peers
        self.sides = [(0, middle)], [(middle, width)]

    def start(self):
        size, (first, second) = self.size, self.sides
        wanted = [(self.terms, size, 3 * size, first, BF16), (self.terms, 2 * size, 4 * size, second, BF16)]
        self.sent = list(combine(wanted, "pair_start"))
        return self.sent

    def ship(self):
        self.got = [swap_chips(sent, bit, self.peers) for sent, bit in zip(self.sent, (1, 2))]
        return self.got

    def hold(self, *behind):
        self.got = [after(array, *behind) for array in self.got]

    def turn(self):
        size, (first, second), (one, two) = self.size, self.sides, self.got
        wanted = [
            (self.terms + [(one, -2 * size, 0)], 3 * size, 4 * size, first, BF16),
            (self.terms + [(two, -size, self.middle)], size, 2 * size, second, BF16),
        ]
        self.sent = list(combine(wanted, "pair_turn"))
        return self.sent

    def finish(self):
        last = [swap_chips(sent, bit, self.peers) for sent, bit in zip(self.sent, (2, 1))]
        (one, two), middle = self.got, self.middle
        arrived = [(one, 0, 0), (two, self.size, middle), (last[0], 0, 0), (last[1], 0, middle)]
        return Scatter(self.terms + arrived, self.size, self.width, self.peers, 2, 2)


class Scatter:
    def __init__(self, terms, rows, width, peers, bit, fresh):
        self.terms, self.rows, self.width, self.peers, self.bit, self.fresh = terms, rows, width, peers, bit, fresh

    def cut(self, bits, *behind):
        self.bits = min(bits, self.peers.bit_length() - 1 - self.bit)
        self.rows >>= self.bits
        wanted = [
            (self.terms, offset * self.rows, (offset + 1) * self.rows, [(0, self.width)], BF16)
            for offset in range(1, 1 << self.bits)
        ]
        self.sent = [after(array, *behind) for array in combine(wanted, "cut")]
        return self.sent

    def ship(self):
        masks = [reverse(offset, self.bits) << self.bit for offset in range(1, 1 << self.bits)]
        got = [swap_chips(sent, mask, self.peers) for sent, mask in zip(self.sent, masks)]
        self.terms = self.terms + side_by_side_rows(got)
        self.bit += self.bits
        self.fresh = len(got)
        return got

    def hold(self, *behind):
        late = [(after(array, *behind), row, first) for array, row, first in self.terms[-self.fresh :]]
        self.terms = self.terms[: -self.fresh] + late

    def finish(self, bits):
        while 1 << self.bit < self.peers:
            self.cut(bits)
            self.ship()
        return self

    def shares(self, *ranges):
        return [(self.terms, 0, self.rows, columns, F32) for columns in ranges]


def side_by_side_rows(arrays):
    return [(array, 0, 0) for array in arrays]


def direct(terms, rows, width, peers, bit):
    size = rows // 4
    wanted = [(terms, place * size, (place + 1) * size, [(0, width)], BF16) for place in range(1, 4)]
    sent = combine(wanted, "direct")
    got = [swap_chips(array, mask, peers) for array, mask in zip(sent, MASKS[1:])]
    return sent, Scatter(terms + side_by_side_rows(got), size, width, peers, bit, 3)


def swap_near(pieces, peers):
    return [swap_chips(piece, offset << 2, peers) for offset, piece in enumerate(pieces[1:], 1)]


def place_of(block, peers):
    rest = peers // 4
    top = block // rest
    return (top ^ (top >> 1)) + (reverse(block % rest, rest.bit_length() - 1) << 2)


def units_body(order_ref, *refs):
    kept, got = refs[:-3:2], refs[1:-3:2]
    near_ref, far_ref, keep_ref = refs[-3:]
    step, half = pl.program_id(0), near_ref.shape[1]
    rows = [(one[...].astype(F32) + two[...].astype(F32)).astype(BF16) for one, two in zip(kept, got)]
    rows = jnp.concatenate(rows, axis=0)
    keep_ref[...] = rows

    @pl.when((step == 1) | (step == 2))
    def _():
        near_ref[...] = rows[:, :half]

    @pl.when(step >= 2)
    def _():
        far_ref[...] = rows[:, half:]


def cut_units(kept, got, order, peers):
    count, width = kept.shape
    size, half, rest = count // peers, width // 2, peers // 4
    if size % 16:
        rows = (kept.astype(F32) + got.astype(F32)).reshape(peers, size, width)
        rows = jnp.take(rows, order, axis=0).reshape(count, width).astype(BF16)
        return rows[count // 4 : 3 * count // 4, :half], rows[count // 2 :, half:], rows
    specs = []
    for index in range(rest):
        specs += [pl.BlockSpec((size, width), lambda j, order, index=index: (order[j * rest + index], 0))] * 2
    return pl.pallas_call(
        units_body,
        grid_spec=pltpu.PrefetchScalarGridSpec(
            num_scalar_prefetch=1,
            grid=(4,),
            in_specs=specs,
            out_specs=[
                pl.BlockSpec((count // 4, half), lambda j, order: (jnp.clip(j - 1, 0, 1), 0)),
                pl.BlockSpec((count // 4, half), lambda j, order: (jnp.clip(j - 2, 0, 1), 0)),
                pl.BlockSpec((count // 4, width), lambda j, order: (j, 0)),
            ],
        ),
        out_shape=(struct((count // 2, half), BF16), struct((count // 2, half), BF16), struct((count, width), BF16)),
        cost_estimate=cost(count * width, 8 * count * width),
        name="cut_units",
    )(order, *(kept, got) * rest)


def region_product_body(*refs):
    *refs, keep_ref, send_ref = refs
    pieces, feats = refs[: len(refs) // 2], refs[len(refs) // 2 :]
    rows, width = feats[0].shape
    half = keep_ref.shape[0]
    turned = jnp.concatenate([piece[:, :rows] for piece in pieces], axis=1)
    vectors = functools.reduce(jnp.add, [piece[:, rows:].astype(F32) for piece in pieces])
    product = dot_nn(turned, jnp.concatenate([ref[...] for ref in feats], axis=0)).astype(BF16)
    for ref, start in ((keep_ref, 0), (send_ref, half)):
        ref[:, :width] = product[start : start + half]
        ref[:, width:] = vectors[start : start + half].astype(BF16)


def region_product(pieces, feats):
    half, width = pieces[0].shape[0] // 2, feats[0].shape[1] + VECS
    return pl.pallas_call(
        region_product_body,
        out_shape=(struct((half, width), BF16), struct((half, width), BF16)),
        cost_estimate=cost(0, 0),
        name="region_product",
    )(*pieces, *feats)


def one_hot_rows(core, place, inner, peers):
    share = D // (2 * peers)
    core, place = core ^ lax.axis_index("enc"), place ^ lax.axis_index("dp")
    row = (core * peers + place) * share + inner
    return (lax.broadcasted_iota(jnp.int32, (D, D), 1) == row).astype(BF16)


def share_order(peers):
    share = D // (2 * peers)
    row = lax.broadcasted_iota(jnp.int32, (D, 1), 0)
    block = row // share
    return one_hot_rows(block // peers, place_of(block % peers, peers), row % share, peers)


def region_order(peers):
    share, rest = D // (2 * peers), peers // 16
    row = lax.broadcasted_iota(jnp.int32, (D, 1), 0)
    block = row // share
    top = (block // rest) % 4
    place = (top ^ (top >> 1)) + ((block // (8 * rest)) << 2) + (reverse(block % rest, rest.bit_length() - 1) << 4)
    return one_hot_rows((block // (4 * rest)) % 2, place, row % share, peers)


def exchange(array):
    return lax.all_to_all(array, "dp", split_axis=0, concat_axis=0, tiled=True)


def per_device(
    text_in,
    text_lengths,
    region_feats,
    region_boxes,
    region_dest,
    region_seq,
    w_region,
    w_box,
    type_embed,
    region_gain,
    region_shift,
    w_qkv,
    q_bias,
    v_bias,
    w_out,
    out_bias,
    attn_gain,
    attn_shift,
    w_up,
    up_bias,
    w_down,
    down_bias,
    ffn_gain,
    ffn_shift,
    cot_text,
    cot_region,
):
    peers = lax.axis_size("dp")
    source_rows = region_feats.shape[0]
    capacity = max(2, 2 * source_rows // peers)
    slots = peers * capacity
    text_count = text_in.shape[0]
    units = w_up.shape[1]

    def row(vector):
        return vector.reshape(1, -1)

    outgoing, cot_sent, hot, region_norm, region_inv = region_forward(
        capacity,
        slots,
        region_feats,
        w_region,
        region_boxes,
        row(region_dest),
        row(region_seq),
        w_box,
        type_embed,
        region_gain,
        region_shift,
        cot_region,
    )
    arrived = exchange(outgoing)
    arrived_cot = exchange(cot_sent)

    far_feats = swap_near([region_feats] + [after(region_feats, arrived)] * 3, peers)

    bias = jnp.concatenate([q_bias, jnp.zeros_like(q_bias), v_bias])[None]
    perm, region_perm = lax.optimization_barrier((share_order(peers), region_order(peers)))
    order = place_of(jnp.arange(peers, dtype=jnp.int32), peers) ^ lax.axis_index("dp")
    qkv_text = (dot_nn(text_in, w_qkv) + bias).astype(BF16)
    qkv_region = (dot_nn(arrived[:, :D], w_qkv) + bias).astype(BF16)
    context, chance, chance_inv = attend(text_lengths, arrived, qkv_text, qkv_region)
    vecs = (out_bias, attn_gain, attn_shift, down_bias, ffn_gain, ffn_shift)
    (
        hidden,
        slope,
        norm,
        inv,
        rows_turned,
        ctx_turned,
        low_turned,
        text_out,
        region_sent,
        d_second,
        d_down,
        ffn_stats,
    ) = feed_forward(context, w_out, text_in, arrived, perm, vecs, w_up, row(up_bias), w_down, cot_text, arrived_cot)

    d_down = after(d_down, *far_feats)
    core = lax.axis_index("enc")
    half = units // 2

    def unit_product(which):
        side = lax.dynamic_slice_in_dim(hidden, which * half, half, axis=1)
        return dot_tn(side, d_down).astype(BF16)

    (got,) = swap_cores([unit_product(1 - core)])
    *sent, kept = cut_units(unit_product(core), got, order, peers)
    down = Pair([(kept, 0, 0)], half, D // 2, D, peers)
    down.sent = sent
    covered = after(d_down, *sent)
    near = down.ship()
    up_keep, up_send, out_keep, out_send, up_grad, d_mid, d_ctx, attn_stats = feed_back(
        covered, slope, w_down, w_up, d_second, norm, inv, attn_gain, w_out, low_turned, ctx_turned
    )
    up_send, out_send = lax.optimization_barrier((up_send, out_send, *near))[:2]
    got = swap_cores([up_send, out_send])
    down_sent = down.turn()
    down = down.finish()
    down_got = [array for array, _, _ in down.terms[-down.fresh :]]
    up_out = Pair(
        side_by_side(up_keep, out_keep) + side_by_side(*got), D // 2, (units + D) // 2, units + D, peers
    )
    returned = exchange(after(region_sent, *down_sent))
    covered = after(d_ctx, returned, *up_out.start())
    near = up_out.ship()
    qkv_keep, qkv_send, qkv_sums, text_grad, d_rows_region = attend_back(
        qkv_text, qkv_region, w_qkv, chance, chance_inv, context, covered, d_mid, rows_turned
    )
    qkv_send = after(qkv_send, *near, *down_got)
    (got,) = swap_cores([qkv_send])
    sent_back = exchange(after(d_rows_region, qkv_send))
    qkv = Pair([(qkv_keep, 0, 0), (got, 0, 0)], D // 2, 3 * D // 2, 3 * D, peers)
    sent = qkv.start()
    qkv_got = qkv.ship()
    up_out.hold(*sent)
    sent = up_out.turn()
    up_out = up_out.finish()
    down.hold(*sent)
    sent_back = after(sent_back, *qkv_got, *down.cut(1))
    down.ship()
    qkv.hold(sent_back)
    qkv_sent = qkv.turn()
    qkv = qkv.finish()

    share = D // (2 * peers)
    quarter = units // D
    up_rows = after(up_grad, *sent).reshape(2 * peers, quarter, share).transpose(1, 0, 2).reshape(quarter, D)
    d_proj, *pieces = region_back(
        sent_back,
        hot,
        region_norm,
        region_inv,
        region_gain,
        region_boxes,
        qkv_sums,
        attn_stats,
        ffn_stats,
        up_rows,
        region_perm,
    )
    feats_width = region_feats.shape[1]
    up_out.hold(*pieces)
    qkv.hold(*pieces)
    down.hold(*pieces)
    region_got = swap_near(pieces, peers)
    qkv_sent = qkv_sent + up_out.cut(1)
    up_out.ship()
    region_got = [after(array, *qkv_sent) for array in region_got]
    last_keep, last_send = region_product(pieces[:1] + region_got, [region_feats] + far_feats)
    (got,) = swap_cores([last_send])
    qkv.hold(last_send)
    down.hold(last_send)
    qkv.cut(1)
    qkv.ship()
    down.finish(1)
    last_sent, last = direct(
        [(last_keep, 0, 0), (got, 0, 0)], last_keep.shape[0], feats_width + VECS, peers, 4
    )
    qkv.hold(*last_sent)
    up_out.hold(*last_sent)
    down.hold(*last_sent)
    d_proj, returned = lax.optimization_barrier((d_proj, returned, *last_sent))[:2]
    region_out = dot_tn(hot, returned).astype(BF16)
    feats_grad = dot_nt(d_proj, w_region).astype(BF16)
    starts = [(3 * pair + part) * PAIR for part in range(3) for pair in range(PAIRS)]
    heads = [(start, start + PAIR) for start in starts]
    w_qkv_share, w_up_share, w_out_share, w_down_share = combine(
        qkv.finish(1).shares(heads)
        + up_out.finish(1).shares([(0, units)], [(units, units + D)])
        + down.finish(1).shares([(0, D)]),
        "shares",
    )
    w_region_share, vectors = combine(
        last.finish(2).shares([(0, feats_width)], [(feats_width, feats_width + VECS)]), "last_shares"
    )
    vectors = vectors.T
    return (
        text_out,
        region_out,
        text_grad,
        feats_grad,
        w_region_share.T,
        vectors[3:7],
        vectors[0],
        vectors[1],
        vectors[2],
        w_qkv_share,
        vectors[7],
        vectors[8],
        w_out_share,
        vectors[9],
        vectors[10],
        vectors[11],
        w_up_share,
        vectors[15 : 15 + quarter].reshape(-1),
        w_down_share,
        vectors[12],
        vectors[13],
        vectors[14],
    )


def solution(mesh):
    both = ("enc", "dp")
    rows, flat, none = P(both, None), P(both), P()
    in_specs = (rows, rows, rows, P(None, both), rows, flat) + (none,) * 18 + (rows, rows)
    out_specs = (
        (rows,) * 4
        + (P(None, both), P(None, both), flat, flat, flat, rows, flat, flat, rows)
        + (flat, flat, flat, rows, flat, rows, flat, flat, flat)
    )
    return jax.shard_map(per_device, mesh=mesh, in_specs=in_specs, out_specs=out_specs, check_vma=False)
```

profile of v0, /device:TPU:0, one launch (start us, length us, event | category | flops | bytes accessed | tf_op | source)
XLA Modules:
  0.0 282.1 jit_solution(18071450598132481524)
XLA Ops:
  0.7 4.3 %region_forward.1 = (bf16[256,896]{1,0:T(8,128)(2,1)}, bf16[256,768]{1,0:T(8,128)(2,1)}, bf16[256,128]{1,0:T(8,128)(2,1)}, f32[128,768]{1,0:T(8,128)}, f32[128,1]{1,0:T(8,128)}) custom-call(bf16[128,2048]{1,0:T(8,128)(2,1)} %refs_4_.1, bf16[2048,768]{1,0:T(8,128)(2,1)} %w_ref.1, f32[4,128]{1,0:T(4,128)} %boxes_ref.3, s32[1,128]{1,0:T(1,128)} %bitcast.33, ...), custom_call_target="tpu_custom_call" | custom-call | flops 402653184 | bytes 3670016 | tf_op jit(solution)/shard_map/region_forward/pallas_call | solution.py:121
  5.0 8.5 %all-to-all-start = ((bf16[16,16,896]{2,1,0:T(8,128)(2,1)}), bf16[16,16,896]{2,1,0:T(8,128)(2,1)S(1)}, u32[]{:S(2)}, u32[]{:S(2)}) async-start(bf16[16,16,896]{2,1,0:T(8,128)(2,1)} %bitcast.28), calls=%async_computation | async-start | bytes 917504 | tf_op jit(solution)/shard_map/all_to_all | solution.py:971
  16.2 5.5 %fusion.text_q_ref.text_k_ref.text_v_ref = bf16[512,2304]{1,0:T(8,128)(2,1)} fusion(bf16[512,768]{1,0:T(8,128)(2,1)S(1)} %copy-done.35, bf16[768,2304]{1,0:T(8,128)(2,1)} %w_v_ref.1, f32[2304]{0:T(1024)S(1)} %pad_maximum_fusion), kind=kOutput, calls=%fused_computation.1 | convolution fusion | flops 1814298624 | bytes 6693888 | tf_op jit(solution)/shard_map/dot_general | solution.py:29
  21.6 5.7 %all-to-all-done = bf16[16,16,896]{2,1,0:T(8,128)(2,1)S(1)} async-done(((bf16[16,16,896]{2,1,0:T(8,128)(2,1)}), bf16[16,16,896]{2,1,0:T(8,128)(2,1)S(1)}, u32[]{:S(2)}, u32[]{:S(2)}) %all-to-all-start) | async-done | bytes 458784 | tf_op jit(solution)/shard_map/all_to_all | solution.py:971
  27.4 3.8 %all-to-all-start.1 = ((bf16[16,16,768]{2,1,0:T(8,128)(2,1)}), bf16[16,16,768]{2,1,0:T(8,128)(2,1)S(1)}, u32[]{:S(2)}, u32[]{:S(2)}) async-start(bf16[16,16,768]{2,1,0:T(8,128)(2,1)} %bitcast.5), calls=%async_computation.1 | async-start | bytes 786432 | tf_op jit(solution)/shard_map/all_to_all | solution.py:971
  31.2 4.2 %fusion.1.region_q_ref.region_k_ref.region_v_ref = bf16[256,2304]{1,0:T(8,128)(2,1)} fusion(bf16[768,2304]{1,0:T(8,128)(2,1)} %w_v_ref.1, f32[2304]{0:T(1024)S(1)} %pad_maximum_fusion, bf16[256,896]{1,0:T(8,128)(2,1)S(1)} %bitcast.25), kind=kOutput, calls=%fused_computation.3 | convolution fusion | flops 907149312 | bytes 5124096 | tf_op jit(solution)/shard_map/dot_general | solution.py:29
  35.4 1.9 collective-permute-start
  37.3 2.4 collective-permute-start.1
  39.8 20.2 %attend.1 = (bf16[768,768]{1,0:T(8,128)(2,1)}, bf16[12,768,768]{2,1,0:T(8,128)(2,1)}, f32[768,768]{1,0:T(8,128)}) custom-call(s32[1,5]{1,0:T(1,128)} %lengths_ref.1, bf16[256,896]{1,0:T(8,128)(2,1)} %bitcast.26, bf16[512,2304]{1,0:T(8,128)(2,1)} %fusion.text_q_ref.text_k_ref.text_v_ref, bf16[512,2304]{1,0:T(8,128)(2,1)} %fusion.text_q_ref.text_k_ref.text_v_ref, ...), custom_call_target="tpu_custom_call" | custom-call | flops 7247757312 | bytes 14155776 | tf_op jit(solution)/shard_map/attend/pallas_call | solution.py:204
  60.7 30.3 %feed_forward.1 = (bf16[768,3072]{1,0:T(8,128)(2,1)}, bf16[768,3072]{1,0:T(8,128)(2,1)}, f32[768,768]{1,0:T(8,128)}, f32[768,1]{1,0:T(8,128)}, bf16[768,768]{1,0...) custom-call(bf16[768,768]{1,0:T(8,128)(2,1)} %get-tuple-element.120., ...), custom_call_target="tpu_custom_call" | custom-call | flops 10871635968 | bytes 18874368 | tf_op jit(solution)/shard_map/feed_forward/pallas_call | solution.py:452
  92.2 5.6 %convolution_convert_fusion = bf16[1536,768]{1,0:T(8,128)(2,1)} fusion(bf16[768,768]{1,0:T(8,128)(2,1)} %get-tuple-element.133.d_down_ref, bf16[768,3072]{1,0:T(8,128)(2,1)} %get-tuple-element.130, s32[]{:T(128)S(6)} %select_n.140), kind=kOutput, calls=%fused_computation.4 | convolution fusion | flops 1813118976 | bytes 5898244 | tf_op jit(solution)/shard_map/dot_general | solution.py:37
  98.3 5.1 %convolution_convert_fusion.1.refs_0_.refs_2_.refs_4_.refs_6_ = bf16[1536,768]{1,0:T(8,128)(2,1)} fusion(bf16[768,768]{1,0:T(8,128)(2,1)S(1)} %copy-done.38, bf16[768,3072]{1,0:T(8,128)(2,1)} %get-tuple-element.130, s32[]{:T(128)S(6)} %select_n.139), kind=kOutput, calls=%fused_computation.5 | convolution fusion | flops 1813118976 | bytes 5898244 | tf_op jit(solution)/shard_map/dot_general | solution.py:37
  104.9 5.6 %cut_units.1 = (bf16[768,384]{1,0:T(8,128)(2,1)}, bf16[768,384]{1,0:T(8,128)(2,1)}, bf16[1536,768]{1,0:T(8,128)(2,1)}) custom-call(s32[16]{0:T(128)} %fusion.41.order_ref, bf16[1536,768]{1,0:T(8,128)(2,1)} %convolution_convert_fusion.1.refs_0_.refs_2_.refs_4_.refs_6_, bf16[1536,768]{1,0:T(8,128)(2,1)} %copy-done.2, ...), custom_call_target="tpu_custom_call" | custom-call | flops 1179648 | bytes 9437184 | tf_op jit(solution)/shard_map/cut_units/pallas_call | solution.py:906
  110.5 1.9 collective-permute-start.4
  113.8 25.0 %feed_back.1 = (bf16[384,3072]{1,0:T(8,128)(2,1)}, bf16[384,3072]{1,0:T(8,128)(2,1)}, bf16[384,768]{1,0:T(8,128)(2,1)}, bf16[384,768]{1,0:T(8,128)(2,1)}, f32[1,...) custom-call(bf16[768,768]{1,0:T(8,128)(2,1)} %get-tuple-element.133.d_down_ref, ...), custom_call_target="tpu_custom_call" | custom-call | flops 12683575296 | bytes 18874368 | tf_op jit(solution)/shard_map/feed_back/pallas_call | solution.py:577
  139.9 2.5 pair_turn.3
  142.4 4.7 %all-to-all-start.2 = ((bf16[16,16,768]{2,1,0:T(8,128)(2,1)}), bf16[16,16,768]{2,1,0:T(8,128)(2,1)}, u32[]{:S(2)}, u32[]{:S(2)}) async-start(bf16[16,16,768]{2,1,0:T(8,128)(2,1)} %bitcast.29), calls=%async_computation.2 | async-start | bytes 786432 | tf_op jit(solution)/shard_map/all_to_all | solution.py:971
  147.2 1.9 collective-permute-start.10
  152.2 4.0 %pair_start.2 = (bf16[192,1920]{1,0:T(8,128)(2,1)}, bf16[192,1920]{1,0:T(8,128)(2,1)}) custom-call(bf16[384,3072]{1,0:T(8,128)(2,1)} %get-tuple-element.146.refs_0_.refs_2_.refs_4_.refs_3_.refs_8_, bf16[384,3072]{1,0:T(8,128)(2,1)} %copy-done, bf16[384,3072]{1,0:T(8,128)(2,1)} %get-tuple-element.146.refs_0_.refs_2_.refs_4_.refs_3_.refs_8_, ...), custom_call_target="tpu_custom_call" | custom-call | tf_op jit(solution)/shard_map/pair_start/pallas_call | solution.py:768
  158.3 1.7 all-to-all-done.2
  160.0 28.3 %attend_back.1 = (bf16[384,2304]{1,0:T(8,128)(2,1)}, bf16[384,2304]{1,0:T(8,128)(2,1)}, f32[1,2304]{1,0:T(1,128)}, bf16[512,768]{1,0:T(8,128)(2,1)}, bf16[256,768]{1,0:T(8,128)(2,1)}) custom-call(bf16[512,2304]{1,0:T(8,128)(2,1)} %fusion.text_q_ref.text_k_ref.text_v_ref, bf16[512,2304]{1,0:T(8,128)(2,1)} %fusion.text_q_ref.text_k_ref.text_v_ref, ...), custom_call_target="tpu_custom_call" | custom-call | flops 19931332608 | bytes 14155776 | tf_op jit(solution)/shard_map/attend_back/pallas_call | solution.py:306
  188.4 4.2 %all-to-all-start.3 = ((bf16[16,16,768]{2,1,0:T(8,128)(2,1)}), bf16[16,16,768]{2,1,0:T(8,128)(2,1)}, u32[]{:S(2)}, u32[]{:S(2)}) async-start(bf16[16,16,768]{2,1,0:T(8,128)(2,1)} %bitcast.30), calls=%async_computation.3 | async-start | bytes 786432 | tf_op jit(solution)/shard_map/all_to_all | solution.py:971
  193.9 3.2 %pair_start.3 = (bf16[192,1152]{1,0:T(8,128)(2,1)}, bf16[192,1152]{1,0:T(8,128)(2,1)}) custom-call(bf16[384,2304]{1,0:T(8,128)(2,1)} %get-tuple-element.161.refs_0_.refs_2_.refs_4_.refs_3_, bf16[384,2304]{1,0:T(8,128)(2,1)} %copy-done.1, bf16[384,2304]{1,0:T(8,128)(2,1)} %get-tuple-element.161.refs_0_.refs_2_.refs_4_.refs_3_, bf16[384,2304]{1,0:T(8,128)(2,1)} %copy-done.1, ...), custom_call_target="tpu_custom_call" | custom-call | tf_op jit(solution)/shard_map/pair_start/pallas_call | solution.py:768
  197.1 1.7 collective-permute-start.13
  200.4 3.0 %pair_turn.4 = (bf16[96,1920]{1,0:T(8,128)(2,1)}, bf16[96,1920]{1,0:T(8,128)(2,1)}) custom-call(bf16[384,3072]{1,0:T(8,128)(2,1)} %get-tuple-element.146.refs_0_.refs_2_.refs_4_.refs_3_.refs_8_, bf16[384,3072]{1,0:T(8,128)(2,1)} %copy-done, bf16[192,1920]{1,0:T(8,128)(2,1)} %copy-done.5, ...), custom_call_target="tpu_custom_call" | custom-call | tf_op jit(solution)/shard_map/pair_turn/pallas_call | solution.py:768
  206.3 2.0 cut.6
  208.3 4.2 %collective-permute-done.13.refs_2_ = bf16[192,1152]{1,0:T(8,128)(2,1)S(1)} collective-permute-done((bf16[192,1152]{1,0:T(8,128)(2,1)}, bf16[192,1152]{1,0:T(8,128)(2,1)S(1)}, u32[]{:S(2)}, u32[]{:S(2)}) %collective-permute-start.13) | collective-permute-done | bytes 442400 | tf_op jit(solution)/shard_map/ppermute | solution.py:701
  213.2 3.5 %region_back.1 = (bf16[128,768]{1,0:T(8,128)(2,1)}, bf16[192,256]{1,0:T(8,128)(2,1)}, bf16[192,256]{1,0:T(8,128)(2,1)}, bf16[192,256]{1,0:T(8,128)(2,1)}, bf16[192,256]{1,0:T(8,128)(2,1)}) custom-call(bf16[256,768]{1,0:T(8,128)(2,1)} %bitcast.10.back_ref, bf16[256,128]{1,0:T(8,128)(2,1)} %get-tuple-element.124.hot_ref, ...), custom_call_target="tpu_custom_call" | custom-call | tf_op jit(solution)/shard_map/region_back/pallas_call | solution.py:664
  218.0 2.1 collective-permute-start.18
  221.2 2.7 pair_turn.5
  223.9 2.3 cut.7
  226.2 1.7 collective-permute-done.18.refs_2_
  229.2 3.2 %region_product.1 = (bf16[96,2176]{1,0:T(8,128)(2,1)}, bf16[96,2176]{1,0:T(8,128)(2,1)}) custom-call(bf16[192,256]{1,0:T(8,128)(2,1)} %get-tuple-element.180.refs_0_, bf16[192,256]{1,0:T(8,128)(2,1)} %copy-done.29, bf16[192,256]{1,0:T(8,128)(2,1)} %copy-done.30, bf16[192,256]{1,0:T(8,128)(2,1)} %copy-done.31, bf16[128,2048]{1,0:T(8,128)(2,1)} %refs_4_.1, ...), custom_call_target="tpu_custom_call" | custom-call | tf_op jit(solution)/shard_map/region_product/pallas_call | solution.py:939
  237.0 5.3 %collective-permute-done.30.refs_3_.refs_21_ = bf16[192,768]{1,0:T(8,128)(2,1)S(1)} collective-permute-done((bf16[192,768]{1,0:T(8,128)(2,1)S(1)}, bf16[192,768]{1,0:T(8,128)(2,1)S(1)}, u32[]{:S(2)}, u32[]{:S(2)}) %collective-permute-start.30) | collective-permute-done | bytes 294944 | tf_op jit(solution)/shard_map/ppermute | solution.py:701
  243.0 1.9 cut.11
  244.9 2.0 collective-permute-start.31
  247.6 2.2 cut.8
  250.8 1.9 direct.1
  253.7 1.8 collective-permute-start.22
  255.5 2.9 %convolution_convert_fusion.2 = bf16[128,2048]{1,0:T(8,128)(2,1)} fusion(bf16[128,768]{1,0:T(8,128)(2,1)} %get-tuple-element.200, bf16[2048,768]{1,0:T(8,128)(2,1)S(1)} %copy-done.4), kind=kOutput, calls=%fused_computation.6 | convolution fusion | flops 402915328 | bytes 3866624 | tf_op jit(solution)/shard_map/dot_general | solution.py:33
  259.1 1.9 convolution_convert_fusion.3
  261.0 1.8 cut.9
  262.8 1.9 collective-permute-start.27
  264.7 2.0 cut.10
  268.5 1.8 last_shares.1
  272.5 2.0 slice_reduce_fusion
  275.0 3.3 %collective-permute-done.29.refs_13_ = bf16[24,3840]{1,0:T(8,128)(2,1)S(1)} collective-permute-done((bf16[24,3840]{1,0:T(8,128)(2,1)}, bf16[24,3840]{1,0:T(8,128)(2,1)S(1)}, u32[]{:S(2)}, u32[]{:S(2)}) %collective-permute-start.29) | collective-permute-done | bytes 184352 | tf_op jit(solution)/shard_map/ppermute | solution.py:701
  278.9 3.0 %shares.1 = (f32[24,2304]{1,0:T(8,128)}, f32[24,3072]{1,0:T(8,128)}, f32[24,768]{1,0:T(8,128)}, f32[96,768]{1,0:T(8,128)}) custom-call(bf16[384,2304]{1,0:T(8,128)(2,1)} %get-tuple-element.161.refs_0_.refs_2_.refs_4_.refs_3_, bf16[384,2304]{1,0:T(8,128)(2,1)} %copy-done.1, bf16[192,1152]{1,0:T(8,128)(2,1)} %copy-done.9, bf16[96,1152]{1,0:T(8,128)(2,1)} %copy-done.15, ...), custom_call_target="tpu_custom_call" | custom-call | tf_op jit(solution)/shard_map/shares/pallas_call | solution.py:768
  (146 shorter events, 38.1 us)
Async XLA Ops:
  5.0 11.1 %copy-start.33 = (f32[768]{0:T(1024)S(1)}, f32[768]{0:T(1024)}, u32[]{:S(2)}) copy-start(f32[768]{0:T(1024)} %param.39) | copy-start | bytes 9220
  5.0 11.1 %copy-start.34 = (f32[768]{0:T(1024)S(1)}, f32[768]{0:T(1024)}, u32[]{:S(2)}) copy-start(f32[768]{0:T(1024)} %param.38) | copy-start | bytes 9220
  5.0 11.1 %copy-start.35 = (bf16[512,768]{1,0:T(8,128)(2,1)S(1)}, bf16[512,768]{1,0:T(8,128)(2,1)}, u32[]{:S(2)}) copy-start(bf16[512,768]{1,0:T(8,128)(2,1)} %text_ref.1) | copy-start | bytes 2359300
  5.0 22.4 %all-to-all-start = ((bf16[16,16,896]{2,1,0:T(8,128)(2,1)}), bf16[16,16,896]{2,1,0:T(8,128)(2,1)S(1)}, u32[]{:S(2)}, u32[]{:S(2)}) async-start(bf16[16,16,896]{2,1,0:T(8,128)(2,1)} %bitcast.28), calls=%async_computation | async-start | bytes 917504 | tf_op jit(solution)/shard_map/all_to_all | solution.py:971
  27.4 8.0 %copy-start.21 = (bf16[16,16,896]{2,1,0:T(8,128)(2,1)}, bf16[16,16,896]{2,1,0:T(8,128)(2,1)S(1)}, u32[]{:S(2)}) copy-start(bf16[16,16,896]{2,1,0:T(8,128)(2,1)S(1)} %all-to-all-done) | copy-start | bytes 1376260
  27.4 32.6 %all-to-all-start.1 = ((bf16[16,16,768]{2,1,0:T(8,128)(2,1)}), bf16[16,16,768]{2,1,0:T(8,128)(2,1)S(1)}, u32[]{:S(2)}, u32[]{:S(2)}) async-start(bf16[16,16,768]{2,1,0:T(8,128)(2,1)} %bitcast.5), calls=%async_computation.1 | async-start | bytes 786432 | tf_op jit(solution)/shard_map/all_to_all | solution.py:971
  35.4 55.7 %collective-permute-start = (bf16[128,2048]{1,0:T(8,128)(2,1)S(1)}, bf16[128,2048]{1,0:T(8,128)(2,1)S(1)}, u32[]{:S(2)}, u32[]{:S(2)}) collective-permute-start(bf16[128,2048]{1,0:T(8,128)(2,1)S(1)} %copy-done.14), channel_id=1, source_target_pairs={{0,4},{1,5},{2,6},{3,7},{4,0},{5,1},{6,2},{7,3},{8,12},{9,13},{10,... | collective-permute-start | bytes 1572872 | tf_op jit(solution)/shard_map/ppermute | solution.py:701
  37.3 53.8 %collective-permute-start.1 = (bf16[128,2048]{1,0:T(8,128)(2,1)S(1)}, bf16[128,2048]{1,0:T(8,128)(2,1)S(1)}, u32[]{:S(2)}, u32[]{:S(2)}) collective-permute-start(bf16[128,2048]{1,0:T(8,128)(2,1)S(1)} %copy-done.14), channel_id=1, source_target_pairs={{0,8},{1,9},{2,10},{3,11},{4,12},{5,13},{6,14},{7,15},{8,0},{9,1},... | collective-permute-start | bytes 1572872 | tf_op jit(solution)/shard_map/ppermute | solution.py:701
  39.6 51.4 %collective-permute-start.2 = (bf16[128,2048]{1,0:T(8,128)(2,1)S(1)}, bf16[128,2048]{1,0:T(8,128)(2,1)S(1)}, u32[]{:S(2)}, u32[]{:S(2)}) collective-permute-start(bf16[128,2048]{1,0:T(8,128)(2,1)S(1)} %copy-done.14), channel_id=1, source_target_pairs={{0,12},{1,13},{2,14},{3,15},{4,8},{5,9},{6,10},{7,11},{8,4},{9,5},... | collective-permute-start | bytes 1572872 | tf_op jit(solution)/shard_map/ppermute | solution.py:701
  97.8 5.7 %collective-permute-start.3 = (bf16[1536,768]{1,0:T(8,128)(2,1)}, bf16[1536,768]{1,0:T(8,128)(2,1)S(1)}, u32[]{:S(2)}, u32[]{:S(2)}) collective-permute-start(bf16[1536,768]{1,0:T(8,128)(2,1)} %convolution_convert_fusion), channel_id=1, source_target_pairs={{0,16},{16,0},{1,17},{17,1},{2,18},{18,2},{3,19},{19,3},{4,20},{20... | collective-permute-start | bytes 7077896 | tf_op jit(solution)/shard_map/ppermute | solution.py:697
  110.5 28.4 %collective-permute-start.4 = (bf16[768,384]{1,0:T(8,128)(2,1)}, bf16[768,384]{1,0:T(8,128)(2,1)S(1)}, u32[]{:S(2)}, u32[]{:S(2)}) collective-permute-start(bf16[768,384]{1,0:T(8,128)(2,1)} %get-tuple-element.131), channel_id=1, source_target_pairs={{0,1},{1,0},{2,3},{3,2},{4,5},{5,4},{6,7},{7,6},{8,9},{9,8},{10,11... | collective-permute-start | bytes 1769480 | tf_op jit(solution)/shard_map/ppermute | solution.py:701
  112.4 26.5 %collective-permute-start.5 = (bf16[768,384]{1,0:T(8,128)(2,1)}, bf16[768,384]{1,0:T(8,128)(2,1)S(1)}, u32[]{:S(2)}, u32[]{:S(2)}) collective-permute-start(bf16[768,384]{1,0:T(8,128)(2,1)} %get-tuple-element.132), channel_id=1, source_target_pairs={{0,2},{1,3},{2,0},{3,1},{4,6},{5,7},{6,4},{7,5},{8,10},{9,11},{10,... | collective-permute-start | bytes 1769480 | tf_op jit(solution)/shard_map/ppermute | solution.py:701
  138.9 11.7 %collective-permute-start.6 = (bf16[384,3072]{1,0:T(8,128)(2,1)}, bf16[384,3072]{1,0:T(8,128)(2,1)S(1)}, u32[]{:S(2)}, u32[]{:S(2)}) collective-permute-start(bf16[384,3072]{1,0:T(8,128)(2,1)} %get-tuple-element.149), channel_id=1, source_target_pairs={{0,16},{16,0},{1,17},{17,1},{2,18},{18,2},{3,19},{19,3},{4,20},{20... | collective-permute-start | bytes 7077896 | tf_op jit(solution)/shard_map/ppermute | solution.py:697
  142.4 17.6 %all-to-all-start.2 = ((bf16[16,16,768]{2,1,0:T(8,128)(2,1)}), bf16[16,16,768]{2,1,0:T(8,128)(2,1)}, u32[]{:S(2)}, u32[]{:S(2)}) async-start(bf16[16,16,768]{2,1,0:T(8,128)(2,1)} %bitcast.29), calls=%async_computation.2 | async-start | bytes 786432 | tf_op jit(solution)/shard_map/all_to_all | solution.py:971
  147.1 3.5 %collective-permute-start.7 = (bf16[384,768]{1,0:T(8,128)(2,1)}, bf16[384,768]{1,0:T(8,128)(2,1)S(1)}, u32[]{:S(2)}, u32[]{:S(2)}) collective-permute-start(bf16[384,768]{1,0:T(8,128)(2,1)} %get-tuple-element.151), channel_id=1, source_target_pairs={{0,16},{16,0},{1,17},{17,1},{2,18},{18,2},{3,19},{19,3},{4,20},{20... | collective-permute-start | bytes 1769480 | tf_op jit(solution)/shard_map/ppermute | solution.py:697
  147.2 41.1 %collective-permute-start.10 = (bf16[384,384]{1,0:T(8,128)(2,1)}, bf16[384,384]{1,0:T(8,128)(2,1)S(1)}, u32[]{:S(2)}, u32[]{:S(2)}) collective-permute-start(bf16[384,384]{1,0:T(8,128)(2,1)} %get-tuple-element.143), channel_id=1, source_target_pairs={{0,2},{1,3},{2,0},{3,1},{4,6},{5,7},{6,4},{7,5},{8,10},{9,11},{10,... | collective-permute-start | bytes 884744 | tf_op jit(solution)/shard_map/ppermute | solution.py:701
  149.1 39.1 %collective-permute-start.11 = (bf16[384,384]{1,0:T(8,128)(2,1)}, bf16[384,384]{1,0:T(8,128)(2,1)}, u32[]{:S(2)}, u32[]{:S(2)}) collective-permute-start(bf16[384,384]{1,0:T(8,128)(2,1)} %get-tuple-element.144), channel_id=1, source_target_pairs={{0,1},{1,0},{2,3},{3,2},{4,5},{5,4},{6,7},{7,6},{8,9},{9,8},{10,11... | collective-permute-start | bytes 884744 | tf_op jit(solution)/shard_map/ppermute | solution.py:701
  156.2 32.1 %collective-permute-start.8 = (bf16[192,1920]{1,0:T(8,128)(2,1)}, bf16[192,1920]{1,0:T(8,128)(2,1)S(1)}, u32[]{:S(2)}, u32[]{:S(2)}) collective-permute-start(bf16[192,1920]{1,0:T(8,128)(2,1)} %get-tuple-element.152), channel_id=1, source_target_pairs={{0,1},{1,0},{2,3},{3,2},{4,5},{5,4},{6,7},{7,6},{8,9},{9,8},{10,11... | collective-permute-start | bytes 2211848 | tf_op jit(solution)/shard_map/ppermute | solution.py:701
  156.8 31.5 %collective-permute-start.9 = (bf16[192,1920]{1,0:T(8,128)(2,1)}, bf16[192,1920]{1,0:T(8,128)(2,1)S(1)}, u32[]{:S(2)}, u32[]{:S(2)}) collective-permute-start(bf16[192,1920]{1,0:T(8,128)(2,1)} %get-tuple-element.153), channel_id=1, source_target_pairs={{0,2},{1,3},{2,0},{3,1},{4,6},{5,7},{6,4},{7,5},{8,10},{9,11},{10,... | collective-permute-start | bytes 2211848 | tf_op jit(solution)/shard_map/ppermute | solution.py:701
  188.3 15.1 %copy-start.13 = (bf16[384,384]{1,0:T(8,128)(2,1)}, bf16[384,384]{1,0:T(8,128)(2,1)S(1)}, u32[]{:S(2)}) copy-start(bf16[384,384]{1,0:T(8,128)(2,1)S(1)} %collective-permute-done.10.refs_2_.refs_20_) | copy-start | bytes 884740
  188.3 8.8 %copy-start.5 = (bf16[192,1920]{1,0:T(8,128)(2,1)}, bf16[192,1920]{1,0:T(8,128)(2,1)S(1)}, u32[]{:S(2)}) copy-start(bf16[192,1920]{1,0:T(8,128)(2,1)S(1)} %collective-permute-done.8.refs_2_.refs_10_) | copy-start | bytes 2211844
  188.3 12.1 %copy-start.6 = (bf16[192,1920]{1,0:T(8,128)(2,1)}, bf16[192,1920]{1,0:T(8,128)(2,1)S(1)}, u32[]{:S(2)}) copy-start(bf16[192,1920]{1,0:T(8,128)(2,1)S(1)} %collective-permute-done.9.refs_5_.refs_4_.refs_14_) | copy-start | bytes 2211844
  188.3 4.3 %collective-permute-start.12 = (bf16[384,2304]{1,0:T(8,128)(2,1)}, bf16[384,2304]{1,0:T(8,128)(2,1)S(1)}, u32[]{:S(2)}, u32[]{:S(2)}) collective-permute-start(bf16[384,2304]{1,0:T(8,128)(2,1)} %get-tuple-element.159), channel_id=1, source_target_pairs={{0,16},{16,0},{1,17},{17,1},{2,18},{18,2},{3,19},{19,3},{4,20},{20... | collective-permute-start | bytes 5308424 | tf_op jit(solution)/shard_map/ppermute | solution.py:697
  188.4 19.9 %all-to-all-start.3 = ((bf16[16,16,768]{2,1,0:T(8,128)(2,1)}), bf16[16,16,768]{2,1,0:T(8,128)(2,1)}, u32[]{:S(2)}, u32[]{:S(2)}) async-start(bf16[16,16,768]{2,1,0:T(8,128)(2,1)} %bitcast.30), calls=%async_computation.3 | async-start | bytes 786432 | tf_op jit(solution)/shard_map/all_to_all | solution.py:971
  197.1 15.4 %collective-permute-start.13 = (bf16[192,1152]{1,0:T(8,128)(2,1)}, bf16[192,1152]{1,0:T(8,128)(2,1)S(1)}, u32[]{:S(2)}, u32[]{:S(2)}) collective-permute-start(bf16[192,1152]{1,0:T(8,128)(2,1)} %get-tuple-element.162), channel_id=1, source_target_pairs={{0,1},{1,0},{2,3},{3,2},{4,5},{5,4},{6,7},{7,6},{8,9},{9,8},{10,11... | collective-permute-start | bytes 1327112 | tf_op jit(solution)/shard_map/ppermute | solution.py:701
  198.9 14.3 %collective-permute-start.14 = (bf16[192,1152]{1,0:T(8,128)(2,1)}, bf16[192,1152]{1,0:T(8,128)(2,1)S(1)}, u32[]{:S(2)}, u32[]{:S(2)}) collective-permute-start(bf16[192,1152]{1,0:T(8,128)(2,1)} %get-tuple-element.163), channel_id=1, source_target_pairs={{0,2},{1,3},{2,0},{3,1},{4,6},{5,7},{6,4},{7,5},{8,10},{9,11},{10,... | collective-permute-start | bytes 1327112 | tf_op jit(solution)/shard_map/ppermute | solution.py:701
  203.4 17.7 %collective-permute-start.16 = (bf16[96,1920]{1,0:T(8,128)(2,1)}, bf16[96,1920]{1,0:T(8,128)(2,1)S(1)}, u32[]{:S(2)}, u32[]{:S(2)}) collective-permute-start(bf16[96,1920]{1,0:T(8,128)(2,1)} %get-tuple-element.166), channel_id=1, source_target_pairs={{0,2},{1,3},{2,0},{3,1},{4,6},{5,7},{6,4},{7,5},{8,10},{9,11},{10,... | collective-permute-start | bytes 1105928 | tf_op jit(solution)/shard_map/ppermute | solution.py:701
  204.0 17.2 %collective-permute-start.17 = (bf16[96,1920]{1,0:T(8,128)(2,1)}, bf16[96,1920]{1,0:T(8,128)(2,1)S(1)}, u32[]{:S(2)}, u32[]{:S(2)}) collective-permute-start(bf16[96,1920]{1,0:T(8,128)(2,1)} %get-tuple-element.167), channel_id=1, source_target_pairs={{0,1},{1,0},{2,3},{3,2},{4,5},{5,4},{6,7},{7,6},{8,9},{9,8},{10,11... | collective-permute-start | bytes 1105928 | tf_op jit(solution)/shard_map/ppermute | solution.py:701
  212.5 8.6 %copy-start.9 = (bf16[192,1152]{1,0:T(8,128)(2,1)}, bf16[192,1152]{1,0:T(8,128)(2,1)S(1)}, u32[]{:S(2)}) copy-start(bf16[192,1152]{1,0:T(8,128)(2,1)S(1)} %collective-permute-done.13.refs_2_) | copy-start | bytes 1327108
  213.2 8.0 %copy-start.10 = (bf16[192,1152]{1,0:T(8,128)(2,1)}, bf16[192,1152]{1,0:T(8,128)(2,1)S(1)}, u32[]{:S(2)}) copy-start(bf16[192,1152]{1,0:T(8,128)(2,1)S(1)} %collective-permute-done.14.refs_5_.refs_4_.refs_6_) | copy-start | bytes 1327108
  216.7 9.5 %collective-permute-start.15 = (bf16[192,256]{1,0:T(8,128)(2,1)}, bf16[192,256]{1,0:T(8,128)(2,1)S(1)}, u32[]{:S(2)}, u32[]{:S(2)}) collective-permute-start(bf16[192,256]{1,0:T(8,128)(2,1)} %get-tuple-element.181), channel_id=1, source_target_pairs={{0,4},{1,5},{2,6},{3,7},{4,0},{5,1},{6,2},{7,3},{8,12},{9,13},{10,... | collective-permute-start | bytes 294920 | tf_op jit(solution)/shard_map/ppermute | solution.py:701
  218.0 9.9 %collective-permute-start.18 = (bf16[192,256]{1,0:T(8,128)(2,1)}, bf16[192,256]{1,0:T(8,128)(2,1)S(1)}, u32[]{:S(2)}, u32[]{:S(2)}) collective-permute-start(bf16[192,256]{1,0:T(8,128)(2,1)} %get-tuple-element.186), channel_id=1, source_target_pairs={{0,8},{1,9},{2,10},{3,11},{4,12},{5,13},{6,14},{7,15},{8,0},{9,1},... | collective-permute-start | bytes 294920 | tf_op jit(solution)/shard_map/ppermute | solution.py:701
  220.1 7.8 %collective-permute-start.19 = (bf16[192,256]{1,0:T(8,128)(2,1)}, bf16[192,256]{1,0:T(8,128)(2,1)S(1)}, u32[]{:S(2)}, u32[]{:S(2)}) collective-permute-start(bf16[192,256]{1,0:T(8,128)(2,1)} %get-tuple-element.187), channel_id=1, source_target_pairs={{0,12},{1,13},{2,14},{3,15},{4,8},{5,9},{6,10},{7,11},{8,4},{9,5},... | collective-permute-start | bytes 294920 | tf_op jit(solution)/shard_map/ppermute | solution.py:701
  226.2 8.6 %copy-start.36 = (bf16[96,1152]{1,0:T(8,128)(2,1)S(1)}, bf16[96,1152]{1,0:T(8,128)(2,1)}, u32[]{:S(2)}) copy-start(bf16[96,1152]{1,0:T(8,128)(2,1)} %get-tuple-element.185) | copy-start | bytes 663556
  232.4 18.5 %collective-permute-start.20 = (bf16[96,2176]{1,0:T(8,128)(2,1)}, bf16[96,2176]{1,0:T(8,128)(2,1)}, u32[]{:S(2)}, u32[]{:S(2)}) collective-permute-start(bf16[96,2176]{1,0:T(8,128)(2,1)} %get-tuple-element.194), channel_id=1, source_target_pairs={{0,16},{16,0},{1,17},{17,1},{2,18},{18,2},{3,19},{19,3},{4,20},{20... | collective-permute-start | bytes 1253384 | tf_op jit(solution)/shard_map/ppermute | solution.py:697
  232.4 9.9 %collective-permute-start.30 = (bf16[192,768]{1,0:T(8,128)(2,1)S(1)}, bf16[192,768]{1,0:T(8,128)(2,1)S(1)}, u32[]{:S(2)}, u32[]{:S(2)}) collective-permute-start(bf16[192,768]{1,0:T(8,128)(2,1)S(1)} %copy-done.23), channel_id=1, source_target_pairs={{0,4},{1,5},{2,6},{3,7},{4,0},{5,1},{6,2},{7,3},{8,12},{9,13},{10,... | collective-permute-start | bytes 884744 | tf_op jit(solution)/shard_map/ppermute | solution.py:701
  233.4 13.5 %collective-permute-start.24 = (bf16[96,1152]{1,0:T(8,128)(2,1)S(1)}, bf16[96,1152]{1,0:T(8,128)(2,1)S(1)}, u32[]{:S(2)}, u32[]{:S(2)}) collective-permute-start(bf16[96,1152]{1,0:T(8,128)(2,1)S(1)} %copy-done.37), channel_id=1, source_target_pairs={{0,2},{1,3},{2,0},{3,1},{4,6},{5,7},{6,4},{7,5},{8,10},{9,11},{10,... | collective-permute-start | bytes 663560 | tf_op jit(solution)/shard_map/ppermute | solution.py:701
  234.8 12.1 %collective-permute-start.25 = (bf16[96,1152]{1,0:T(8,128)(2,1)S(1)}, bf16[96,1152]{1,0:T(8,128)(2,1)}, u32[]{:S(2)}, u32[]{:S(2)}) collective-permute-start(bf16[96,1152]{1,0:T(8,128)(2,1)S(1)} %copy-done.36), channel_id=1, source_target_pairs={{0,1},{1,0},{2,3},{3,2},{4,5},{5,4},{6,7},{7,6},{8,9},{9,8},{10,11... | collective-permute-start | bytes 663560 | tf_op jit(solution)/shard_map/ppermute | solution.py:701
  236.0 26.8 %collective-permute-start.28 = (bf16[48,3840]{1,0:T(8,128)(2,1)}, bf16[48,3840]{1,0:T(8,128)(2,1)}, u32[]{:S(2)}, u32[]{:S(2)}) collective-permute-start(bf16[48,3840]{1,0:T(8,128)(2,1)} %cut.7), channel_id=1, source_target_pairs={{0,4},{1,5},{2,6},{3,7},{4,0},{5,1},{6,2},{7,3},{8,12},{9,13},{10,... | collective-permute-start | bytes 1105928 | tf_op jit(solution)/shard_map/ppermute | solution.py:701
  244.9 21.8 %collective-permute-start.31 = (bf16[96,768]{1,0:T(8,128)(2,1)}, bf16[96,768]{1,0:T(8,128)(2,1)S(1)}, u32[]{:S(2)}, u32[]{:S(2)}) collective-permute-start(bf16[96,768]{1,0:T(8,128)(2,1)} %cut.11), channel_id=1, source_target_pairs={{0,8},{1,9},{2,10},{3,11},{4,12},{5,13},{6,14},{7,15},{8,0},{9,1},... | collective-permute-start | bytes 442376 | tf_op jit(solution)/shard_map/ppermute | solution.py:701
  247.6 7.9 %copy-start.4 = (bf16[2048,768]{1,0:T(8,128)(2,1)S(1)}, bf16[2048,768]{1,0:T(8,128)(2,1)}, u32[]{:S(2)}) copy-start(bf16[2048,768]{1,0:T(8,128)(2,1)} %w_ref.1) | copy-start | bytes 9437188
  249.8 8.6 %collective-permute-start.26 = (bf16[48,2304]{1,0:T(8,128)(2,1)}, bf16[48,2304]{1,0:T(8,128)(2,1)S(1)}, u32[]{:S(2)}, u32[]{:S(2)}) collective-permute-start(bf16[48,2304]{1,0:T(8,128)(2,1)} %cut.8), channel_id=1, source_target_pairs={{0,4},{1,5},{2,6},{3,7},{4,0},{5,1},{6,2},{7,3},{8,12},{9,13},{10,... | collective-permute-start | bytes 663560 | tf_op jit(solution)/shard_map/ppermute | solution.py:701
  252.7 15.1 %collective-permute-start.21 = (bf16[24,2176]{1,0:T(8,128)(2,1)}, bf16[24,2176]{1,0:T(8,128)(2,1)}, u32[]{:S(2)}, u32[]{:S(2)}) collective-permute-start(bf16[24,2176]{1,0:T(8,128)(2,1)} %get-tuple-element.195), channel_id=1, source_target_pairs={{0,1},{1,0},{2,3},{3,2},{4,5},{5,4},{6,7},{7,6},{8,9},{9,8},{10,11... | collective-permute-start | bytes 313352 | tf_op jit(solution)/shard_map/ppermute | solution.py:701
  253.7 14.1 %collective-permute-start.22 = (bf16[24,2176]{1,0:T(8,128)(2,1)}, bf16[24,2176]{1,0:T(8,128)(2,1)}, u32[]{:S(2)}, u32[]{:S(2)}) collective-permute-start(bf16[24,2176]{1,0:T(8,128)(2,1)} %get-tuple-element.196), channel_id=1, source_target_pairs={{0,3},{1,2},{2,1},{3,0},{4,7},{5,6},{6,5},{7,4},{8,11},{9,10},{10,... | collective-permute-start | bytes 313352 | tf_op jit(solution)/shard_map/ppermute | solution.py:701
  258.3 9.5 %collective-permute-start.23 = (bf16[24,2176]{1,0:T(8,128)(2,1)}, bf16[24,2176]{1,0:T(8,128)(2,1)S(1)}, u32[]{:S(2)}, u32[]{:S(2)}) collective-permute-start(bf16[24,2176]{1,0:T(8,128)(2,1)} %get-tuple-element.197), channel_id=1, source_target_pairs={{0,2},{1,3},{2,0},{3,1},{4,6},{5,7},{6,4},{7,5},{8,10},{9,11},{10,... | collective-permute-start | bytes 313352 | tf_op jit(solution)/shard_map/ppermute | solution.py:701
  262.8 12.2 %collective-permute-start.27 = (bf16[24,2304]{1,0:T(8,128)(2,1)}, bf16[24,2304]{1,0:T(8,128)(2,1)S(1)}, u32[]{:S(2)}, u32[]{:S(2)}) collective-permute-start(bf16[24,2304]{1,0:T(8,128)(2,1)} %cut.9), channel_id=1, source_target_pairs={{0,8},{1,9},{2,10},{3,11},{4,12},{5,13},{6,14},{7,15},{8,0},{9,1},... | collective-permute-start | bytes 331784 | tf_op jit(solution)/shard_map/ppermute | solution.py:701
  266.7 11.6 %copy-start.26 = (bf16[96,768]{1,0:T(8,128)(2,1)}, bf16[96,768]{1,0:T(8,128)(2,1)S(1)}, u32[]{:S(2)}) copy-start(bf16[96,768]{1,0:T(8,128)(2,1)S(1)} %collective-permute-done.31.refs_22_) | copy-start | bytes 442372
  266.7 11.6 %collective-permute-start.29 = (bf16[24,3840]{1,0:T(8,128)(2,1)}, bf16[24,3840]{1,0:T(8,128)(2,1)S(1)}, u32[]{:S(2)}, u32[]{:S(2)}) collective-permute-start(bf16[24,3840]{1,0:T(8,128)(2,1)} %cut.10), channel_id=1, source_target_pairs={{0,8},{1,9},{2,10},{3,11},{4,12},{5,13},{6,14},{7,15},{8,0},{9,1},... | collective-permute-start | bytes 552968 | tf_op jit(solution)/shard_map/ppermute | solution.py:701
  (27 other events, 63.6 us)
where the time goes:
time: 283 us; the launch traced here: 282 us
  Pallas kernels  155 us (55%)
  starting transfers between devices  57.3 us (20%)
  matrix products  25.1 us (9%)
  waiting for transfers between devices  23.1 us (8%)
  local copies, waits for them, and re-layouts  16.6 us (6%)
  other arithmetic  3.8 us (1%)
    ppermute x27, starting transfers between devices, swap_chips(): lax.ppermute(sent, 'dp', [(peer, peer ^ mask) for peer in range(peers)])  35.9 us
    pallas_call x14, Pallas kernels, combine(): pl.pallas_call(functools.partial(combine_body, plans, len(operands)), gri...  34.4 us
    pallas_call x1, Pallas kernels, feed_forward(): pl.pallas_call(feed_body, grid=(units // chunk,), in_specs=[whole((count,...  30.3 us
    pallas_call x1, Pallas kernels, attend_back(): pl.pallas_call(attend_back_body, grid=(PAIRS,), in_specs=thirds(text_coun...  28.3 us
    pallas_call x1, Pallas kernels, feed_back(): pl.pallas_call(feed_back_body, grid=(units // chunk,), in_specs=[whole((c...  25 us
    all_to_all x4, starting transfers between devices, exchange(): return lax.all_to_all(array, 'dp', split_axis=0, concat_axis=0, tiled=True)  21.2 us
    pallas_call x1, Pallas kernels, attend(): pl.pallas_call(attend_body, grid_spec=pltpu.PrefetchScalarGridSpec(num_sc...  20.2 us
    ppermute x27, waiting for transfers between devices, swap_chips(): lax.ppermute(sent, 'dp', [(peer, peer ^ mask) for peer in range(peers)])  15.7 us
  transfers between devices with their start and end apart: 36, of which 8 were waited for; matrix products, arithmetic and copies ran while one was open for 10% of the time, Pallas kernels for 49%

commit v1 on v0

--- a/solution.py
+++ b/solution.py
@@ -182,20 +182,28 @@
     values = join(text_v_ref, region_v_ref)
     step = 256
     first = head_mask(0)
-    for start in range(0, count, step):
+    tasks = [(start, head) for start in range(0, count, step) for head in range(2)]
+
+    def scores_of(start, head):
+        q_part = jnp.where(head_mask(head), queries[start : start + step], jnp.zeros((), BF16))
+        return dot_nt(q_part, key_rows)
+
+    following, outs, invs = scores_of(*tasks[0]), [], []
+    for index, (start, head) in enumerate(tasks):
         stop = start + step
-        outs, invs = [], []
-        for head in range(2):
-            q_part = jnp.where(head_mask(head), queries[start:stop], jnp.zeros((), BF16))
-            scores = dot_nt(q_part, key_rows) + bias_ref[start:stop, :]
-            exp_terms = jnp.exp(scores - jnp.max(scores, axis=1, keepdims=True))
-            inv = 1.0 / jnp.sum(exp_terms, axis=1, keepdims=True)
-            low_terms = exp_terms.astype(BF16)
-            chance_ref[head, start:stop, :] = low_terms
-            outs.append(dot_nn(low_terms, values) * inv)
-            invs.append(inv)
-        ctx_ref[start:stop, :] = jnp.where(first, outs[0], outs[1]).astype(BF16)
-        inv_ref[start:stop, :] = jnp.where(first, invs[0], invs[1])
+        scores = following + bias_ref[start:stop, :]
+        if index + 1 < len(tasks):
+            following = scores_of(*tasks[index + 1])
+        exp_terms = jnp.exp(scores - jnp.max(scores, axis=1, keepdims=True))
+        inv = 1.0 / jnp.sum(exp_terms, axis=1, keepdims=True)
+        low_terms = exp_terms.astype(BF16)
+        chance_ref[head, start:stop, :] = low_terms
+        outs.append(dot_nn(low_terms, values) * inv)
+        invs.append(inv)
+        if head == 1:
+            ctx_ref[start:stop, :] = jnp.where(first, outs[0], outs[1]).astype(BF16)
+            inv_ref[start:stop, :] = jnp.where(first, invs[0], invs[1])
+            outs, invs = [], []
 
 
 def attend(lengths, arrived, qkv_text, qkv_region):
@@ -261,24 +269,30 @@
     step = 256
     first = head_mask(0)
     keys_turned, values_turned = [None, None], [None, None]
-    for start in range(0, count, step):
-        stop = start + step
-        ques = []
-        for head in range(2):
-            mask = head_mask(head)
-            low, high = head * HDIM, (head + 1) * HDIM
-            low_terms = chance_ref[head, start:stop, :]
-            delta = jnp.sum(jnp.where(mask, product[start:stop], 0.0), axis=1, keepdims=True)
-            d_part = jnp.where(mask, scaled_low[start:stop], jnp.zeros((), BF16))
-            d_chance = dot_nt(d_part, values)
-            d_scores = (low_terms.astype(F32) * (d_chance - delta)).astype(BF16)
-            ques.append(dot_nn(d_scores, key_rows))
-            v_add = dot_nn(scaled_turned[low:high, start:stop], low_terms)
-            k_add = dot_nn(q_turned[low:high, start:stop], d_scores)
-            values_turned[head] = v_add if start == 0 else values_turned[head] + v_add
-            keys_turned[head] = k_add if start == 0 else keys_turned[head] + k_add
-        d_ques = (jnp.where(first, ques[0], ques[1]) * SCALE).astype(BF16)
-        grad_ref[start:stop, :PAIR] = d_ques
+    tasks = [(start, head) for start in range(0, count, step) for head in range(2)]
+
+    def d_chance_of(start, head):
+        d_part = jnp.where(head_mask(head), scaled_low[start : start + step], jnp.zeros((), BF16))
+        return dot_nt(d_part, values)
+
+    following, ques = d_chance_of(*tasks[0]), []
+    for index, (start, head) in enumerate(tasks):
+        stop, low, high = start + step, head * HDIM, (head + 1) * HDIM
+        d_chance = following
+        if index + 1 < len(tasks):
+            following = d_chance_of(*tasks[index + 1])
+        low_terms = chance_ref[head, start:stop, :]
+        delta = jnp.sum(jnp.where(head_mask(head), product[start:stop], 0.0), axis=1, keepdims=True)
+        d_scores = (low_terms.astype(F32) * (d_chance - delta)).astype(BF16)
+        ques.append(dot_nn(d_scores, key_rows))
+        v_add = dot_nn(scaled_turned[low:high, start:stop], low_terms)
+        k_add = dot_nn(q_turned[low:high, start:stop], d_scores)
+        values_turned[head] = v_add if start == 0 else values_turned[head] + v_add
+        keys_turned[head] = k_add if start == 0 else keys_turned[head] + k_add
+        if head == 1:
+            d_ques = (jnp.where(first, ques[0], ques[1]) * SCALE).astype(BF16)
+            grad_ref[start:stop, :PAIR] = d_ques
+            ques = []
     grad_ref[:, PAIR : 2 * PAIR] = jnp.concatenate(keys_turned, axis=0).T.astype(BF16)
     d_values = jnp.concatenate(values_turned, axis=0).T.astype(BF16)
     grad_ref[:, 2 * PAIR :] = d_values
@@ -338,14 +352,14 @@
 
 
 def gelu_parts(inputs):
-    weight = jnp.exp(inputs * inputs * (-0.5))
+    weight = jnp.exp2(inputs * inputs * (-0.5 * 1.4426950408889634))
     place = 1.0 / (1.0 + jnp.abs(inputs) * TAIL_RATE)
-    poly = TAIL[4]
+    poly = 0.5 * TAIL[4]
     for factor in TAIL[3::-1]:
-        poly = poly * place + factor
-    tail = (0.5 * weight) * (poly * place)
+        poly = poly * place + 0.5 * factor
+    tail = weight * (poly * place)
     phi_sum = jnp.where(inputs >= 0.0, 1.0 - tail, tail)
-    return inputs * phi_sum, phi_sum + inputs * (weight * 0.3989422804014327)
+    return inputs * phi_sum, phi_sum + inputs * weight * 0.3989422804014327
 
 
 def feed_body(
@@ -415,8 +429,14 @@
 
         each(first)
 
-    for start, stop in parts:
-        up_sum = dot_nn(low_ref[start:stop, :], w_up_ref[...]) + up_bias_ref[...]
+    def up_of(start, stop):
+        return dot_nn(low_ref[start:stop, :], w_up_ref[...]) + up_bias_ref[...]
+
+    following = up_of(*parts[0])
+    for index, (start, stop) in enumerate(parts):
+        up_sum = following
+        if index + 1 < len(parts):
+            following = up_of(*parts[index + 1])
         value, slope = gelu_parts(up_sum)
         hidden = value.astype(BF16)
         hidden_ref[start:stop, :] = hidden
@@ -538,8 +558,14 @@
         total_ref[...] = d_second_ref[...]
 
     up_total = jnp.zeros(up_sum_ref.shape, F32)
-    for start, stop in parts:
-        d_hidden = dot_nt(d_down_ref[start:stop, :], w_down_ref[...])
+    def hidden_of(start, stop):
+        return dot_nt(d_down_ref[start:stop, :], w_down_ref[...])
+
+    following = hidden_of(*parts[0])
+    for index, (start, stop) in enumerate(parts):
+        d_hidden = following
+        if index + 1 < len(parts):
+            following = hidden_of(*parts[index + 1])
         d_up = (d_hidden * slope_ref[start:stop, :].astype(F32)).astype(BF16)
         d_up_ref[start:stop, :] = d_up
         up_total = up_total + column_sum(d_up.astype(F32))
@@ -1069,19 +1095,21 @@
     )
     up_send, out_send = lax.optimization_barrier((up_send, out_send, *near))[:2]
     got = swap_cores([up_send, out_send])
-    down_sent = down.turn()
+    down.turn()
     down = down.finish()
-    down_got = [array for array, _, _ in down.terms[-down.fresh :]]
     up_out = Pair(
         side_by_side(up_keep, out_keep) + side_by_side(*got), D // 2, (units + D) // 2, units + D, peers
     )
-    returned = exchange(after(region_sent, *down_sent))
-    covered = after(d_ctx, returned, *up_out.start())
+    sent = up_out.start()
     near = up_out.ship()
+    returned = exchange(after(region_sent, *sent))
+    down.hold(*sent)
+    covered = after(d_ctx, *sent, *down.cut(2))
+    far = down.ship()
     qkv_keep, qkv_send, qkv_sums, text_grad, d_rows_region = attend_back(
         qkv_text, qkv_region, w_qkv, chance, chance_inv, context, covered, d_mid, rows_turned
     )
-    qkv_send = after(qkv_send, *near, *down_got)
+    qkv_send = after(qkv_send, returned, *near, *far)
     (got,) = swap_cores([qkv_send])
     sent_back = exchange(after(d_rows_region, qkv_send))
     qkv = Pair([(qkv_keep, 0, 0), (got, 0, 0)], D // 2, 3 * D // 2, 3 * D, peers)
@@ -1090,12 +1118,7 @@
     up_out.hold(*sent)
     sent = up_out.turn()
     up_out = up_out.finish()
-    down.hold(*sent)
-    sent_back = after(sent_back, *qkv_got, *down.cut(1))
-    down.ship()
-    qkv.hold(sent_back)
-    qkv_sent = qkv.turn()
-    qkv = qkv.finish()
+    sent_back = after(sent_back, *qkv_got)
 
     share = D // (2 * peers)
     quarter = units // D
@@ -1116,25 +1139,27 @@
     feats_width = region_feats.shape[1]
     up_out.hold(*pieces)
     qkv.hold(*pieces)
-    down.hold(*pieces)
     region_got = swap_near(pieces, peers)
-    qkv_sent = qkv_sent + up_out.cut(1)
+    qkv.turn()
+    qkv = qkv.finish()
+    qkv_got = [array for array, _, _ in qkv.terms[-qkv.fresh :]]
+    sent = up_out.cut(1)
     up_out.ship()
-    region_got = [after(array, *qkv_sent) for array in region_got]
+    region_got = [after(array, *qkv_got, *sent) for array in region_got]
     last_keep, last_send = region_product(pieces[:1] + region_got, [region_feats] + far_feats)
     (got,) = swap_cores([last_send])
     qkv.hold(last_send)
-    down.hold(last_send)
     qkv.cut(1)
     qkv.ship()
-    down.finish(1)
     last_sent, last = direct(
         [(last_keep, 0, 0), (got, 0, 0)], last_keep.shape[0], feats_width + VECS, peers, 4
     )
     qkv.hold(*last_sent)
     up_out.hold(*last_sent)
     down.hold(*last_sent)
-    d_proj, returned = lax.optimization_barrier((d_proj, returned, *last_sent))[:2]
+    sent = up_out.cut(1)
+    up_out.ship()
+    d_proj, returned = lax.optimization_barrier((d_proj, returned, *sent))[:2]
     region_out = dot_tn(hot, returned).astype(BF16)
     feats_grad = dot_nt(d_proj, w_region).astype(BF16)
     starts = [(3 * pair + part) * PAIR for part in range(3) for pair in range(PAIRS)]
@@ -1142,7 +1167,7 @@
     w_qkv_share, w_up_share, w_out_share, w_down_share = combine(
         qkv.finish(1).shares(heads)
         + up_out.finish(1).shares([(0, units)], [(units, units + D)])
-        + down.finish(1).shares([(0, D)]),
+        + down.finish(2).shares([(0, D)]),
         "shares",
     )
     w_region_share, vectors = combine(

time: 283 us -> 277 us (0.979)
  Pallas kernels: 155 us -> 149 us
    all_to_all x4, starting transfers between devices: 21.2 us -> 25 us  [exchange(): return lax.all_to_all(array, 'dp', split_axis=0, concat_axis=0, tiled=True)]
    ppermute x27 -> x28, waiting for transfers between devices: 15.7 us -> 13.1 us  [swap_chips(): lax.ppermute(sent, 'dp', [(peer, peer ^ mask) for peer in range(peers)])]
    ppermute x27 -> x28, starting transfers between devices: 35.9 us -> 33.4 us  [swap_chips(): lax.ppermute(sent, 'dp', [(peer, peer ^ mask) for peer in range(peers)])]
    pallas_call x14 -> x13, Pallas kernels: 34.4 us -> 32.5 us  [combine(): pl.pallas_call(functools.partial(combine_body, plans, len(operands)), gri...]
    unnamed x79 -> x85, local copies, waits for them, and re-layouts: 11.7 us -> 12.7 us
  transfers between devices with their start and end apart: 36 -> 37, of which waited for: 8 -> 7; matrix products, arithmetic and copies ran while one was open for 10% -> 10% of each run, Pallas kernels for 49% -> 48%
where the time goes in v1:
time: 277 us; the launch traced here: 276 us
  Pallas kernels  149 us (54%)
  starting transfers between devices  59 us (21%)
  matrix products  24.2 us (9%)
  waiting for transfers between devices  20.5 us (7%)
  local copies, waits for them, and re-layouts  17.6 us (6%)
  other arithmetic  3.78 us (1%)
    ppermute x28, starting transfers between devices, swap_chips(): lax.ppermute(sent, 'dp', [(peer, peer ^ mask) for peer in range(peers)])  33.4 us
    pallas_call x13, Pallas kernels, combine(): pl.pallas_call(functools.partial(combine_body, plans, len(operands)), gri...  32.5 us
    pallas_call x1, Pallas kernels, attend_back(): pl.pallas_call(attend_back_body, grid=(PAIRS,), in_specs=thirds(text_coun...  28.6 us
    pallas_call x1, Pallas kernels, feed_forward(): pl.pallas_call(feed_body, grid=(units // chunk,), in_specs=[whole((count,...  27.7 us
    all_to_all x4, starting transfers between devices, exchange(): return lax.all_to_all(array, 'dp', split_axis=0, concat_axis=0, tiled=True)  25 us
    pallas_call x1, Pallas kernels, feed_back(): pl.pallas_call(feed_back_body, grid=(units // chunk,), in_specs=[whole((c...  23.7 us
    pallas_call x1, Pallas kernels, attend(): pl.pallas_call(attend_body, grid_spec=pltpu.PrefetchScalarGridSpec(num_sc...  20.3 us
    ppermute x28, waiting for transfers between devices, swap_chips(): lax.ppermute(sent, 'dp', [(peer, peer ^ mask) for peer in range(peers)])  13.1 us
  transfers between devices with their start and end apart: 37, of which 7 were waited for; matrix products, arithmetic and copies ran while one was open for 10% of the time, Pallas kernels for 48%

profile of v1, /device:TPU:0, one launch (start us, length us, event | category | flops | bytes accessed | tf_op | source)
XLA Modules:
  0.0 275.8 jit_solution(8898645747573222412)
XLA Ops:
  0.7 4.3 %region_forward.1 = (bf16[256,896]{1,0:T(8,128)(2,1)}, bf16[256,768]{1,0:T(8,128)(2,1)}, bf16[256,128]{1,0:T(8,128)(2,1)}, f32[128,768]{1,0:T(8,128)}, f32[128,1]{1,0:T(8,128)}) custom-call(bf16[128,2048]{1,0:T(8,128)(2,1)} %refs_4_.1, bf16[2048,768]{1,0:T(8,128)(2,1)} %w_ref.1, f32[4,128]{1,0:T(4,128)} %boxes_ref.3, s32[1,128]{1,0:T(1,128)} %bitcast.33, ...), custom_call_target="tpu_custom_call" | custom-call | flops 402653184 | bytes 3670016 | tf_op jit(solution)/shard_map/region_forward/pallas_call | solution.py:121
  5.0 8.5 %all-to-all-start = ((bf16[16,16,896]{2,1,0:T(8,128)(2,1)}), bf16[16,16,896]{2,1,0:T(8,128)(2,1)S(1)}, u32[]{:S(2)}, u32[]{:S(2)}) async-start(bf16[16,16,896]{2,1,0:T(8,128)(2,1)} %bitcast.29), calls=%async_computation | async-start | bytes 917504 | tf_op jit(solution)/shard_map/all_to_all | solution.py:997
  16.1 5.5 %fusion.text_q_ref.text_k_ref.text_v_ref = bf16[512,2304]{1,0:T(8,128)(2,1)} fusion(bf16[512,768]{1,0:T(8,128)(2,1)S(1)} %copy-done.37, bf16[768,2304]{1,0:T(8,128)(2,1)} %w_v_ref.1, f32[2304]{0:T(1024)S(1)} %pad_maximum_fusion), kind=kOutput, calls=%fused_computation.1 | convolution fusion | flops 1814298624 | bytes 6693888 | tf_op jit(solution)/shard_map/dot_general | solution.py:29
  21.6 5.7 %all-to-all-done = bf16[16,16,896]{2,1,0:T(8,128)(2,1)S(1)} async-done(((bf16[16,16,896]{2,1,0:T(8,128)(2,1)}), bf16[16,16,896]{2,1,0:T(8,128)(2,1)S(1)}, u32[]{:S(2)}, u32[]{:S(2)}) %all-to-all-start) | async-done | bytes 458784 | tf_op jit(solution)/shard_map/all_to_all | solution.py:997
  27.4 3.8 %all-to-all-start.1 = ((bf16[16,16,768]{2,1,0:T(8,128)(2,1)}), bf16[16,16,768]{2,1,0:T(8,128)(2,1)S(1)}, u32[]{:S(2)}, u32[]{:S(2)}) async-start(bf16[16,16,768]{2,1,0:T(8,128)(2,1)} %bitcast.5), calls=%async_computation.1 | async-start | bytes 786432 | tf_op jit(solution)/shard_map/all_to_all | solution.py:997
  31.2 4.2 %fusion.1.region_q_ref.region_k_ref.region_v_ref = bf16[256,2304]{1,0:T(8,128)(2,1)} fusion(bf16[768,2304]{1,0:T(8,128)(2,1)} %w_v_ref.1, f32[2304]{0:T(1024)S(1)} %pad_maximum_fusion, bf16[256,896]{1,0:T(8,128)(2,1)S(1)} %bitcast.26), kind=kOutput, calls=%fused_computation.3 | convolution fusion | flops 907149312 | bytes 5124096 | tf_op jit(solution)/shard_map/dot_general | solution.py:29
  35.4 1.9 collective-permute-start
  37.3 2.4 collective-permute-start.1
  39.8 20.3 %attend.1 = (bf16[768,768]{1,0:T(8,128)(2,1)}, bf16[12,768,768]{2,1,0:T(8,128)(2,1)}, f32[768,768]{1,0:T(8,128)}) custom-call(s32[1,5]{1,0:T(1,128)} %lengths_ref.1, bf16[256,896]{1,0:T(8,128)(2,1)} %bitcast.27, bf16[512,2304]{1,0:T(8,128)(2,1)} %fusion.text_q_ref.text_k_ref.text_v_ref, bf16[512,2304]{1,0:T(8,128)(2,1)} %fusion.text_q_ref.text_k_ref.text_v_ref, ...), custom_call_target="tpu_custom_call" | custom-call | flops 7247757312 | bytes 14155776 | tf_op jit(solution)/shard_map/attend/pallas_call | solution.py:212
  60.8 27.7 %feed_forward.1 = (bf16[768,3072]{1,0:T(8,128)(2,1)}, bf16[768,3072]{1,0:T(8,128)(2,1)}, f32[768,768]{1,0:T(8,128)}, f32[768,1]{1,0:T(8,128)}, bf16[768,768]{1,0...) custom-call(bf16[768,768]{1,0:T(8,128)(2,1)} %get-tuple-element.121., ...), custom_call_target="tpu_custom_call" | custom-call | flops 10871635968 | bytes 18874368 | tf_op jit(solution)/shard_map/feed_forward/pallas_call | solution.py:472
  89.6 5.6 %convolution_convert_fusion = bf16[1536,768]{1,0:T(8,128)(2,1)} fusion(bf16[768,768]{1,0:T(8,128)(2,1)} %get-tuple-element.134.d_down_ref, bf16[768,3072]{1,0:T(8,128)(2,1)} %get-tuple-element.131, s32[]{:T(128)S(6)} %select_n.140), kind=kOutput, calls=%fused_computation.4 | convolution fusion | flops 1813118976 | bytes 5898244 | tf_op jit(solution)/shard_map/dot_general | solution.py:37
  95.7 5.1 %convolution_convert_fusion.1.refs_0_.refs_2_.refs_4_.refs_6_ = bf16[1536,768]{1,0:T(8,128)(2,1)} fusion(bf16[768,768]{1,0:T(8,128)(2,1)S(1)} %copy-done.41, bf16[768,3072]{1,0:T(8,128)(2,1)} %get-tuple-element.131, s32[]{:T(128)S(6)} %select_n.139), kind=kOutput, calls=%fused_computation.5 | convolution fusion | flops 1813118976 | bytes 5898244 | tf_op jit(solution)/shard_map/dot_general | solution.py:37
  100.9 1.4 copy-done.2
  102.3 5.6 %cut_units.1 = (bf16[768,384]{1,0:T(8,128)(2,1)}, bf16[768,384]{1,0:T(8,128)(2,1)}, bf16[1536,768]{1,0:T(8,128)(2,1)}) custom-call(s32[16]{0:T(128)} %fusion.41.order_ref, bf16[1536,768]{1,0:T(8,128)(2,1)} %convolution_convert_fusion.1.refs_0_.refs_2_.refs_4_.refs_6_, bf16[1536,768]{1,0:T(8,128)(2,1)} %copy-done.2, ...), custom_call_target="tpu_custom_call" | custom-call | flops 1179648 | bytes 9437184 | tf_op jit(solution)/shard_map/cut_units/pallas_call | solution.py:932
  107.9 1.9 collective-permute-start.4
  109.8 1.5 collective-permute-start.5
  111.3 23.7 %feed_back.1 = (bf16[384,3072]{1,0:T(8,128)(2,1)}, bf16[384,3072]{1,0:T(8,128)(2,1)}, bf16[384,768]{1,0:T(8,128)(2,1)}, bf16[384,768]{1,0:T(8,128)(2,1)}, f32[1,...) custom-call(bf16[768,768]{1,0:T(8,128)(2,1)} %get-tuple-element.134.d_down_ref, ...), custom_call_target="tpu_custom_call" | custom-call | flops 12683575296 | bytes 18874368 | tf_op jit(solution)/shard_map/feed_back/pallas_call | solution.py:603
  136.0 2.5 pair_turn.3
  139.2 1.6 collective-permute-done.7.refs_7_.refs_8_.refs_17_
  142.2 4.0 %pair_start.2 = (bf16[192,1920]{1,0:T(8,128)(2,1)}, bf16[192,1920]{1,0:T(8,128)(2,1)}) custom-call(bf16[384,3072]{1,0:T(8,128)(2,1)} %get-tuple-element.142.refs_0_.refs_2_.refs_4_.refs_3_.refs_8_, bf16[384,3072]{1,0:T(8,128)(2,1)} %copy-done, bf16[384,3072]{1,0:T(8,128)(2,1)} %get-tuple-element.142.refs_0_.refs_2_.refs_4_.refs_3_.refs_8_, ...), custom_call_target="tpu_custom_call" | custom-call | tf_op jit(solution)/shard_map/pair_start/pallas_call | solution.py:794
  148.7 2.3 cut.5
  151.1 1.5 collective-permute-start.12
  152.5 2.4 collective-permute-start.13
  155.5 5.8 %all-to-all-start.2 = ((bf16[16,16,768]{2,1,0:T(8,128)(2,1)}), bf16[16,16,768]{2,1,0:T(8,128)(2,1)S(1)}, u32[]{:S(2)}, u32[]{:S(2)}) async-start(bf16[16,16,768]{2,1,0:T(8,128)(2,1)} %bitcast.7), calls=%async_computation.2 | async-start | bytes 786432 | tf_op jit(solution)/shard_map/all_to_all | solution.py:997
  161.3 28.6 %attend_back.1 = (bf16[384,2304]{1,0:T(8,128)(2,1)}, bf16[384,2304]{1,0:T(8,128)(2,1)}, f32[1,2304]{1,0:T(1,128)}, bf16[512,768]{1,0:T(8,128)(2,1)}, bf16[256,768]{1,0:T(8,128)(2,1)}) custom-call(bf16[512,2304]{1,0:T(8,128)(2,1)} %fusion.text_q_ref.text_k_ref.text_v_ref, bf16[512,2304]{1,0:T(8,128)(2,1)} %fusion.text_q_ref.text_k_ref.text_v_ref, ...), custom_call_target="tpu_custom_call" | custom-call | flops 19931332608 | bytes 14155776 | tf_op jit(solution)/shard_map/attend_back/pallas_call | solution.py:320
  190.8 6.9 %all-to-all-start.3 = ((bf16[16,16,768]{2,1,0:T(8,128)(2,1)}), bf16[16,16,768]{2,1,0:T(8,128)(2,1)}, u32[]{:S(2)}, u32[]{:S(2)}) async-start(bf16[16,16,768]{2,1,0:T(8,128)(2,1)} %bitcast.30), calls=%async_computation.3 | async-start | bytes 786432 | tf_op jit(solution)/shard_map/all_to_all | solution.py:997
  199.0 3.2 %pair_start.3 = (bf16[192,1152]{1,0:T(8,128)(2,1)}, bf16[192,1152]{1,0:T(8,128)(2,1)}) custom-call(bf16[384,2304]{1,0:T(8,128)(2,1)} %get-tuple-element.167.refs_0_.refs_2_.refs_4_.refs_3_, bf16[384,2304]{1,0:T(8,128)(2,1)} %copy-done.1, bf16[384,2304]{1,0:T(8,128)(2,1)} %get-tuple-element.167.refs_0_.refs_2_.refs_4_.refs_3_, bf16[384,2304]{1,0:T(8,128)(2,1)} %copy-done.1, ...), custom_call_target="tpu_custom_call" | custom-call | tf_op jit(solution)/shard_map/pair_start/pallas_call | solution.py:794
  202.2 1.9 collective-permute-start.16
  204.1 1.5 collective-permute-start.17
  205.5 3.0 %pair_turn.4 = (bf16[96,1920]{1,0:T(8,128)(2,1)}, bf16[96,1920]{1,0:T(8,128)(2,1)}) custom-call(bf16[384,3072]{1,0:T(8,128)(2,1)} %get-tuple-element.142.refs_0_.refs_2_.refs_4_.refs_3_.refs_8_, bf16[384,3072]{1,0:T(8,128)(2,1)} %copy-done, bf16[192,1920]{1,0:T(8,128)(2,1)} %copy-done.6, ...), custom_call_target="tpu_custom_call" | custom-call | tf_op jit(solution)/shard_map/pair_turn/pallas_call | solution.py:794
  211.3 6.1 %collective-permute-done.16.refs_2_ = bf16[192,1152]{1,0:T(8,128)(2,1)S(1)} collective-permute-done((bf16[192,1152]{1,0:T(8,128)(2,1)}, bf16[192,1152]{1,0:T(8,128)(2,1)S(1)}, u32[]{:S(2)}, u32[]{:S(2)}) %collective-permute-start.16) | collective-permute-done | bytes 442400 | tf_op jit(solution)/shard_map/ppermute | solution.py:727
  218.3 3.5 %region_back.1 = (bf16[128,768]{1,0:T(8,128)(2,1)}, bf16[192,256]{1,0:T(8,128)(2,1)}, bf16[192,256]{1,0:T(8,128)(2,1)}, bf16[192,256]{1,0:T(8,128)(2,1)}, bf16[192,256]{1,0:T(8,128)(2,1)}) custom-call(bf16[256,768]{1,0:T(8,128)(2,1)} %bitcast.10.back_ref, bf16[256,128]{1,0:T(8,128)(2,1)} %get-tuple-element.125.hot_ref, ...), custom_call_target="tpu_custom_call" | custom-call | tf_op jit(solution)/shard_map/region_back/pallas_call | solution.py:690
  221.8 2.5 pair_turn.5
  226.2 1.7 collective-permute-start.21
  227.9 2.0 collective-permute-start.24
  230.7 2.3 cut.6
  233.0 3.6 %collective-permute-done.24.refs_2_ = bf16[192,256]{1,0:T(8,128)(2,1)S(1)} collective-permute-done((bf16[192,256]{1,0:T(8,128)(2,1)S(1)}, bf16[192,256]{1,0:T(8,128)(2,1)S(1)}, u32[]{:S(2)}, u32[]{:S(2)}) %collective-permute-start.24) | collective-permute-done | bytes 98336 | tf_op jit(solution)/shard_map/ppermute | solution.py:727
  237.9 3.2 %region_product.1 = (bf16[96,2176]{1,0:T(8,128)(2,1)}, bf16[96,2176]{1,0:T(8,128)(2,1)}) custom-call(bf16[192,256]{1,0:T(8,128)(2,1)} %get-tuple-element.184.refs_0_, bf16[192,256]{1,0:T(8,128)(2,1)} %copy-done.31, bf16[192,256]{1,0:T(8,128)(2,1)} %copy-done.32, bf16[192,256]{1,0:T(8,128)(2,1)} %copy-done.33, bf16[128,2048]{1,0:T(8,128)(2,1)} %refs_4_.1, ...), custom_call_target="tpu_custom_call" | custom-call | tf_op jit(solution)/shard_map/region_product/pallas_call | solution.py:965
  242.1 2.0 cut.8
  246.0 1.9 direct.1
  251.4 1.4 collective-permute-done.20.refs_4_.refs_12_
  253.6 2.0 cut.7
  255.6 2.2 collective-permute-start.32
  257.8 2.9 %convolution_convert_fusion.2 = bf16[128,2048]{1,0:T(8,128)(2,1)} fusion(bf16[128,768]{1,0:T(8,128)(2,1)} %get-tuple-element.205, bf16[2048,768]{1,0:T(8,128)(2,1)S(1)} %copy-done.5), kind=kOutput, calls=%fused_computation.6 | convolution fusion | flops 402915328 | bytes 3866624 | tf_op jit(solution)/shard_map/dot_general | solution.py:33
  261.6 1.8 cut.9
  264.1 1.8 last_shares.1
  268.2 2.0 slice_reduce_fusion
  272.6 3.0 %shares.1 = (f32[24,2304]{1,0:T(8,128)}, f32[24,3072]{1,0:T(8,128)}, f32[24,768]{1,0:T(8,128)}, f32[96,768]{1,0:T(8,128)}) custom-call(bf16[384,2304]{1,0:T(8,128)(2,1)} %get-tuple-element.167.refs_0_.refs_2_.refs_4_.refs_3_, bf16[384,2304]{1,0:T(8,128)(2,1)} %copy-done.1, bf16[192,1152]{1,0:T(8,128)(2,1)} %copy-done.8, bf16[96,1152]{1,0:T(8,128)(2,1)} %copy-done.15, ...), custom_call_target="tpu_custom_call" | custom-call | tf_op jit(solution)/shard_map/shares/pallas_call | solution.py:794
  (153 shorter events, 34.1 us)
Async XLA Ops:
  5.0 11.1 %copy-start.35 = (f32[768]{0:T(1024)S(1)}, f32[768]{0:T(1024)}, u32[]{:S(2)}) copy-start(f32[768]{0:T(1024)} %param.39) | copy-start | bytes 9220
  5.0 11.1 %copy-start.36 = (f32[768]{0:T(1024)S(1)}, f32[768]{0:T(1024)}, u32[]{:S(2)}) copy-start(f32[768]{0:T(1024)} %param.38) | copy-start | bytes 9220
  5.0 11.1 %copy-start.37 = (bf16[512,768]{1,0:T(8,128)(2,1)S(1)}, bf16[512,768]{1,0:T(8,128)(2,1)}, u32[]{:S(2)}) copy-start(bf16[512,768]{1,0:T(8,128)(2,1)} %text_ref.1) | copy-start | bytes 2359300
  5.0 22.4 %all-to-all-start = ((bf16[16,16,896]{2,1,0:T(8,128)(2,1)}), bf16[16,16,896]{2,1,0:T(8,128)(2,1)S(1)}, u32[]{:S(2)}, u32[]{:S(2)}) async-start(bf16[16,16,896]{2,1,0:T(8,128)(2,1)} %bitcast.29), calls=%async_computation | async-start | bytes 917504 | tf_op jit(solution)/shard_map/all_to_all | solution.py:997
  27.4 8.0 %copy-start.23 = (bf16[16,16,896]{2,1,0:T(8,128)(2,1)}, bf16[16,16,896]{2,1,0:T(8,128)(2,1)S(1)}, u32[]{:S(2)}) copy-start(bf16[16,16,896]{2,1,0:T(8,128)(2,1)S(1)} %all-to-all-done) | copy-start | bytes 1376260
  27.4 32.7 %all-to-all-start.1 = ((bf16[16,16,768]{2,1,0:T(8,128)(2,1)}), bf16[16,16,768]{2,1,0:T(8,128)(2,1)S(1)}, u32[]{:S(2)}, u32[]{:S(2)}) async-start(bf16[16,16,768]{2,1,0:T(8,128)(2,1)} %bitcast.5), calls=%async_computation.1 | async-start | bytes 786432 | tf_op jit(solution)/shard_map/all_to_all | solution.py:997
  35.4 53.1 %collective-permute-start = (bf16[128,2048]{1,0:T(8,128)(2,1)S(1)}, bf16[128,2048]{1,0:T(8,128)(2,1)S(1)}, u32[]{:S(2)}, u32[]{:S(2)}) collective-permute-start(bf16[128,2048]{1,0:T(8,128)(2,1)S(1)} %copy-done.14), channel_id=1, source_target_pairs={{0,4},{1,5},{2,6},{3,7},{4,0},{5,1},{6,2},{7,3},{8,12},{9,13},{10,... | collective-permute-start | bytes 1572872 | tf_op jit(solution)/shard_map/ppermute | solution.py:727
  37.3 51.2 %collective-permute-start.1 = (bf16[128,2048]{1,0:T(8,128)(2,1)S(1)}, bf16[128,2048]{1,0:T(8,128)(2,1)S(1)}, u32[]{:S(2)}, u32[]{:S(2)}) collective-permute-start(bf16[128,2048]{1,0:T(8,128)(2,1)S(1)} %copy-done.14), channel_id=1, source_target_pairs={{0,8},{1,9},{2,10},{3,11},{4,12},{5,13},{6,14},{7,15},{8,0},{9,1},... | collective-permute-start | bytes 1572872 | tf_op jit(solution)/shard_map/ppermute | solution.py:727
  39.6 48.9 %collective-permute-start.2 = (bf16[128,2048]{1,0:T(8,128)(2,1)S(1)}, bf16[128,2048]{1,0:T(8,128)(2,1)S(1)}, u32[]{:S(2)}, u32[]{:S(2)}) collective-permute-start(bf16[128,2048]{1,0:T(8,128)(2,1)S(1)} %copy-done.14), channel_id=1, source_target_pairs={{0,12},{1,13},{2,14},{3,15},{4,8},{5,9},{6,10},{7,11},{8,4},{9,5},... | collective-permute-start | bytes 1572872 | tf_op jit(solution)/shard_map/ppermute | solution.py:727
  95.2 5.7 %collective-permute-start.3 = (bf16[1536,768]{1,0:T(8,128)(2,1)}, bf16[1536,768]{1,0:T(8,128)(2,1)S(1)}, u32[]{:S(2)}, u32[]{:S(2)}) collective-permute-start(bf16[1536,768]{1,0:T(8,128)(2,1)} %convolution_convert_fusion), channel_id=1, source_target_pairs={{0,16},{16,0},{1,17},{17,1},{2,18},{18,2},{3,19},{19,3},{4,20},{20... | collective-permute-start | bytes 7077896 | tf_op jit(solution)/shard_map/ppermute | solution.py:723
  107.9 27.1 %collective-permute-start.4 = (bf16[768,384]{1,0:T(8,128)(2,1)}, bf16[768,384]{1,0:T(8,128)(2,1)S(1)}, u32[]{:S(2)}, u32[]{:S(2)}) collective-permute-start(bf16[768,384]{1,0:T(8,128)(2,1)} %get-tuple-element.132), channel_id=1, source_target_pairs={{0,1},{1,0},{2,3},{3,2},{4,5},{5,4},{6,7},{7,6},{8,9},{9,8},{10,11... | collective-permute-start | bytes 1769480 | tf_op jit(solution)/shard_map/ppermute | solution.py:727
  109.8 25.2 %collective-permute-start.5 = (bf16[768,384]{1,0:T(8,128)(2,1)}, bf16[768,384]{1,0:T(8,128)(2,1)S(1)}, u32[]{:S(2)}, u32[]{:S(2)}) collective-permute-start(bf16[768,384]{1,0:T(8,128)(2,1)} %get-tuple-element.133), channel_id=1, source_target_pairs={{0,2},{1,3},{2,0},{3,1},{4,6},{5,7},{6,4},{7,5},{8,10},{9,11},{10,... | collective-permute-start | bytes 1769480 | tf_op jit(solution)/shard_map/ppermute | solution.py:727
  135.0 5.8 %collective-permute-start.6 = (bf16[384,3072]{1,0:T(8,128)(2,1)}, bf16[384,3072]{1,0:T(8,128)(2,1)S(1)}, u32[]{:S(2)}, u32[]{:S(2)}) collective-permute-start(bf16[384,3072]{1,0:T(8,128)(2,1)} %get-tuple-element.145), channel_id=1, source_target_pairs={{0,16},{16,0},{1,17},{17,1},{2,18},{18,2},{3,19},{19,3},{4,20},{20... | collective-permute-start | bytes 7077896 | tf_op jit(solution)/shard_map/ppermute | solution.py:723
  135.1 5.7 %collective-permute-start.7 = (bf16[384,768]{1,0:T(8,128)(2,1)}, bf16[384,768]{1,0:T(8,128)(2,1)}, u32[]{:S(2)}, u32[]{:S(2)}) collective-permute-start(bf16[384,768]{1,0:T(8,128)(2,1)} %get-tuple-element.147), channel_id=1, source_target_pairs={{0,16},{16,0},{1,17},{17,1},{2,18},{18,2},{3,19},{19,3},{4,20},{20... | collective-permute-start | bytes 1769480 | tf_op jit(solution)/shard_map/ppermute | solution.py:723
  138.5 9.5 %collective-permute-start.8 = (bf16[384,384]{1,0:T(8,128)(2,1)}, bf16[384,384]{1,0:T(8,128)(2,1)S(1)}, u32[]{:S(2)}, u32[]{:S(2)}) collective-permute-start(bf16[384,384]{1,0:T(8,128)(2,1)} %get-tuple-element.151), channel_id=1, source_target_pairs={{0,2},{1,3},{2,0},{3,1},{4,6},{5,7},{6,4},{7,5},{8,10},{9,11},{10,... | collective-permute-start | bytes 884744 | tf_op jit(solution)/shard_map/ppermute | solution.py:727
  139.1 8.9 %collective-permute-start.9 = (bf16[384,384]{1,0:T(8,128)(2,1)}, bf16[384,384]{1,0:T(8,128)(2,1)}, u32[]{:S(2)}, u32[]{:S(2)}) collective-permute-start(bf16[384,384]{1,0:T(8,128)(2,1)} %get-tuple-element.153), channel_id=1, source_target_pairs={{0,1},{1,0},{2,3},{3,2},{4,5},{5,4},{6,7},{7,6},{8,9},{9,8},{10,11... | collective-permute-start | bytes 884744 | tf_op jit(solution)/shard_map/ppermute | solution.py:727
  146.2 43.7 %collective-permute-start.10 = (bf16[192,1920]{1,0:T(8,128)(2,1)}, bf16[192,1920]{1,0:T(8,128)(2,1)S(1)}, u32[]{:S(2)}, u32[]{:S(2)}) collective-permute-start(bf16[192,1920]{1,0:T(8,128)(2,1)} %get-tuple-element.148), channel_id=1, source_target_pairs={{0,1},{1,0},{2,3},{3,2},{4,5},{5,4},{6,7},{7,6},{8,9},{9,8},{10,11... | collective-permute-start | bytes 2211848 | tf_op jit(solution)/shard_map/ppermute | solution.py:727
  146.8 43.2 %collective-permute-start.11 = (bf16[192,1920]{1,0:T(8,128)(2,1)}, bf16[192,1920]{1,0:T(8,128)(2,1)S(1)}, u32[]{:S(2)}, u32[]{:S(2)}) collective-permute-start(bf16[192,1920]{1,0:T(8,128)(2,1)} %get-tuple-element.149), channel_id=1, source_target_pairs={{0,2},{1,3},{2,0},{3,1},{4,6},{5,7},{6,4},{7,5},{8,10},{9,11},{10,... | collective-permute-start | bytes 2211848 | tf_op jit(solution)/shard_map/ppermute | solution.py:727
  151.1 38.8 %collective-permute-start.12 = (bf16[96,768]{1,0:T(8,128)(2,1)}, bf16[96,768]{1,0:T(8,128)(2,1)S(1)}, u32[]{:S(2)}, u32[]{:S(2)}) collective-permute-start(bf16[96,768]{1,0:T(8,128)(2,1)} %get-tuple-element.155), channel_id=1, source_target_pairs={{0,8},{1,9},{2,10},{3,11},{4,12},{5,13},{6,14},{7,15},{8,0},{9,1},... | collective-permute-start | bytes 442376 | tf_op jit(solution)/shard_map/ppermute | solution.py:727
  152.5 37.4 %collective-permute-start.13 = (bf16[96,768]{1,0:T(8,128)(2,1)}, bf16[96,768]{1,0:T(8,128)(2,1)S(1)}, u32[]{:S(2)}, u32[]{:S(2)}) collective-permute-start(bf16[96,768]{1,0:T(8,128)(2,1)} %get-tuple-element.156), channel_id=1, source_target_pairs={{0,4},{1,5},{2,6},{3,7},{4,0},{5,1},{6,2},{7,3},{8,12},{9,13},{10,... | collective-permute-start | bytes 442376 | tf_op jit(solution)/shard_map/ppermute | solution.py:727
  154.9 35.0 %collective-permute-start.14 = (bf16[96,768]{1,0:T(8,128)(2,1)}, bf16[96,768]{1,0:T(8,128)(2,1)S(1)}, u32[]{:S(2)}, u32[]{:S(2)}) collective-permute-start(bf16[96,768]{1,0:T(8,128)(2,1)} %get-tuple-element.157), channel_id=1, source_target_pairs={{0,12},{1,13},{2,14},{3,15},{4,8},{5,9},{6,10},{7,11},{8,4},{9,5},... | collective-permute-start | bytes 442376 | tf_op jit(solution)/shard_map/ppermute | solution.py:727
  155.5 34.5 %all-to-all-start.2 = ((bf16[16,16,768]{2,1,0:T(8,128)(2,1)}), bf16[16,16,768]{2,1,0:T(8,128)(2,1)S(1)}, u32[]{:S(2)}, u32[]{:S(2)}) async-start(bf16[16,16,768]{2,1,0:T(8,128)(2,1)} %bitcast.7), calls=%async_computation.2 | async-start | bytes 786432 | tf_op jit(solution)/shard_map/all_to_all | solution.py:997
  190.0 12.2 %copy-start.6 = (bf16[192,1920]{1,0:T(8,128)(2,1)}, bf16[192,1920]{1,0:T(8,128)(2,1)S(1)}, u32[]{:S(2)}) copy-start(bf16[192,1920]{1,0:T(8,128)(2,1)S(1)} %collective-permute-done.10.refs_2_.refs_10_) | copy-start | bytes 2211844
  190.0 15.5 %copy-start.7 = (bf16[192,1920]{1,0:T(8,128)(2,1)}, bf16[192,1920]{1,0:T(8,128)(2,1)S(1)}, u32[]{:S(2)}) copy-start(bf16[192,1920]{1,0:T(8,128)(2,1)S(1)} %collective-permute-done.11.refs_5_.refs_4_.refs_14_) | copy-start | bytes 2211844
  190.8 7.0 %collective-permute-start.15 = (bf16[384,2304]{1,0:T(8,128)(2,1)}, bf16[384,2304]{1,0:T(8,128)(2,1)S(1)}, u32[]{:S(2)}, u32[]{:S(2)}) collective-permute-start(bf16[384,2304]{1,0:T(8,128)(2,1)} %get-tuple-element.165), channel_id=1, source_target_pairs={{0,16},{16,0},{1,17},{17,1},{2,18},{18,2},{3,19},{19,3},{4,20},{20... | collective-permute-start | bytes 5308424 | tf_op jit(solution)/shard_map/ppermute | solution.py:723
  190.8 20.5 %all-to-all-start.3 = ((bf16[16,16,768]{2,1,0:T(8,128)(2,1)}), bf16[16,16,768]{2,1,0:T(8,128)(2,1)}, u32[]{:S(2)}, u32[]{:S(2)}) async-start(bf16[16,16,768]{2,1,0:T(8,128)(2,1)} %bitcast.30), calls=%async_computation.3 | async-start | bytes 786432 | tf_op jit(solution)/shard_map/all_to_all | solution.py:997
  202.2 15.2 %collective-permute-start.16 = (bf16[192,1152]{1,0:T(8,128)(2,1)}, bf16[192,1152]{1,0:T(8,128)(2,1)S(1)}, u32[]{:S(2)}, u32[]{:S(2)}) collective-permute-start(bf16[192,1152]{1,0:T(8,128)(2,1)} %get-tuple-element.168), channel_id=1, source_target_pairs={{0,1},{1,0},{2,3},{3,2},{4,5},{5,4},{6,7},{7,6},{8,9},{9,8},{10,11... | collective-permute-start | bytes 1327112 | tf_op jit(solution)/shard_map/ppermute | solution.py:727
  204.1 14.2 %collective-permute-start.17 = (bf16[192,1152]{1,0:T(8,128)(2,1)}, bf16[192,1152]{1,0:T(8,128)(2,1)S(1)}, u32[]{:S(2)}, u32[]{:S(2)}) collective-permute-start(bf16[192,1152]{1,0:T(8,128)(2,1)} %get-tuple-element.169), channel_id=1, source_target_pairs={{0,2},{1,3},{2,0},{3,1},{4,6},{5,7},{6,4},{7,5},{8,10},{9,11},{10,... | collective-permute-start | bytes 1327112 | tf_op jit(solution)/shard_map/ppermute | solution.py:727
  208.5 19.4 %collective-permute-start.18 = (bf16[96,1920]{1,0:T(8,128)(2,1)}, bf16[96,1920]{1,0:T(8,128)(2,1)S(1)}, u32[]{:S(2)}, u32[]{:S(2)}) collective-permute-start(bf16[96,1920]{1,0:T(8,128)(2,1)} %get-tuple-element.179), channel_id=1, source_target_pairs={{0,2},{1,3},{2,0},{3,1},{4,6},{5,7},{6,4},{7,5},{8,10},{9,11},{10,... | collective-permute-start | bytes 1105928 | tf_op jit(solution)/shard_map/ppermute | solution.py:727
  209.1 20.8 %collective-permute-start.19 = (bf16[96,1920]{1,0:T(8,128)(2,1)}, bf16[96,1920]{1,0:T(8,128)(2,1)S(1)}, u32[]{:S(2)}, u32[]{:S(2)}) collective-permute-start(bf16[96,1920]{1,0:T(8,128)(2,1)} %get-tuple-element.180), channel_id=1, source_target_pairs={{0,1},{1,0},{2,3},{3,2},{4,5},{5,4},{6,7},{7,6},{8,9},{9,8},{10,11... | collective-permute-start | bytes 1105928 | tf_op jit(solution)/shard_map/ppermute | solution.py:727
  221.8 6.1 %copy-start.39 = (bf16[192,256]{1,0:T(8,128)(2,1)S(1)}, bf16[192,256]{1,0:T(8,128)(2,1)}, u32[]{:S(2)}) copy-start(bf16[192,256]{1,0:T(8,128)(2,1)} %get-tuple-element.186) | copy-start | bytes 294916
  221.8 8.1 %copy-start.38 = (bf16[192,256]{1,0:T(8,128)(2,1)S(1)}, bf16[192,256]{1,0:T(8,128)(2,1)}, u32[]{:S(2)}) copy-start(bf16[192,256]{1,0:T(8,128)(2,1)} %get-tuple-element.187) | copy-start | bytes 294916
  224.3 8.6 %collective-permute-start.22 = (bf16[96,1152]{1,0:T(8,128)(2,1)}, bf16[96,1152]{1,0:T(8,128)(2,1)S(1)}, u32[]{:S(2)}, u32[]{:S(2)}) collective-permute-start(bf16[96,1152]{1,0:T(8,128)(2,1)} %get-tuple-element.192), channel_id=1, source_target_pairs={{0,2},{1,3},{2,0},{3,1},{4,6},{5,7},{6,4},{7,5},{8,10},{9,11},{10,... | collective-permute-start | bytes 663560 | tf_op jit(solution)/shard_map/ppermute | solution.py:727
  225.6 7.4 %collective-permute-start.23 = (bf16[96,1152]{1,0:T(8,128)(2,1)}, bf16[96,1152]{1,0:T(8,128)(2,1)S(1)}, u32[]{:S(2)}, u32[]{:S(2)}) collective-permute-start(bf16[96,1152]{1,0:T(8,128)(2,1)} %get-tuple-element.193), channel_id=1, source_target_pairs={{0,1},{1,0},{2,3},{3,2},{4,5},{5,4},{6,7},{7,6},{8,9},{9,8},{10,11... | collective-permute-start | bytes 663560 | tf_op jit(solution)/shard_map/ppermute | solution.py:727
  226.2 6.8 %collective-permute-start.21 = (bf16[192,256]{1,0:T(8,128)(2,1)S(1)}, bf16[192,256]{1,0:T(8,128)(2,1)S(1)}, u32[]{:S(2)}, u32[]{:S(2)}) collective-permute-start(bf16[192,256]{1,0:T(8,128)(2,1)S(1)} %copy-done.40), channel_id=1, source_target_pairs={{0,4},{1,5},{2,6},{3,7},{4,0},{5,1},{6,2},{7,3},{8,12},{9,13},{10,... | collective-permute-start | bytes 294920 | tf_op jit(solution)/shard_map/ppermute | solution.py:727
  227.9 8.7 %collective-permute-start.24 = (bf16[192,256]{1,0:T(8,128)(2,1)S(1)}, bf16[192,256]{1,0:T(8,128)(2,1)S(1)}, u32[]{:S(2)}, u32[]{:S(2)}) collective-permute-start(bf16[192,256]{1,0:T(8,128)(2,1)S(1)} %copy-done.39), channel_id=1, source_target_pairs={{0,8},{1,9},{2,10},{3,11},{4,12},{5,13},{6,14},{7,15},{8,0},{9,1},... | collective-permute-start | bytes 294920 | tf_op jit(solution)/shard_map/ppermute | solution.py:727
  229.9 6.7 %collective-permute-start.25 = (bf16[192,256]{1,0:T(8,128)(2,1)S(1)}, bf16[192,256]{1,0:T(8,128)(2,1)S(1)}, u32[]{:S(2)}, u32[]{:S(2)}) collective-permute-start(bf16[192,256]{1,0:T(8,128)(2,1)S(1)} %copy-done.38), channel_id=1, source_target_pairs={{0,12},{1,13},{2,14},{3,15},{4,8},{5,9},{6,10},{7,11},{8,4},{9,5},... | collective-permute-start | bytes 294920 | tf_op jit(solution)/shard_map/ppermute | solution.py:727
  233.0 9.2 %copy-start.15 = (bf16[96,1152]{1,0:T(8,128)(2,1)}, bf16[96,1152]{1,0:T(8,128)(2,1)S(1)}, u32[]{:S(2)}) copy-start(bf16[96,1152]{1,0:T(8,128)(2,1)S(1)} %collective-permute-done.22.refs_3_) | copy-start | bytes 663556
  233.0 9.1 %copy-start.16 = (bf16[96,1152]{1,0:T(8,128)(2,1)}, bf16[96,1152]{1,0:T(8,128)(2,1)S(1)}, u32[]{:S(2)}) copy-start(bf16[96,1152]{1,0:T(8,128)(2,1)S(1)} %collective-permute-done.23.refs_5_.refs_6_.refs_7_) | copy-start | bytes 663556
  241.1 4.1 %collective-permute-start.26 = (bf16[96,2176]{1,0:T(8,128)(2,1)}, bf16[96,2176]{1,0:T(8,128)(2,1)S(1)}, u32[]{:S(2)}, u32[]{:S(2)}) collective-permute-start(bf16[96,2176]{1,0:T(8,128)(2,1)} %get-tuple-element.198), channel_id=1, source_target_pairs={{0,16},{16,0},{1,17},{17,1},{2,18},{18,2},{3,19},{19,3},{4,20},{20... | collective-permute-start | bytes 1253384 | tf_op jit(solution)/shard_map/ppermute | solution.py:723
  241.2 11.7 %collective-permute-start.20 = (bf16[48,3840]{1,0:T(8,128)(2,1)}, bf16[48,3840]{1,0:T(8,128)(2,1)S(1)}, u32[]{:S(2)}, u32[]{:S(2)}) collective-permute-start(bf16[48,3840]{1,0:T(8,128)(2,1)} %cut.6), channel_id=1, source_target_pairs={{0,4},{1,5},{2,6},{3,7},{4,0},{5,1},{6,2},{7,3},{8,12},{9,13},{10,... | collective-permute-start | bytes 1105928 | tf_op jit(solution)/shard_map/ppermute | solution.py:727
  244.2 17.4 %collective-permute-start.30 = (bf16[48,2304]{1,0:T(8,128)(2,1)}, bf16[48,2304]{1,0:T(8,128)(2,1)}, u32[]{:S(2)}, u32[]{:S(2)}) collective-permute-start(bf16[48,2304]{1,0:T(8,128)(2,1)} %cut.8), channel_id=1, source_target_pairs={{0,4},{1,5},{2,6},{3,7},{4,0},{5,1},{6,2},{7,3},{8,12},{9,13},{10,... | collective-permute-start | bytes 663560 | tf_op jit(solution)/shard_map/ppermute | solution.py:727
  247.9 16.2 %collective-permute-start.27 = (bf16[24,2176]{1,0:T(8,128)(2,1)}, bf16[24,2176]{1,0:T(8,128)(2,1)}, u32[]{:S(2)}, u32[]{:S(2)}) collective-permute-start(bf16[24,2176]{1,0:T(8,128)(2,1)} %get-tuple-element.199), channel_id=1, source_target_pairs={{0,1},{1,0},{2,3},{3,2},{4,5},{5,4},{6,7},{7,6},{8,9},{9,8},{10,11... | collective-permute-start | bytes 313352 | tf_op jit(solution)/shard_map/ppermute | solution.py:727
  249.3 14.8 %collective-permute-start.28 = (bf16[24,2176]{1,0:T(8,128)(2,1)}, bf16[24,2176]{1,0:T(8,128)(2,1)}, u32[]{:S(2)}, u32[]{:S(2)}) collective-permute-start(bf16[24,2176]{1,0:T(8,128)(2,1)} %get-tuple-element.200), channel_id=1, source_target_pairs={{0,3},{1,2},{2,1},{3,0},{4,7},{5,6},{6,5},{7,4},{8,11},{9,10},{10,... | collective-permute-start | bytes 313352 | tf_op jit(solution)/shard_map/ppermute | solution.py:727
  250.3 7.5 %copy-start.5 = (bf16[2048,768]{1,0:T(8,128)(2,1)S(1)}, bf16[2048,768]{1,0:T(8,128)(2,1)}, u32[]{:S(2)}) copy-start(bf16[2048,768]{1,0:T(8,128)(2,1)} %w_ref.1) | copy-start | bytes 9437188
  250.3 13.8 %collective-permute-start.29 = (bf16[24,2176]{1,0:T(8,128)(2,1)}, bf16[24,2176]{1,0:T(8,128)(2,1)}, u32[]{:S(2)}, u32[]{:S(2)}) collective-permute-start(bf16[24,2176]{1,0:T(8,128)(2,1)} %get-tuple-element.201), channel_id=1, source_target_pairs={{0,2},{1,3},{2,0},{3,1},{4,6},{5,7},{6,4},{7,5},{8,10},{9,11},{10,... | collective-permute-start | bytes 313352 | tf_op jit(solution)/shard_map/ppermute | solution.py:727
  255.6 15.6 %collective-permute-start.32 = (bf16[24,3840]{1,0:T(8,128)(2,1)}, bf16[24,3840]{1,0:T(8,128)(2,1)S(1)}, u32[]{:S(2)}, u32[]{:S(2)}) collective-permute-start(bf16[24,3840]{1,0:T(8,128)(2,1)} %cut.7), channel_id=1, source_target_pairs={{0,8},{1,9},{2,10},{3,11},{4,12},{5,13},{6,14},{7,15},{8,0},{9,1},... | collective-permute-start | bytes 552968 | tf_op jit(solution)/shard_map/ppermute | solution.py:727
  263.4 7.8 %collective-permute-start.31 = (bf16[24,2304]{1,0:T(8,128)(2,1)}, bf16[24,2304]{1,0:T(8,128)(2,1)S(1)}, u32[]{:S(2)}, u32[]{:S(2)}) collective-permute-start(bf16[24,2304]{1,0:T(8,128)(2,1)} %cut.9), channel_id=1, source_target_pairs={{0,8},{1,9},{2,10},{3,11},{4,12},{5,13},{6,14},{7,15},{8,0},{9,1},... | collective-permute-start | bytes 331784 | tf_op jit(solution)/shard_map/ppermute | solution.py:727
  (31 other events, 62.8 us)

commit v2 on v1

--- a/solution.py
+++ b/solution.py
@@ -179,7 +179,7 @@
 
     queries = join(text_q_ref, region_q_ref) * jnp.asarray(SCALE, BF16)
     key_rows = join(text_k_ref, region_k_ref)
-    values = join(text_v_ref, region_v_ref)
+    values = jnp.concatenate([join(text_v_ref, region_v_ref), jnp.ones((count, PAIR), BF16)], axis=1)
     step = 256
     first = head_mask(0)
     tasks = [(start, head) for start in range(0, count, step) for head in range(2)]
@@ -195,10 +195,11 @@
         if index + 1 < len(tasks):
             following = scores_of(*tasks[index + 1])
         exp_terms = jnp.exp(scores - jnp.max(scores, axis=1, keepdims=True))
-        inv = 1.0 / jnp.sum(exp_terms, axis=1, keepdims=True)
         low_terms = exp_terms.astype(BF16)
         chance_ref[head, start:stop, :] = low_terms
-        outs.append(dot_nn(low_terms, values) * inv)
+        summed = dot_nn(low_terms, values)
+        inv = 1.0 / summed[:, PAIR:]
+        outs.append(summed[:, :PAIR] * inv)
         invs.append(inv)
         if head == 1:
             ctx_ref[start:stop, :] = jnp.where(first, outs[0], outs[1]).astype(BF16)

time: 277 us -> 272 us (0.982)
  Pallas kernels: 149 us -> 145 us
    pallas_call x1, Pallas kernels: 20.3 us -> 15.5 us  [attend(): pl.pallas_call(attend_body, grid_spec=pltpu.PrefetchScalarGridSpec(num_sc...]
  transfers between devices with their start and end apart: 37 -> 37, of which waited for: 7 -> 7; matrix products, arithmetic and copies ran while one was open for 10% -> 10% of each run, Pallas kernels for 48% -> 47%
where the time goes in v2:
time: 272 us; the launch traced here: 271 us
  Pallas kernels  145 us (53%)
  starting transfers between devices  59 us (22%)
  matrix products  24.2 us (9%)
  waiting for transfers between devices  20.5 us (8%)
  local copies, waits for them, and re-layouts  17.6 us (6%)
  other arithmetic  3.78 us (1%)
    ppermute x28, starting transfers between devices, swap_chips(): lax.ppermute(sent, 'dp', [(peer, peer ^ mask) for peer in range(peers)])  34.4 us
    pallas_call x13, Pallas kernels, combine(): pl.pallas_call(functools.partial(combine_body, plans, len(operands)), gri...  32.5 us
    pallas_call x1, Pallas kernels, attend_back(): pl.pallas_call(attend_back_body, grid=(PAIRS,), in_specs=thirds(text_coun...  28.6 us
    pallas_call x1, Pallas kernels, feed_forward(): pl.pallas_call(feed_body, grid=(units // chunk,), in_specs=[whole((count,...  27.7 us
    all_to_all x4, starting transfers between devices, exchange(): return lax.all_to_all(array, 'dp', split_axis=0, concat_axis=0, tiled=True)  24 us
    pallas_call x1, Pallas kernels, feed_back(): pl.pallas_call(feed_back_body, grid=(units // chunk,), in_specs=[whole((c...  23.7 us
    pallas_call x1, Pallas kernels, attend(): pl.pallas_call(attend_body, grid_spec=pltpu.PrefetchScalarGridSpec(num_sc...  15.5 us
    ppermute x28, waiting for transfers between devices, swap_chips(): lax.ppermute(sent, 'dp', [(peer, peer ^ mask) for peer in range(peers)])  13.1 us
  transfers between devices with their start and end apart: 37, of which 7 were waited for; matrix products, arithmetic and copies ran while one was open for 10% of the time, Pallas kernels for 47%

profile of v2, /device:TPU:0, one launch (start us, length us, event | category | flops | bytes accessed | tf_op | source)
XLA Modules:
  0.0 271.1 jit_solution(11364996159418076131)
XLA Ops:
  0.7 4.3 %region_forward.1 = (bf16[256,896]{1,0:T(8,128)(2,1)}, bf16[256,768]{1,0:T(8,128)(2,1)}, bf16[256,128]{1,0:T(8,128)(2,1)}, f32[128,768]{1,0:T(8,128)}, f32[128,1]{1,0:T(8,128)}) custom-call(bf16[128,2048]{1,0:T(8,128)(2,1)} %refs_4_.1, bf16[2048,768]{1,0:T(8,128)(2,1)} %w_ref.1, f32[4,128]{1,0:T(4,128)} %boxes_ref.3, s32[1,128]{1,0:T(1,128)} %bitcast.33, ...), custom_call_target="tpu_custom_call" | custom-call | flops 402653184 | bytes 3670016 | tf_op jit(solution)/shard_map/region_forward/pallas_call | solution.py:121
  5.0 8.5 %all-to-all-start = ((bf16[16,16,896]{2,1,0:T(8,128)(2,1)}), bf16[16,16,896]{2,1,0:T(8,128)(2,1)S(1)}, u32[]{:S(2)}, u32[]{:S(2)}) async-start(bf16[16,16,896]{2,1,0:T(8,128)(2,1)} %bitcast.29), calls=%async_computation | async-start | bytes 917504 | tf_op jit(solution)/shard_map/all_to_all | solution.py:998
  16.1 5.5 %fusion.text_q_ref.text_k_ref.text_v_ref = bf16[512,2304]{1,0:T(8,128)(2,1)} fusion(bf16[512,768]{1,0:T(8,128)(2,1)S(1)} %copy-done.37, bf16[768,2304]{1,0:T(8,128)(2,1)} %w_v_ref.1, f32[2304]{0:T(1024)S(1)} %pad_maximum_fusion), kind=kOutput, calls=%fused_computation.1 | convolution fusion | flops 1814298624 | bytes 6693888 | tf_op jit(solution)/shard_map/dot_general | solution.py:29
  21.6 5.7 %all-to-all-done = bf16[16,16,896]{2,1,0:T(8,128)(2,1)S(1)} async-done(((bf16[16,16,896]{2,1,0:T(8,128)(2,1)}), bf16[16,16,896]{2,1,0:T(8,128)(2,1)S(1)}, u32[]{:S(2)}, u32[]{:S(2)}) %all-to-all-start) | async-done | bytes 458784 | tf_op jit(solution)/shard_map/all_to_all | solution.py:998
  27.4 3.8 %all-to-all-start.1 = ((bf16[16,16,768]{2,1,0:T(8,128)(2,1)}), bf16[16,16,768]{2,1,0:T(8,128)(2,1)S(1)}, u32[]{:S(2)}, u32[]{:S(2)}) async-start(bf16[16,16,768]{2,1,0:T(8,128)(2,1)} %bitcast.5), calls=%async_computation.1 | async-start | bytes 786432 | tf_op jit(solution)/shard_map/all_to_all | solution.py:998
  31.2 4.2 %fusion.1.region_q_ref.region_k_ref.region_v_ref = bf16[256,2304]{1,0:T(8,128)(2,1)} fusion(bf16[768,2304]{1,0:T(8,128)(2,1)} %w_v_ref.1, f32[2304]{0:T(1024)S(1)} %pad_maximum_fusion, bf16[256,896]{1,0:T(8,128)(2,1)S(1)} %bitcast.26), kind=kOutput, calls=%fused_computation.3 | convolution fusion | flops 907149312 | bytes 5124096 | tf_op jit(solution)/shard_map/dot_general | solution.py:29
  35.4 1.9 collective-permute-start
  37.3 2.4 collective-permute-start.1
  39.8 15.5 %attend.1 = (bf16[768,768]{1,0:T(8,128)(2,1)}, bf16[12,768,768]{2,1,0:T(8,128)(2,1)}, f32[768,768]{1,0:T(8,128)}) custom-call(s32[1,5]{1,0:T(1,128)} %lengths_ref.1, bf16[256,896]{1,0:T(8,128)(2,1)} %bitcast.27, bf16[512,2304]{1,0:T(8,128)(2,1)} %fusion.text_q_ref.text_k_ref.text_v_ref, bf16[512,2304]{1,0:T(8,128)(2,1)} %fusion.text_q_ref.text_k_ref.text_v_ref, ...), custom_call_target="tpu_custom_call" | custom-call | flops 7247757312 | bytes 14155776 | tf_op jit(solution)/shard_map/attend/pallas_call | solution.py:213
  56.1 27.7 %feed_forward.1 = (bf16[768,3072]{1,0:T(8,128)(2,1)}, bf16[768,3072]{1,0:T(8,128)(2,1)}, f32[768,768]{1,0:T(8,128)}, f32[768,1]{1,0:T(8,128)}, bf16[768,768]{1,0...) custom-call(bf16[768,768]{1,0:T(8,128)(2,1)} %get-tuple-element.121., ...), custom_call_target="tpu_custom_call" | custom-call | flops 10871635968 | bytes 18874368 | tf_op jit(solution)/shard_map/feed_forward/pallas_call | solution.py:473
  84.9 5.6 %convolution_convert_fusion = bf16[1536,768]{1,0:T(8,128)(2,1)} fusion(bf16[768,768]{1,0:T(8,128)(2,1)} %get-tuple-element.134.d_down_ref, bf16[768,3072]{1,0:T(8,128)(2,1)} %get-tuple-element.131, s32[]{:T(128)S(6)} %select_n.140), kind=kOutput, calls=%fused_computation.4 | convolution fusion | flops 1813118976 | bytes 5898244 | tf_op jit(solution)/shard_map/dot_general | solution.py:37
  91.0 5.1 %convolution_convert_fusion.1.refs_0_.refs_2_.refs_4_.refs_6_ = bf16[1536,768]{1,0:T(8,128)(2,1)} fusion(bf16[768,768]{1,0:T(8,128)(2,1)S(1)} %copy-done.41, bf16[768,3072]{1,0:T(8,128)(2,1)} %get-tuple-element.131, s32[]{:T(128)S(6)} %select_n.139), kind=kOutput, calls=%fused_computation.5 | convolution fusion | flops 1813118976 | bytes 5898244 | tf_op jit(solution)/shard_map/dot_general | solution.py:37
  96.1 1.4 copy-done.2
  97.5 5.6 %cut_units.1 = (bf16[768,384]{1,0:T(8,128)(2,1)}, bf16[768,384]{1,0:T(8,128)(2,1)}, bf16[1536,768]{1,0:T(8,128)(2,1)}) custom-call(s32[16]{0:T(128)} %fusion.41.order_ref, bf16[1536,768]{1,0:T(8,128)(2,1)} %convolution_convert_fusion.1.refs_0_.refs_2_.refs_4_.refs_6_, bf16[1536,768]{1,0:T(8,128)(2,1)} %copy-done.2, ...), custom_call_target="tpu_custom_call" | custom-call | flops 1179648 | bytes 9437184 | tf_op jit(solution)/shard_map/cut_units/pallas_call | solution.py:933
  103.2 1.9 collective-permute-start.4
  105.1 1.5 collective-permute-start.5
  106.5 23.7 %feed_back.1 = (bf16[384,3072]{1,0:T(8,128)(2,1)}, bf16[384,3072]{1,0:T(8,128)(2,1)}, bf16[384,768]{1,0:T(8,128)(2,1)}, bf16[384,768]{1,0:T(8,128)(2,1)}, f32[1,...) custom-call(bf16[768,768]{1,0:T(8,128)(2,1)} %get-tuple-element.134.d_down_ref, ...), custom_call_target="tpu_custom_call" | custom-call | flops 12683575296 | bytes 18874368 | tf_op jit(solution)/shard_map/feed_back/pallas_call | solution.py:604
  131.3 2.5 pair_turn.3
  134.5 1.6 collective-permute-done.7.refs_7_.refs_8_.refs_17_
  137.5 4.0 %pair_start.2 = (bf16[192,1920]{1,0:T(8,128)(2,1)}, bf16[192,1920]{1,0:T(8,128)(2,1)}) custom-call(bf16[384,3072]{1,0:T(8,128)(2,1)} %get-tuple-element.142.refs_0_.refs_2_.refs_4_.refs_3_.refs_8_, bf16[384,3072]{1,0:T(8,128)(2,1)} %copy-done, bf16[384,3072]{1,0:T(8,128)(2,1)} %get-tuple-element.142.refs_0_.refs_2_.refs_4_.refs_3_.refs_8_, ...), custom_call_target="tpu_custom_call" | custom-call | tf_op jit(solution)/shard_map/pair_start/pallas_call | solution.py:795
  144.0 2.3 cut.5
  146.3 3.1 %collective-permute-start.12 = (bf16[96,768]{1,0:T(8,128)(2,1)}, bf16[96,768]{1,0:T(8,128)(2,1)S(1)}, u32[]{:S(2)}, u32[]{:S(2)}) collective-permute-start(bf16[96,768]{1,0:T(8,128)(2,1)} %get-tuple-element.155), channel_id=1, source_target_pairs={{0,8},{1,9},{2,10},{3,11},{4,12},{5,13},{6,14},{7,15},{8,0},{9,1},... | collective-permute-start | bytes 442376 | tf_op jit(solution)/shard_map/ppermute | solution.py:728
  150.2 1.6 collective-permute-start.14
  151.8 4.8 %all-to-all-start.2 = ((bf16[16,16,768]{2,1,0:T(8,128)(2,1)}), bf16[16,16,768]{2,1,0:T(8,128)(2,1)S(1)}, u32[]{:S(2)}, u32[]{:S(2)}) async-start(bf16[16,16,768]{2,1,0:T(8,128)(2,1)} %bitcast.7), calls=%async_computation.2 | async-start | bytes 786432 | tf_op jit(solution)/shard_map/all_to_all | solution.py:998
  156.6 28.6 %attend_back.1 = (bf16[384,2304]{1,0:T(8,128)(2,1)}, bf16[384,2304]{1,0:T(8,128)(2,1)}, f32[1,2304]{1,0:T(1,128)}, bf16[512,768]{1,0:T(8,128)(2,1)}, bf16[256,768]{1,0:T(8,128)(2,1)}) custom-call(bf16[512,2304]{1,0:T(8,128)(2,1)} %fusion.text_q_ref.text_k_ref.text_v_ref, bf16[512,2304]{1,0:T(8,128)(2,1)} %fusion.text_q_ref.text_k_ref.text_v_ref, ...), custom_call_target="tpu_custom_call" | custom-call | flops 19931332608 | bytes 14155776 | tf_op jit(solution)/shard_map/attend_back/pallas_call | solution.py:321
  186.1 6.9 %all-to-all-start.3 = ((bf16[16,16,768]{2,1,0:T(8,128)(2,1)}), bf16[16,16,768]{2,1,0:T(8,128)(2,1)}, u32[]{:S(2)}, u32[]{:S(2)}) async-start(bf16[16,16,768]{2,1,0:T(8,128)(2,1)} %bitcast.30), calls=%async_computation.3 | async-start | bytes 786432 | tf_op jit(solution)/shard_map/all_to_all | solution.py:998
  194.3 3.2 %pair_start.3 = (bf16[192,1152]{1,0:T(8,128)(2,1)}, bf16[192,1152]{1,0:T(8,128)(2,1)}) custom-call(bf16[384,2304]{1,0:T(8,128)(2,1)} %get-tuple-element.167.refs_0_.refs_2_.refs_4_.refs_3_, bf16[384,2304]{1,0:T(8,128)(2,1)} %copy-done.1, bf16[384,2304]{1,0:T(8,128)(2,1)} %get-tuple-element.167.refs_0_.refs_2_.refs_4_.refs_3_, bf16[384,2304]{1,0:T(8,128)(2,1)} %copy-done.1, ...), custom_call_target="tpu_custom_call" | custom-call | tf_op jit(solution)/shard_map/pair_start/pallas_call | solution.py:795
  197.4 1.9 collective-permute-start.16
  199.3 1.5 collective-permute-start.17
  200.8 3.0 %pair_turn.4 = (bf16[96,1920]{1,0:T(8,128)(2,1)}, bf16[96,1920]{1,0:T(8,128)(2,1)}) custom-call(bf16[384,3072]{1,0:T(8,128)(2,1)} %get-tuple-element.142.refs_0_.refs_2_.refs_4_.refs_3_.refs_8_, bf16[384,3072]{1,0:T(8,128)(2,1)} %copy-done, bf16[192,1920]{1,0:T(8,128)(2,1)} %copy-done.6, ...), custom_call_target="tpu_custom_call" | custom-call | tf_op jit(solution)/shard_map/pair_turn/pallas_call | solution.py:795
  206.6 6.1 %collective-permute-done.16.refs_2_ = bf16[192,1152]{1,0:T(8,128)(2,1)S(1)} collective-permute-done((bf16[192,1152]{1,0:T(8,128)(2,1)}, bf16[192,1152]{1,0:T(8,128)(2,1)S(1)}, u32[]{:S(2)}, u32[]{:S(2)}) %collective-permute-start.16) | collective-permute-done | bytes 442400 | tf_op jit(solution)/shard_map/ppermute | solution.py:728
  213.5 3.5 %region_back.1 = (bf16[128,768]{1,0:T(8,128)(2,1)}, bf16[192,256]{1,0:T(8,128)(2,1)}, bf16[192,256]{1,0:T(8,128)(2,1)}, bf16[192,256]{1,0:T(8,128)(2,1)}, bf16[192,256]{1,0:T(8,128)(2,1)}) custom-call(bf16[256,768]{1,0:T(8,128)(2,1)} %bitcast.10.back_ref, bf16[256,128]{1,0:T(8,128)(2,1)} %get-tuple-element.125.hot_ref, ...), custom_call_target="tpu_custom_call" | custom-call | tf_op jit(solution)/shard_map/region_back/pallas_call | solution.py:691
  217.1 2.5 pair_turn.5
  221.4 1.7 collective-permute-start.21
  223.2 2.0 collective-permute-start.24
  226.0 2.3 cut.6
  228.3 3.6 %collective-permute-done.24.refs_2_ = bf16[192,256]{1,0:T(8,128)(2,1)S(1)} collective-permute-done((bf16[192,256]{1,0:T(8,128)(2,1)S(1)}, bf16[192,256]{1,0:T(8,128)(2,1)S(1)}, u32[]{:S(2)}, u32[]{:S(2)}) %collective-permute-start.24) | collective-permute-done | bytes 98336 | tf_op jit(solution)/shard_map/ppermute | solution.py:728
  233.2 3.2 %region_product.1 = (bf16[96,2176]{1,0:T(8,128)(2,1)}, bf16[96,2176]{1,0:T(8,128)(2,1)}) custom-call(bf16[192,256]{1,0:T(8,128)(2,1)} %get-tuple-element.184.refs_0_, bf16[192,256]{1,0:T(8,128)(2,1)} %copy-done.31, bf16[192,256]{1,0:T(8,128)(2,1)} %copy-done.32, bf16[192,256]{1,0:T(8,128)(2,1)} %copy-done.33, bf16[128,2048]{1,0:T(8,128)(2,1)} %refs_4_.1, ...), custom_call_target="tpu_custom_call" | custom-call | tf_op jit(solution)/shard_map/region_product/pallas_call | solution.py:966
  237.4 2.0 cut.8
  241.3 1.9 direct.1
  246.7 1.4 collective-permute-done.20.refs_4_.refs_12_
  248.8 2.0 cut.7
  250.9 2.2 collective-permute-start.32
  253.1 2.9 %convolution_convert_fusion.2 = bf16[128,2048]{1,0:T(8,128)(2,1)} fusion(bf16[128,768]{1,0:T(8,128)(2,1)} %get-tuple-element.205, bf16[2048,768]{1,0:T(8,128)(2,1)S(1)} %copy-done.5), kind=kOutput, calls=%fused_computation.6 | convolution fusion | flops 402915328 | bytes 3866624 | tf_op jit(solution)/shard_map/dot_general | solution.py:33
  256.9 1.8 cut.9
  259.4 1.8 last_shares.1
  263.4 2.0 slice_reduce_fusion
  267.8 3.0 %shares.1 = (f32[24,2304]{1,0:T(8,128)}, f32[24,3072]{1,0:T(8,128)}, f32[24,768]{1,0:T(8,128)}, f32[96,768]{1,0:T(8,128)}) custom-call(bf16[384,2304]{1,0:T(8,128)(2,1)} %get-tuple-element.167.refs_0_.refs_2_.refs_4_.refs_3_, bf16[384,2304]{1,0:T(8,128)(2,1)} %copy-done.1, bf16[192,1152]{1,0:T(8,128)(2,1)} %copy-done.8, bf16[96,1152]{1,0:T(8,128)(2,1)} %copy-done.15, ...), custom_call_target="tpu_custom_call" | custom-call | tf_op jit(solution)/shard_map/shares/pallas_call | solution.py:795
  (153 shorter events, 34.2 us)
Async XLA Ops:
  5.0 11.1 %copy-start.35 = (f32[768]{0:T(1024)S(1)}, f32[768]{0:T(1024)}, u32[]{:S(2)}) copy-start(f32[768]{0:T(1024)} %param.39) | copy-start | bytes 9220
  5.0 11.1 %copy-start.36 = (f32[768]{0:T(1024)S(1)}, f32[768]{0:T(1024)}, u32[]{:S(2)}) copy-start(f32[768]{0:T(1024)} %param.38) | copy-start | bytes 9220
  5.0 11.1 %copy-start.37 = (bf16[512,768]{1,0:T(8,128)(2,1)S(1)}, bf16[512,768]{1,0:T(8,128)(2,1)}, u32[]{:S(2)}) copy-start(bf16[512,768]{1,0:T(8,128)(2,1)} %text_ref.1) | copy-start | bytes 2359300
  5.0 22.4 %all-to-all-start = ((bf16[16,16,896]{2,1,0:T(8,128)(2,1)}), bf16[16,16,896]{2,1,0:T(8,128)(2,1)S(1)}, u32[]{:S(2)}, u32[]{:S(2)}) async-start(bf16[16,16,896]{2,1,0:T(8,128)(2,1)} %bitcast.29), calls=%async_computation | async-start | bytes 917504 | tf_op jit(solution)/shard_map/all_to_all | solution.py:998
  27.4 8.0 %copy-start.23 = (bf16[16,16,896]{2,1,0:T(8,128)(2,1)}, bf16[16,16,896]{2,1,0:T(8,128)(2,1)S(1)}, u32[]{:S(2)}) copy-start(bf16[16,16,896]{2,1,0:T(8,128)(2,1)S(1)} %all-to-all-done) | copy-start | bytes 1376260
  27.4 27.9 %all-to-all-start.1 = ((bf16[16,16,768]{2,1,0:T(8,128)(2,1)}), bf16[16,16,768]{2,1,0:T(8,128)(2,1)S(1)}, u32[]{:S(2)}, u32[]{:S(2)}) async-start(bf16[16,16,768]{2,1,0:T(8,128)(2,1)} %bitcast.5), calls=%async_computation.1 | async-start | bytes 786432 | tf_op jit(solution)/shard_map/all_to_all | solution.py:998
  35.4 48.4 %collective-permute-start = (bf16[128,2048]{1,0:T(8,128)(2,1)S(1)}, bf16[128,2048]{1,0:T(8,128)(2,1)S(1)}, u32[]{:S(2)}, u32[]{:S(2)}) collective-permute-start(bf16[128,2048]{1,0:T(8,128)(2,1)S(1)} %copy-done.14), channel_id=1, source_target_pairs={{0,4},{1,5},{2,6},{3,7},{4,0},{5,1},{6,2},{7,3},{8,12},{9,13},{10,... | collective-permute-start | bytes 1572872 | tf_op jit(solution)/shard_map/ppermute | solution.py:728
  37.3 46.5 %collective-permute-start.1 = (bf16[128,2048]{1,0:T(8,128)(2,1)S(1)}, bf16[128,2048]{1,0:T(8,128)(2,1)S(1)}, u32[]{:S(2)}, u32[]{:S(2)}) collective-permute-start(bf16[128,2048]{1,0:T(8,128)(2,1)S(1)} %copy-done.14), channel_id=1, source_target_pairs={{0,8},{1,9},{2,10},{3,11},{4,12},{5,13},{6,14},{7,15},{8,0},{9,1},... | collective-permute-start | bytes 1572872 | tf_op jit(solution)/shard_map/ppermute | solution.py:728
  39.6 44.1 %collective-permute-start.2 = (bf16[128,2048]{1,0:T(8,128)(2,1)S(1)}, bf16[128,2048]{1,0:T(8,128)(2,1)S(1)}, u32[]{:S(2)}, u32[]{:S(2)}) collective-permute-start(bf16[128,2048]{1,0:T(8,128)(2,1)S(1)} %copy-done.14), channel_id=1, source_target_pairs={{0,12},{1,13},{2,14},{3,15},{4,8},{5,9},{6,10},{7,11},{8,4},{9,5},... | collective-permute-start | bytes 1572872 | tf_op jit(solution)/shard_map/ppermute | solution.py:728
  90.5 5.7 %collective-permute-start.3 = (bf16[1536,768]{1,0:T(8,128)(2,1)}, bf16[1536,768]{1,0:T(8,128)(2,1)S(1)}, u32[]{:S(2)}, u32[]{:S(2)}) collective-permute-start(bf16[1536,768]{1,0:T(8,128)(2,1)} %convolution_convert_fusion), channel_id=1, source_target_pairs={{0,16},{16,0},{1,17},{17,1},{2,18},{18,2},{3,19},{19,3},{4,20},{20... | collective-permute-start | bytes 7077896 | tf_op jit(solution)/shard_map/ppermute | solution.py:724
  103.2 27.1 %collective-permute-start.4 = (bf16[768,384]{1,0:T(8,128)(2,1)}, bf16[768,384]{1,0:T(8,128)(2,1)S(1)}, u32[]{:S(2)}, u32[]{:S(2)}) collective-permute-start(bf16[768,384]{1,0:T(8,128)(2,1)} %get-tuple-element.132), channel_id=1, source_target_pairs={{0,1},{1,0},{2,3},{3,2},{4,5},{5,4},{6,7},{7,6},{8,9},{9,8},{10,11... | collective-permute-start | bytes 1769480 | tf_op jit(solution)/shard_map/ppermute | solution.py:728
  105.1 25.2 %collective-permute-start.5 = (bf16[768,384]{1,0:T(8,128)(2,1)}, bf16[768,384]{1,0:T(8,128)(2,1)S(1)}, u32[]{:S(2)}, u32[]{:S(2)}) collective-permute-start(bf16[768,384]{1,0:T(8,128)(2,1)} %get-tuple-element.133), channel_id=1, source_target_pairs={{0,2},{1,3},{2,0},{3,1},{4,6},{5,7},{6,4},{7,5},{8,10},{9,11},{10,... | collective-permute-start | bytes 1769480 | tf_op jit(solution)/shard_map/ppermute | solution.py:728
  130.3 5.8 %collective-permute-start.6 = (bf16[384,3072]{1,0:T(8,128)(2,1)}, bf16[384,3072]{1,0:T(8,128)(2,1)S(1)}, u32[]{:S(2)}, u32[]{:S(2)}) collective-permute-start(bf16[384,3072]{1,0:T(8,128)(2,1)} %get-tuple-element.145), channel_id=1, source_target_pairs={{0,16},{16,0},{1,17},{17,1},{2,18},{18,2},{3,19},{19,3},{4,20},{20... | collective-permute-start | bytes 7077896 | tf_op jit(solution)/shard_map/ppermute | solution.py:724
  130.4 5.7 %collective-permute-start.7 = (bf16[384,768]{1,0:T(8,128)(2,1)}, bf16[384,768]{1,0:T(8,128)(2,1)}, u32[]{:S(2)}, u32[]{:S(2)}) collective-permute-start(bf16[384,768]{1,0:T(8,128)(2,1)} %get-tuple-element.147), channel_id=1, source_target_pairs={{0,16},{16,0},{1,17},{17,1},{2,18},{18,2},{3,19},{19,3},{4,20},{20... | collective-permute-start | bytes 1769480 | tf_op jit(solution)/shard_map/ppermute | solution.py:724
  133.8 9.5 %collective-permute-start.8 = (bf16[384,384]{1,0:T(8,128)(2,1)}, bf16[384,384]{1,0:T(8,128)(2,1)S(1)}, u32[]{:S(2)}, u32[]{:S(2)}) collective-permute-start(bf16[384,384]{1,0:T(8,128)(2,1)} %get-tuple-element.151), channel_id=1, source_target_pairs={{0,2},{1,3},{2,0},{3,1},{4,6},{5,7},{6,4},{7,5},{8,10},{9,11},{10,... | collective-permute-start | bytes 884744 | tf_op jit(solution)/shard_map/ppermute | solution.py:728
  134.3 8.9 %collective-permute-start.9 = (bf16[384,384]{1,0:T(8,128)(2,1)}, bf16[384,384]{1,0:T(8,128)(2,1)}, u32[]{:S(2)}, u32[]{:S(2)}) collective-permute-start(bf16[384,384]{1,0:T(8,128)(2,1)} %get-tuple-element.153), channel_id=1, source_target_pairs={{0,1},{1,0},{2,3},{3,2},{4,5},{5,4},{6,7},{7,6},{8,9},{9,8},{10,11... | collective-permute-start | bytes 884744 | tf_op jit(solution)/shard_map/ppermute | solution.py:728
  141.5 43.7 %collective-permute-start.10 = (bf16[192,1920]{1,0:T(8,128)(2,1)}, bf16[192,1920]{1,0:T(8,128)(2,1)S(1)}, u32[]{:S(2)}, u32[]{:S(2)}) collective-permute-start(bf16[192,1920]{1,0:T(8,128)(2,1)} %get-tuple-element.148), channel_id=1, source_target_pairs={{0,1},{1,0},{2,3},{3,2},{4,5},{5,4},{6,7},{7,6},{8,9},{9,8},{10,11... | collective-permute-start | bytes 2211848 | tf_op jit(solution)/shard_map/ppermute | solution.py:728
  142.1 43.2 %collective-permute-start.11 = (bf16[192,1920]{1,0:T(8,128)(2,1)}, bf16[192,1920]{1,0:T(8,128)(2,1)S(1)}, u32[]{:S(2)}, u32[]{:S(2)}) collective-permute-start(bf16[192,1920]{1,0:T(8,128)(2,1)} %get-tuple-element.149), channel_id=1, source_target_pairs={{0,2},{1,3},{2,0},{3,1},{4,6},{5,7},{6,4},{7,5},{8,10},{9,11},{10,... | collective-permute-start | bytes 2211848 | tf_op jit(solution)/shard_map/ppermute | solution.py:728
  146.3 38.8 %collective-permute-start.12 = (bf16[96,768]{1,0:T(8,128)(2,1)}, bf16[96,768]{1,0:T(8,128)(2,1)S(1)}, u32[]{:S(2)}, u32[]{:S(2)}) collective-permute-start(bf16[96,768]{1,0:T(8,128)(2,1)} %get-tuple-element.155), channel_id=1, source_target_pairs={{0,8},{1,9},{2,10},{3,11},{4,12},{5,13},{6,14},{7,15},{8,0},{9,1},... | collective-permute-start | bytes 442376 | tf_op jit(solution)/shard_map/ppermute | solution.py:728
  149.5 35.7 %collective-permute-start.13 = (bf16[96,768]{1,0:T(8,128)(2,1)}, bf16[96,768]{1,0:T(8,128)(2,1)S(1)}, u32[]{:S(2)}, u32[]{:S(2)}) collective-permute-start(bf16[96,768]{1,0:T(8,128)(2,1)} %get-tuple-element.156), channel_id=1, source_target_pairs={{0,4},{1,5},{2,6},{3,7},{4,0},{5,1},{6,2},{7,3},{8,12},{9,13},{10,... | collective-permute-start | bytes 442376 | tf_op jit(solution)/shard_map/ppermute | solution.py:728
  150.2 35.0 %collective-permute-start.14 = (bf16[96,768]{1,0:T(8,128)(2,1)}, bf16[96,768]{1,0:T(8,128)(2,1)S(1)}, u32[]{:S(2)}, u32[]{:S(2)}) collective-permute-start(bf16[96,768]{1,0:T(8,128)(2,1)} %get-tuple-element.157), channel_id=1, source_target_pairs={{0,12},{1,13},{2,14},{3,15},{4,8},{5,9},{6,10},{7,11},{8,4},{9,5},... | collective-permute-start | bytes 442376 | tf_op jit(solution)/shard_map/ppermute | solution.py:728
  151.8 33.4 %all-to-all-start.2 = ((bf16[16,16,768]{2,1,0:T(8,128)(2,1)}), bf16[16,16,768]{2,1,0:T(8,128)(2,1)S(1)}, u32[]{:S(2)}, u32[]{:S(2)}) async-start(bf16[16,16,768]{2,1,0:T(8,128)(2,1)} %bitcast.7), calls=%async_computation.2 | async-start | bytes 786432 | tf_op jit(solution)/shard_map/all_to_all | solution.py:998
  185.2 12.2 %copy-start.6 = (bf16[192,1920]{1,0:T(8,128)(2,1)}, bf16[192,1920]{1,0:T(8,128)(2,1)S(1)}, u32[]{:S(2)}) copy-start(bf16[192,1920]{1,0:T(8,128)(2,1)S(1)} %collective-permute-done.10.refs_2_.refs_10_) | copy-start | bytes 2211844
  185.3 15.5 %copy-start.7 = (bf16[192,1920]{1,0:T(8,128)(2,1)}, bf16[192,1920]{1,0:T(8,128)(2,1)S(1)}, u32[]{:S(2)}) copy-start(bf16[192,1920]{1,0:T(8,128)(2,1)S(1)} %collective-permute-done.11.refs_5_.refs_4_.refs_14_) | copy-start | bytes 2211844
  186.1 7.0 %collective-permute-start.15 = (bf16[384,2304]{1,0:T(8,128)(2,1)}, bf16[384,2304]{1,0:T(8,128)(2,1)S(1)}, u32[]{:S(2)}, u32[]{:S(2)}) collective-permute-start(bf16[384,2304]{1,0:T(8,128)(2,1)} %get-tuple-element.165), channel_id=1, source_target_pairs={{0,16},{16,0},{1,17},{17,1},{2,18},{18,2},{3,19},{19,3},{4,20},{20... | collective-permute-start | bytes 5308424 | tf_op jit(solution)/shard_map/ppermute | solution.py:724
  186.1 20.5 %all-to-all-start.3 = ((bf16[16,16,768]{2,1,0:T(8,128)(2,1)}), bf16[16,16,768]{2,1,0:T(8,128)(2,1)}, u32[]{:S(2)}, u32[]{:S(2)}) async-start(bf16[16,16,768]{2,1,0:T(8,128)(2,1)} %bitcast.30), calls=%async_computation.3 | async-start | bytes 786432 | tf_op jit(solution)/shard_map/all_to_all | solution.py:998
  197.4 15.2 %collective-permute-start.16 = (bf16[192,1152]{1,0:T(8,128)(2,1)}, bf16[192,1152]{1,0:T(8,128)(2,1)S(1)}, u32[]{:S(2)}, u32[]{:S(2)}) collective-permute-start(bf16[192,1152]{1,0:T(8,128)(2,1)} %get-tuple-element.168), channel_id=1, source_target_pairs={{0,1},{1,0},{2,3},{3,2},{4,5},{5,4},{6,7},{7,6},{8,9},{9,8},{10,11... | collective-permute-start | bytes 1327112 | tf_op jit(solution)/shard_map/ppermute | solution.py:728
  199.3 14.2 %collective-permute-start.17 = (bf16[192,1152]{1,0:T(8,128)(2,1)}, bf16[192,1152]{1,0:T(8,128)(2,1)S(1)}, u32[]{:S(2)}, u32[]{:S(2)}) collective-permute-start(bf16[192,1152]{1,0:T(8,128)(2,1)} %get-tuple-element.169), channel_id=1, source_target_pairs={{0,2},{1,3},{2,0},{3,1},{4,6},{5,7},{6,4},{7,5},{8,10},{9,11},{10,... | collective-permute-start | bytes 1327112 | tf_op jit(solution)/shard_map/ppermute | solution.py:728
  203.8 19.4 %collective-permute-start.18 = (bf16[96,1920]{1,0:T(8,128)(2,1)}, bf16[96,1920]{1,0:T(8,128)(2,1)S(1)}, u32[]{:S(2)}, u32[]{:S(2)}) collective-permute-start(bf16[96,1920]{1,0:T(8,128)(2,1)} %get-tuple-element.179), channel_id=1, source_target_pairs={{0,2},{1,3},{2,0},{3,1},{4,6},{5,7},{6,4},{7,5},{8,10},{9,11},{10,... | collective-permute-start | bytes 1105928 | tf_op jit(solution)/shard_map/ppermute | solution.py:728
  204.4 20.8 %collective-permute-start.19 = (bf16[96,1920]{1,0:T(8,128)(2,1)}, bf16[96,1920]{1,0:T(8,128)(2,1)S(1)}, u32[]{:S(2)}, u32[]{:S(2)}) collective-permute-start(bf16[96,1920]{1,0:T(8,128)(2,1)} %get-tuple-element.180), channel_id=1, source_target_pairs={{0,1},{1,0},{2,3},{3,2},{4,5},{5,4},{6,7},{7,6},{8,9},{9,8},{10,11... | collective-permute-start | bytes 1105928 | tf_op jit(solution)/shard_map/ppermute | solution.py:728
  217.1 6.1 %copy-start.39 = (bf16[192,256]{1,0:T(8,128)(2,1)S(1)}, bf16[192,256]{1,0:T(8,128)(2,1)}, u32[]{:S(2)}) copy-start(bf16[192,256]{1,0:T(8,128)(2,1)} %get-tuple-element.186) | copy-start | bytes 294916
  217.1 8.1 %copy-start.38 = (bf16[192,256]{1,0:T(8,128)(2,1)S(1)}, bf16[192,256]{1,0:T(8,128)(2,1)}, u32[]{:S(2)}) copy-start(bf16[192,256]{1,0:T(8,128)(2,1)} %get-tuple-element.187) | copy-start | bytes 294916
  219.6 8.6 %collective-permute-start.22 = (bf16[96,1152]{1,0:T(8,128)(2,1)}, bf16[96,1152]{1,0:T(8,128)(2,1)S(1)}, u32[]{:S(2)}, u32[]{:S(2)}) collective-permute-start(bf16[96,1152]{1,0:T(8,128)(2,1)} %get-tuple-element.192), channel_id=1, source_target_pairs={{0,2},{1,3},{2,0},{3,1},{4,6},{5,7},{6,4},{7,5},{8,10},{9,11},{10,... | collective-permute-start | bytes 663560 | tf_op jit(solution)/shard_map/ppermute | solution.py:728
  220.9 7.4 %collective-permute-start.23 = (bf16[96,1152]{1,0:T(8,128)(2,1)}, bf16[96,1152]{1,0:T(8,128)(2,1)S(1)}, u32[]{:S(2)}, u32[]{:S(2)}) collective-permute-start(bf16[96,1152]{1,0:T(8,128)(2,1)} %get-tuple-element.193), channel_id=1, source_target_pairs={{0,1},{1,0},{2,3},{3,2},{4,5},{5,4},{6,7},{7,6},{8,9},{9,8},{10,11... | collective-permute-start | bytes 663560 | tf_op jit(solution)/shard_map/ppermute | solution.py:728
  221.4 6.8 %collective-permute-start.21 = (bf16[192,256]{1,0:T(8,128)(2,1)S(1)}, bf16[192,256]{1,0:T(8,128)(2,1)S(1)}, u32[]{:S(2)}, u32[]{:S(2)}) collective-permute-start(bf16[192,256]{1,0:T(8,128)(2,1)S(1)} %copy-done.40), channel_id=1, source_target_pairs={{0,4},{1,5},{2,6},{3,7},{4,0},{5,1},{6,2},{7,3},{8,12},{9,13},{10,... | collective-permute-start | bytes 294920 | tf_op jit(solution)/shard_map/ppermute | solution.py:728
  223.2 8.7 %collective-permute-start.24 = (bf16[192,256]{1,0:T(8,128)(2,1)S(1)}, bf16[192,256]{1,0:T(8,128)(2,1)S(1)}, u32[]{:S(2)}, u32[]{:S(2)}) collective-permute-start(bf16[192,256]{1,0:T(8,128)(2,1)S(1)} %copy-done.39), channel_id=1, source_target_pairs={{0,8},{1,9},{2,10},{3,11},{4,12},{5,13},{6,14},{7,15},{8,0},{9,1},... | collective-permute-start | bytes 294920 | tf_op jit(solution)/shard_map/ppermute | solution.py:728
  225.2 6.7 %collective-permute-start.25 = (bf16[192,256]{1,0:T(8,128)(2,1)S(1)}, bf16[192,256]{1,0:T(8,128)(2,1)S(1)}, u32[]{:S(2)}, u32[]{:S(2)}) collective-permute-start(bf16[192,256]{1,0:T(8,128)(2,1)S(1)} %copy-done.38), channel_id=1, source_target_pairs={{0,12},{1,13},{2,14},{3,15},{4,8},{5,9},{6,10},{7,11},{8,4},{9,5},... | collective-permute-start | bytes 294920 | tf_op jit(solution)/shard_map/ppermute | solution.py:728
  228.3 9.2 %copy-start.15 = (bf16[96,1152]{1,0:T(8,128)(2,1)}, bf16[96,1152]{1,0:T(8,128)(2,1)S(1)}, u32[]{:S(2)}) copy-start(bf16[96,1152]{1,0:T(8,128)(2,1)S(1)} %collective-permute-done.22.refs_3_) | copy-start | bytes 663556
  228.3 9.1 %copy-start.16 = (bf16[96,1152]{1,0:T(8,128)(2,1)}, bf16[96,1152]{1,0:T(8,128)(2,1)S(1)}, u32[]{:S(2)}) copy-start(bf16[96,1152]{1,0:T(8,128)(2,1)S(1)} %collective-permute-done.23.refs_5_.refs_6_.refs_7_) | copy-start | bytes 663556
  236.4 4.1 %collective-permute-start.26 = (bf16[96,2176]{1,0:T(8,128)(2,1)}, bf16[96,2176]{1,0:T(8,128)(2,1)S(1)}, u32[]{:S(2)}, u32[]{:S(2)}) collective-permute-start(bf16[96,2176]{1,0:T(8,128)(2,1)} %get-tuple-element.198), channel_id=1, source_target_pairs={{0,16},{16,0},{1,17},{17,1},{2,18},{18,2},{3,19},{19,3},{4,20},{20... | collective-permute-start | bytes 1253384 | tf_op jit(solution)/shard_map/ppermute | solution.py:724
  236.4 11.7 %collective-permute-start.20 = (bf16[48,3840]{1,0:T(8,128)(2,1)}, bf16[48,3840]{1,0:T(8,128)(2,1)S(1)}, u32[]{:S(2)}, u32[]{:S(2)}) collective-permute-start(bf16[48,3840]{1,0:T(8,128)(2,1)} %cut.6), channel_id=1, source_target_pairs={{0,4},{1,5},{2,6},{3,7},{4,0},{5,1},{6,2},{7,3},{8,12},{9,13},{10,... | collective-permute-start | bytes 1105928 | tf_op jit(solution)/shard_map/ppermute | solution.py:728
  239.5 17.4 %collective-permute-start.30 = (bf16[48,2304]{1,0:T(8,128)(2,1)}, bf16[48,2304]{1,0:T(8,128)(2,1)}, u32[]{:S(2)}, u32[]{:S(2)}) collective-permute-start(bf16[48,2304]{1,0:T(8,128)(2,1)} %cut.8), channel_id=1, source_target_pairs={{0,4},{1,5},{2,6},{3,7},{4,0},{5,1},{6,2},{7,3},{8,12},{9,13},{10,... | collective-permute-start | bytes 663560 | tf_op jit(solution)/shard_map/ppermute | solution.py:728
  243.2 16.2 %collective-permute-start.27 = (bf16[24,2176]{1,0:T(8,128)(2,1)}, bf16[24,2176]{1,0:T(8,128)(2,1)}, u32[]{:S(2)}, u32[]{:S(2)}) collective-permute-start(bf16[24,2176]{1,0:T(8,128)(2,1)} %get-tuple-element.199), channel_id=1, source_target_pairs={{0,1},{1,0},{2,3},{3,2},{4,5},{5,4},{6,7},{7,6},{8,9},{9,8},{10,11... | collective-permute-start | bytes 313352 | tf_op jit(solution)/shard_map/ppermute | solution.py:728
  244.6 14.8 %collective-permute-start.28 = (bf16[24,2176]{1,0:T(8,128)(2,1)}, bf16[24,2176]{1,0:T(8,128)(2,1)}, u32[]{:S(2)}, u32[]{:S(2)}) collective-permute-start(bf16[24,2176]{1,0:T(8,128)(2,1)} %get-tuple-element.200), channel_id=1, source_target_pairs={{0,3},{1,2},{2,1},{3,0},{4,7},{5,6},{6,5},{7,4},{8,11},{9,10},{10,... | collective-permute-start | bytes 313352 | tf_op jit(solution)/shard_map/ppermute | solution.py:728
  245.6 7.5 %copy-start.5 = (bf16[2048,768]{1,0:T(8,128)(2,1)S(1)}, bf16[2048,768]{1,0:T(8,128)(2,1)}, u32[]{:S(2)}) copy-start(bf16[2048,768]{1,0:T(8,128)(2,1)} %w_ref.1) | copy-start | bytes 9437188
  245.6 13.8 %collective-permute-start.29 = (bf16[24,2176]{1,0:T(8,128)(2,1)}, bf16[24,2176]{1,0:T(8,128)(2,1)}, u32[]{:S(2)}, u32[]{:S(2)}) collective-permute-start(bf16[24,2176]{1,0:T(8,128)(2,1)} %get-tuple-element.201), channel_id=1, source_target_pairs={{0,2},{1,3},{2,0},{3,1},{4,6},{5,7},{6,4},{7,5},{8,10},{9,11},{10,... | collective-permute-start | bytes 313352 | tf_op jit(solution)/shard_map/ppermute | solution.py:728
  250.9 15.6 %collective-permute-start.32 = (bf16[24,3840]{1,0:T(8,128)(2,1)}, bf16[24,3840]{1,0:T(8,128)(2,1)S(1)}, u32[]{:S(2)}, u32[]{:S(2)}) collective-permute-start(bf16[24,3840]{1,0:T(8,128)(2,1)} %cut.7), channel_id=1, source_target_pairs={{0,8},{1,9},{2,10},{3,11},{4,12},{5,13},{6,14},{7,15},{8,0},{9,1},... | collective-permute-start | bytes 552968 | tf_op jit(solution)/shard_map/ppermute | solution.py:728
  258.7 7.8 %collective-permute-start.31 = (bf16[24,2304]{1,0:T(8,128)(2,1)}, bf16[24,2304]{1,0:T(8,128)(2,1)S(1)}, u32[]{:S(2)}, u32[]{:S(2)}) collective-permute-start(bf16[24,2304]{1,0:T(8,128)(2,1)} %cut.9), channel_id=1, source_target_pairs={{0,8},{1,9},{2,10},{3,11},{4,12},{5,13},{6,14},{7,15},{8,0},{9,1},... | collective-permute-start | bytes 331784 | tf_op jit(solution)/shard_map/ppermute | solution.py:728
  (31 other events, 62.8 us)

commit v3 on v2

--- a/solution.py
+++ b/solution.py
@@ -1053,12 +1053,12 @@
     arrived = exchange(outgoing)
     arrived_cot = exchange(cot_sent)
 
-    far_feats = swap_near([region_feats] + [after(region_feats, arrived)] * 3, peers)
 
     bias = jnp.concatenate([q_bias, jnp.zeros_like(q_bias), v_bias])[None]
     perm, region_perm = lax.optimization_barrier((share_order(peers), region_order(peers)))
     order = place_of(jnp.arange(peers, dtype=jnp.int32), peers) ^ lax.axis_index("dp")
     qkv_text = (dot_nn(text_in, w_qkv) + bias).astype(BF16)
+    far_feats = swap_near([region_feats] + [after(region_feats, qkv_text)] * 3, peers)
     qkv_region = (dot_nn(arrived[:, :D], w_qkv) + bias).astype(BF16)
     context, chance, chance_inv = attend(text_lengths, arrived, qkv_text, qkv_region)
     vecs = (out_bias, attn_gain, attn_shift, down_bias, ffn_gain, ffn_shift)

time: 272 us -> 295 us (1.085)
  waiting for transfers between devices: 20.5 us -> 42.6 us
    all_to_all x4, waiting for transfers between devices: 5.75 us -> 29.5 us  [exchange(): return lax.all_to_all(array, 'dp', split_axis=0, concat_axis=0, tiled=True)]
  transfers between devices with their start and end apart: 37 -> 37, of which waited for: 7 -> 7; matrix products, arithmetic and copies ran while one was open for 10% -> 10% of each run, Pallas kernels for 47% -> 44%
where the time goes in v3:
time: 295 us; the launch traced here: 293 us
  Pallas kernels  145 us (49%)
  starting transfers between devices  59.1 us (20%)
  waiting for transfers between devices  42.6 us (14%)
  matrix products  24.1 us (8%)
  local copies, waits for them, and re-layouts  17.6 us (6%)
  other arithmetic  3.78 us (1%)
    ppermute x28, starting transfers between devices, swap_chips(): lax.ppermute(sent, 'dp', [(peer, peer ^ mask) for peer in range(peers)])  33.9 us
    pallas_call x13, Pallas kernels, combine(): pl.pallas_call(functools.partial(combine_body, plans, len(operands)), gri...  32.5 us
    all_to_all x4, waiting for transfers between devices, exchange(): return lax.all_to_all(array, 'dp', split_axis=0, concat_axis=0, tiled=True)  29.5 us
    pallas_call x1, Pallas kernels, attend_back(): pl.pallas_call(attend_back_body, grid=(PAIRS,), in_specs=thirds(text_coun...  28.6 us
    pallas_call x1, Pallas kernels, feed_forward(): pl.pallas_call(feed_body, grid=(units // chunk,), in_specs=[whole((count,...  27.7 us
    all_to_all x4, starting transfers between devices, exchange(): return lax.all_to_all(array, 'dp', split_axis=0, concat_axis=0, tiled=True)  24.6 us
    pallas_call x1, Pallas kernels, feed_back(): pl.pallas_call(feed_back_body, grid=(units // chunk,), in_specs=[whole((c...  23.7 us
    pallas_call x1, Pallas kernels, attend(): pl.pallas_call(attend_body, grid_spec=pltpu.PrefetchScalarGridSpec(num_sc...  15.5 us
  transfers between devices with their start and end apart: 37, of which 7 were waited for; matrix products, arithmetic and copies ran while one was open for 10% of the time, Pallas kernels for 44%

profile of v3, /device:TPU:0, one launch (start us, length us, event | category | flops | bytes accessed | tf_op | source)
XLA Modules:
  0.0 293.3 jit_solution(8896683405039784497)
XLA Ops:
  0.7 4.4 %region_forward.1 = (bf16[256,896]{1,0:T(8,128)(2,1)}, bf16[256,768]{1,0:T(8,128)(2,1)}, bf16[256,128]{1,0:T(8,128)(2,1)}, f32[128,768]{1,0:T(8,128)}, f32[128,1]{1,0:T(8,128)}) custom-call(bf16[128,2048]{1,0:T(8,128)(2,1)} %refs_4_.1, bf16[2048,768]{1,0:T(8,128)(2,1)} %w_ref.1, f32[4,128]{1,0:T(4,128)} %boxes_ref.3, s32[1,128]{1,0:T(1,128)} %bitcast.33, ...), custom_call_target="tpu_custom_call" | custom-call | flops 402653184 | bytes 3670016 | tf_op jit(solution)/shard_map/region_forward/pallas_call | solution.py:121
  5.1 8.3 %all-to-all-start = ((bf16[16,16,896]{2,1,0:T(8,128)(2,1)}), bf16[16,16,896]{2,1,0:T(8,128)(2,1)S(1)}, u32[]{:S(2)}, u32[]{:S(2)}) async-start(bf16[16,16,896]{2,1,0:T(8,128)(2,1)} %bitcast.29), calls=%async_computation | async-start | bytes 917504 | tf_op jit(solution)/shard_map/all_to_all | solution.py:998
  13.5 5.5 %fusion.text_q_ref.text_k_ref.text_v_ref = bf16[512,2304]{1,0:T(8,128)(2,1)} fusion(bf16[512,768]{1,0:T(8,128)(2,1)S(1)} %copy-done.37, bf16[768,2304]{1,0:T(8,128)(2,1)} %w_v_ref.1, f32[2304]{0:T(1024)S(1)} %pad_maximum_fusion), kind=kOutput, calls=%fused_computation.1 | convolution fusion | flops 1814298624 | bytes 6693888 | tf_op jit(solution)/shard_map/dot_general | solution.py:29
  19.1 1.9 collective-permute-start
  21.0 2.4 collective-permute-start.1
  27.3 5.7 %all-to-all-start.1 = ((bf16[16,16,768]{2,1,0:T(8,128)(2,1)}), bf16[16,16,768]{2,1,0:T(8,128)(2,1)S(1)}, u32[]{:S(2)}, u32[]{:S(2)}) async-start(bf16[16,16,768]{2,1,0:T(8,128)(2,1)} %bitcast.5), calls=%async_computation.1 | async-start | bytes 786432 | tf_op jit(solution)/shard_map/all_to_all | solution.py:998
  32.9 4.1 %fusion.1.region_q_ref.region_k_ref.region_v_ref = bf16[256,2304]{1,0:T(8,128)(2,1)} fusion(bf16[768,2304]{1,0:T(8,128)(2,1)} %w_v_ref.1, f32[2304]{0:T(1024)S(1)} %pad_maximum_fusion, bf16[256,896]{1,0:T(8,128)(2,1)S(1)} %bitcast.26), kind=kOutput, calls=%fused_computation.3 | convolution fusion | flops 907149312 | bytes 5124096 | tf_op jit(solution)/shard_map/dot_general | solution.py:29
  37.1 15.5 %attend.1 = (bf16[768,768]{1,0:T(8,128)(2,1)}, bf16[12,768,768]{2,1,0:T(8,128)(2,1)}, f32[768,768]{1,0:T(8,128)}) custom-call(s32[1,5]{1,0:T(1,128)} %lengths_ref.1, bf16[256,896]{1,0:T(8,128)(2,1)} %bitcast.27, bf16[512,2304]{1,0:T(8,128)(2,1)} %fusion.text_q_ref.text_k_ref.text_v_ref, bf16[512,2304]{1,0:T(8,128)(2,1)} %fusion.text_q_ref.text_k_ref.text_v_ref, ...), custom_call_target="tpu_custom_call" | custom-call | flops 7247757312 | bytes 14155776 | tf_op jit(solution)/shard_map/attend/pallas_call | solution.py:213
  52.6 28.2 %all-to-all-done.1 = bf16[16,16,768]{2,1,0:T(8,128)(2,1)S(1)} async-done(((bf16[16,16,768]{2,1,0:T(8,128)(2,1)}), bf16[16,16,768]{2,1,0:T(8,128)(2,1)S(1)}, u32[]{:S(2)}, u32[]{:S(2)}) %all-to-all-start.1) | async-done | bytes 393248 | tf_op jit(solution)/shard_map/all_to_all | solution.py:998
  81.6 27.7 %feed_forward.1 = (bf16[768,3072]{1,0:T(8,128)(2,1)}, bf16[768,3072]{1,0:T(8,128)(2,1)}, f32[768,768]{1,0:T(8,128)}, f32[768,1]{1,0:T(8,128)}, bf16[768,768]{1,0...) custom-call(bf16[768,768]{1,0:T(8,128)(2,1)} %get-tuple-element.121., ...), custom_call_target="tpu_custom_call" | custom-call | flops 10871635968 | bytes 18874368 | tf_op jit(solution)/shard_map/feed_forward/pallas_call | solution.py:473
  110.4 5.6 %convolution_convert_fusion = bf16[1536,768]{1,0:T(8,128)(2,1)} fusion(bf16[768,768]{1,0:T(8,128)(2,1)} %get-tuple-element.134.d_down_ref, bf16[768,3072]{1,0:T(8,128)(2,1)} %get-tuple-element.131, s32[]{:T(128)S(6)} %select_n.140), kind=kOutput, calls=%fused_computation.4 | convolution fusion | flops 1813118976 | bytes 5898244 | tf_op jit(solution)/shard_map/dot_general | solution.py:37
  116.5 5.1 %convolution_convert_fusion.1.refs_0_.refs_2_.refs_4_.refs_6_ = bf16[1536,768]{1,0:T(8,128)(2,1)} fusion(bf16[768,768]{1,0:T(8,128)(2,1)S(1)} %copy-done.41, bf16[768,3072]{1,0:T(8,128)(2,1)} %get-tuple-element.131, s32[]{:T(128)S(6)} %select_n.139), kind=kOutput, calls=%fused_computation.5 | convolution fusion | flops 1813118976 | bytes 5898244 | tf_op jit(solution)/shard_map/dot_general | solution.py:37
  121.7 1.4 copy-done.2
  123.1 5.6 %cut_units.1 = (bf16[768,384]{1,0:T(8,128)(2,1)}, bf16[768,384]{1,0:T(8,128)(2,1)}, bf16[1536,768]{1,0:T(8,128)(2,1)}) custom-call(s32[16]{0:T(128)} %fusion.41.order_ref, bf16[1536,768]{1,0:T(8,128)(2,1)} %convolution_convert_fusion.1.refs_0_.refs_2_.refs_4_.refs_6_, bf16[1536,768]{1,0:T(8,128)(2,1)} %copy-done.2, ...), custom_call_target="tpu_custom_call" | custom-call | flops 1179648 | bytes 9437184 | tf_op jit(solution)/shard_map/cut_units/pallas_call | solution.py:933
  130.1 23.7 %feed_back.1 = (bf16[384,3072]{1,0:T(8,128)(2,1)}, bf16[384,3072]{1,0:T(8,128)(2,1)}, bf16[384,768]{1,0:T(8,128)(2,1)}, bf16[384,768]{1,0:T(8,128)(2,1)}, f32[1,...) custom-call(bf16[768,768]{1,0:T(8,128)(2,1)} %get-tuple-element.134.d_down_ref, ...), custom_call_target="tpu_custom_call" | custom-call | flops 12683575296 | bytes 18874368 | tf_op jit(solution)/shard_map/feed_back/pallas_call | solution.py:604
  154.8 2.5 pair_turn.3
  158.5 1.4 collective-permute-start.9
  160.0 1.4 copy-done
  161.4 4.0 %pair_start.2 = (bf16[192,1920]{1,0:T(8,128)(2,1)}, bf16[192,1920]{1,0:T(8,128)(2,1)}) custom-call(bf16[384,3072]{1,0:T(8,128)(2,1)} %get-tuple-element.142.refs_0_.refs_2_.refs_4_.refs_3_.refs_8_, bf16[384,3072]{1,0:T(8,128)(2,1)} %copy-done, bf16[384,3072]{1,0:T(8,128)(2,1)} %get-tuple-element.142.refs_0_.refs_2_.refs_4_.refs_3_.refs_8_, ...), custom_call_target="tpu_custom_call" | custom-call | tf_op jit(solution)/shard_map/pair_start/pallas_call | solution.py:795
  168.4 2.3 cut.5
  171.2 1.7 collective-permute-start.13
  173.0 2.2 collective-permute-start.14
  175.2 3.8 %all-to-all-start.2 = ((bf16[16,16,768]{2,1,0:T(8,128)(2,1)}), bf16[16,16,768]{2,1,0:T(8,128)(2,1)S(1)}, u32[]{:S(2)}, u32[]{:S(2)}) async-start(bf16[16,16,768]{2,1,0:T(8,128)(2,1)} %bitcast.7), calls=%async_computation.2 | async-start | bytes 786432 | tf_op jit(solution)/shard_map/all_to_all | solution.py:998
  179.0 28.6 %attend_back.1 = (bf16[384,2304]{1,0:T(8,128)(2,1)}, bf16[384,2304]{1,0:T(8,128)(2,1)}, f32[1,2304]{1,0:T(1,128)}, bf16[512,768]{1,0:T(8,128)(2,1)}, bf16[256,768]{1,0:T(8,128)(2,1)}) custom-call(bf16[512,2304]{1,0:T(8,128)(2,1)} %fusion.text_q_ref.text_k_ref.text_v_ref, bf16[512,2304]{1,0:T(8,128)(2,1)} %fusion.text_q_ref.text_k_ref.text_v_ref, ...), custom_call_target="tpu_custom_call" | custom-call | flops 19931332608 | bytes 14155776 | tf_op jit(solution)/shard_map/attend_back/pallas_call | solution.py:321
  208.5 6.8 %all-to-all-start.3 = ((bf16[16,16,768]{2,1,0:T(8,128)(2,1)}), bf16[16,16,768]{2,1,0:T(8,128)(2,1)}, u32[]{:S(2)}, u32[]{:S(2)}) async-start(bf16[16,16,768]{2,1,0:T(8,128)(2,1)} %bitcast.30), calls=%async_computation.3 | async-start | bytes 786432 | tf_op jit(solution)/shard_map/all_to_all | solution.py:998
  216.5 3.2 %pair_start.3 = (bf16[192,1152]{1,0:T(8,128)(2,1)}, bf16[192,1152]{1,0:T(8,128)(2,1)}) custom-call(bf16[384,2304]{1,0:T(8,128)(2,1)} %get-tuple-element.167.refs_0_.refs_2_.refs_4_.refs_3_, bf16[384,2304]{1,0:T(8,128)(2,1)} %copy-done.1, bf16[384,2304]{1,0:T(8,128)(2,1)} %get-tuple-element.167.refs_0_.refs_2_.refs_4_.refs_3_, bf16[384,2304]{1,0:T(8,128)(2,1)} %copy-done.1, ...), custom_call_target="tpu_custom_call" | custom-call | tf_op jit(solution)/shard_map/pair_start/pallas_call | solution.py:795
  219.7 1.9 collective-permute-start.16
  221.6 1.5 collective-permute-start.17
  223.1 3.0 %pair_turn.4 = (bf16[96,1920]{1,0:T(8,128)(2,1)}, bf16[96,1920]{1,0:T(8,128)(2,1)}) custom-call(bf16[384,3072]{1,0:T(8,128)(2,1)} %get-tuple-element.142.refs_0_.refs_2_.refs_4_.refs_3_.refs_8_, bf16[384,3072]{1,0:T(8,128)(2,1)} %copy-done, bf16[192,1920]{1,0:T(8,128)(2,1)} %copy-done.6, ...), custom_call_target="tpu_custom_call" | custom-call | tf_op jit(solution)/shard_map/pair_turn/pallas_call | solution.py:795
  228.8 6.1 %collective-permute-done.16.refs_2_ = bf16[192,1152]{1,0:T(8,128)(2,1)S(1)} collective-permute-done((bf16[192,1152]{1,0:T(8,128)(2,1)}, bf16[192,1152]{1,0:T(8,128)(2,1)S(1)}, u32[]{:S(2)}, u32[]{:S(2)}) %collective-permute-start.16) | collective-permute-done | bytes 442400 | tf_op jit(solution)/shard_map/ppermute | solution.py:728
  235.8 3.5 %region_back.1 = (bf16[128,768]{1,0:T(8,128)(2,1)}, bf16[192,256]{1,0:T(8,128)(2,1)}, bf16[192,256]{1,0:T(8,128)(2,1)}, bf16[192,256]{1,0:T(8,128)(2,1)}, bf16[192,256]{1,0:T(8,128)(2,1)}) custom-call(bf16[256,768]{1,0:T(8,128)(2,1)} %bitcast.10.back_ref, bf16[256,128]{1,0:T(8,128)(2,1)} %get-tuple-element.125.hot_ref, ...), custom_call_target="tpu_custom_call" | custom-call | tf_op jit(solution)/shard_map/region_back/pallas_call | solution.py:691
  239.4 2.5 pair_turn.5
  243.7 1.7 collective-permute-start.21
  245.4 2.0 collective-permute-start.24
  248.2 2.3 cut.6
  250.6 3.6 %collective-permute-done.24.refs_2_ = bf16[192,256]{1,0:T(8,128)(2,1)S(1)} collective-permute-done((bf16[192,256]{1,0:T(8,128)(2,1)S(1)}, bf16[192,256]{1,0:T(8,128)(2,1)S(1)}, u32[]{:S(2)}, u32[]{:S(2)}) %collective-permute-start.24) | collective-permute-done | bytes 98336 | tf_op jit(solution)/shard_map/ppermute | solution.py:728
  255.5 3.2 %region_product.1 = (bf16[96,2176]{1,0:T(8,128)(2,1)}, bf16[96,2176]{1,0:T(8,128)(2,1)}) custom-call(bf16[192,256]{1,0:T(8,128)(2,1)} %get-tuple-element.184.refs_0_, bf16[192,256]{1,0:T(8,128)(2,1)} %copy-done.31, bf16[192,256]{1,0:T(8,128)(2,1)} %copy-done.32, bf16[192,256]{1,0:T(8,128)(2,1)} %copy-done.33, bf16[128,2048]{1,0:T(8,128)(2,1)} %refs_4_.1, ...), custom_call_target="tpu_custom_call" | custom-call | tf_op jit(solution)/shard_map/region_product/pallas_call | solution.py:966
  259.7 2.0 cut.8
  263.6 1.9 direct.1
  265.5 1.4 collective-permute-start.27
  269.0 1.4 collective-permute-done.20.refs_4_.refs_12_
  271.1 2.0 cut.7
  273.2 2.2 collective-permute-start.32
  275.4 2.9 convolution_convert_fusion.2
  279.1 1.8 cut.9
  281.7 1.8 last_shares.1
  285.7 2.0 slice_reduce_fusion
  290.1 3.0 %shares.1 = (f32[24,2304]{1,0:T(8,128)}, f32[24,3072]{1,0:T(8,128)}, f32[24,768]{1,0:T(8,128)}, f32[96,768]{1,0:T(8,128)}) custom-call(bf16[384,2304]{1,0:T(8,128)(2,1)} %get-tuple-element.167.refs_0_.refs_2_.refs_4_.refs_3_, bf16[384,2304]{1,0:T(8,128)(2,1)} %copy-done.1, bf16[192,1152]{1,0:T(8,128)(2,1)} %copy-done.8, bf16[96,1152]{1,0:T(8,128)(2,1)} %copy-done.15, ...), custom_call_target="tpu_custom_call" | custom-call | tf_op jit(solution)/shard_map/shares/pallas_call | solution.py:795
  (153 shorter events, 34.9 us)
Async XLA Ops:
  0.7 12.8 %copy-start.35 = (f32[768]{0:T(1024)S(1)}, f32[768]{0:T(1024)}, u32[]{:S(2)}) copy-start(f32[768]{0:T(1024)} %param.39) | copy-start | bytes 9220
  0.7 12.8 %copy-start.36 = (f32[768]{0:T(1024)S(1)}, f32[768]{0:T(1024)}, u32[]{:S(2)}) copy-start(f32[768]{0:T(1024)} %param.38) | copy-start | bytes 9220
  0.7 12.8 %copy-start.37 = (bf16[512,768]{1,0:T(8,128)(2,1)S(1)}, bf16[512,768]{1,0:T(8,128)(2,1)}, u32[]{:S(2)}) copy-start(bf16[512,768]{1,0:T(8,128)(2,1)} %text_ref.1) | copy-start | bytes 2359300
  5.1 22.2 %all-to-all-start = ((bf16[16,16,896]{2,1,0:T(8,128)(2,1)}), bf16[16,16,896]{2,1,0:T(8,128)(2,1)S(1)}, u32[]{:S(2)}, u32[]{:S(2)}) async-start(bf16[16,16,896]{2,1,0:T(8,128)(2,1)} %bitcast.29), calls=%async_computation | async-start | bytes 917504 | tf_op jit(solution)/shard_map/all_to_all | solution.py:998
  19.1 90.2 %collective-permute-start = (bf16[128,2048]{1,0:T(8,128)(2,1)S(1)}, bf16[128,2048]{1,0:T(8,128)(2,1)S(1)}, u32[]{:S(2)}, u32[]{:S(2)}) collective-permute-start(bf16[128,2048]{1,0:T(8,128)(2,1)S(1)} %copy-done.14), channel_id=1, source_target_pairs={{0,4},{1,5},{2,6},{3,7},{4,0},{5,1},{6,2},{7,3},{8,12},{9,13},{10,... | collective-permute-start | bytes 1572872 | tf_op jit(solution)/shard_map/ppermute | solution.py:728
  21.0 88.3 %collective-permute-start.1 = (bf16[128,2048]{1,0:T(8,128)(2,1)S(1)}, bf16[128,2048]{1,0:T(8,128)(2,1)S(1)}, u32[]{:S(2)}, u32[]{:S(2)}) collective-permute-start(bf16[128,2048]{1,0:T(8,128)(2,1)S(1)} %copy-done.14), channel_id=1, source_target_pairs={{0,8},{1,9},{2,10},{3,11},{4,12},{5,13},{6,14},{7,15},{8,0},{9,1},... | collective-permute-start | bytes 1572872 | tf_op jit(solution)/shard_map/ppermute | solution.py:728
  23.3 86.0 %collective-permute-start.2 = (bf16[128,2048]{1,0:T(8,128)(2,1)S(1)}, bf16[128,2048]{1,0:T(8,128)(2,1)S(1)}, u32[]{:S(2)}, u32[]{:S(2)}) collective-permute-start(bf16[128,2048]{1,0:T(8,128)(2,1)S(1)} %copy-done.14), channel_id=1, source_target_pairs={{0,12},{1,13},{2,14},{3,15},{4,8},{5,9},{6,10},{7,11},{8,4},{9,5},... | collective-permute-start | bytes 1572872 | tf_op jit(solution)/shard_map/ppermute | solution.py:728
  27.3 9.8 %copy-start.23 = (bf16[16,16,896]{2,1,0:T(8,128)(2,1)}, bf16[16,16,896]{2,1,0:T(8,128)(2,1)S(1)}, u32[]{:S(2)}) copy-start(bf16[16,16,896]{2,1,0:T(8,128)(2,1)S(1)} %all-to-all-done) | copy-start | bytes 1376260
  27.3 53.6 %all-to-all-start.1 = ((bf16[16,16,768]{2,1,0:T(8,128)(2,1)}), bf16[16,16,768]{2,1,0:T(8,128)(2,1)S(1)}, u32[]{:S(2)}, u32[]{:S(2)}) async-start(bf16[16,16,768]{2,1,0:T(8,128)(2,1)} %bitcast.5), calls=%async_computation.1 | async-start | bytes 786432 | tf_op jit(solution)/shard_map/all_to_all | solution.py:998
  116.0 5.7 %collective-permute-start.3 = (bf16[1536,768]{1,0:T(8,128)(2,1)}, bf16[1536,768]{1,0:T(8,128)(2,1)S(1)}, u32[]{:S(2)}, u32[]{:S(2)}) collective-permute-start(bf16[1536,768]{1,0:T(8,128)(2,1)} %convolution_convert_fusion), channel_id=1, source_target_pairs={{0,16},{16,0},{1,17},{17,1},{2,18},{18,2},{3,19},{19,3},{4,20},{20... | collective-permute-start | bytes 7077896 | tf_op jit(solution)/shard_map/ppermute | solution.py:724
  128.7 25.1 %collective-permute-start.4 = (bf16[768,384]{1,0:T(8,128)(2,1)}, bf16[768,384]{1,0:T(8,128)(2,1)S(1)}, u32[]{:S(2)}, u32[]{:S(2)}) collective-permute-start(bf16[768,384]{1,0:T(8,128)(2,1)} %get-tuple-element.132), channel_id=1, source_target_pairs={{0,1},{1,0},{2,3},{3,2},{4,5},{5,4},{6,7},{7,6},{8,9},{9,8},{10,11... | collective-permute-start | bytes 1769480 | tf_op jit(solution)/shard_map/ppermute | solution.py:728
  129.3 24.6 %collective-permute-start.5 = (bf16[768,384]{1,0:T(8,128)(2,1)}, bf16[768,384]{1,0:T(8,128)(2,1)S(1)}, u32[]{:S(2)}, u32[]{:S(2)}) collective-permute-start(bf16[768,384]{1,0:T(8,128)(2,1)} %get-tuple-element.133), channel_id=1, source_target_pairs={{0,2},{1,3},{2,0},{3,1},{4,6},{5,7},{6,4},{7,5},{8,10},{9,11},{10,... | collective-permute-start | bytes 1769480 | tf_op jit(solution)/shard_map/ppermute | solution.py:728
  153.8 6.2 %collective-permute-start.6 = (bf16[384,3072]{1,0:T(8,128)(2,1)}, bf16[384,3072]{1,0:T(8,128)(2,1)S(1)}, u32[]{:S(2)}, u32[]{:S(2)}) collective-permute-start(bf16[384,3072]{1,0:T(8,128)(2,1)} %get-tuple-element.145), channel_id=1, source_target_pairs={{0,16},{16,0},{1,17},{17,1},{2,18},{18,2},{3,19},{19,3},{4,20},{20... | collective-permute-start | bytes 7077896 | tf_op jit(solution)/shard_map/ppermute | solution.py:724
  153.9 6.1 %collective-permute-start.7 = (bf16[384,768]{1,0:T(8,128)(2,1)}, bf16[384,768]{1,0:T(8,128)(2,1)}, u32[]{:S(2)}, u32[]{:S(2)}) collective-permute-start(bf16[384,768]{1,0:T(8,128)(2,1)} %get-tuple-element.147), channel_id=1, source_target_pairs={{0,16},{16,0},{1,17},{17,1},{2,18},{18,2},{3,19},{19,3},{4,20},{20... | collective-permute-start | bytes 1769480 | tf_op jit(solution)/shard_map/ppermute | solution.py:724
  157.3 10.4 %collective-permute-start.8 = (bf16[384,384]{1,0:T(8,128)(2,1)}, bf16[384,384]{1,0:T(8,128)(2,1)S(1)}, u32[]{:S(2)}, u32[]{:S(2)}) collective-permute-start(bf16[384,384]{1,0:T(8,128)(2,1)} %get-tuple-element.151), channel_id=1, source_target_pairs={{0,2},{1,3},{2,0},{3,1},{4,6},{5,7},{6,4},{7,5},{8,10},{9,11},{10,... | collective-permute-start | bytes 884744 | tf_op jit(solution)/shard_map/ppermute | solution.py:728
  158.5 9.2 %collective-permute-start.9 = (bf16[384,384]{1,0:T(8,128)(2,1)}, bf16[384,384]{1,0:T(8,128)(2,1)}, u32[]{:S(2)}, u32[]{:S(2)}) collective-permute-start(bf16[384,384]{1,0:T(8,128)(2,1)} %get-tuple-element.153), channel_id=1, source_target_pairs={{0,1},{1,0},{2,3},{3,2},{4,5},{5,4},{6,7},{7,6},{8,9},{9,8},{10,11... | collective-permute-start | bytes 884744 | tf_op jit(solution)/shard_map/ppermute | solution.py:728
  165.4 42.3 %collective-permute-start.10 = (bf16[192,1920]{1,0:T(8,128)(2,1)}, bf16[192,1920]{1,0:T(8,128)(2,1)S(1)}, u32[]{:S(2)}, u32[]{:S(2)}) collective-permute-start(bf16[192,1920]{1,0:T(8,128)(2,1)} %get-tuple-element.148), channel_id=1, source_target_pairs={{0,1},{1,0},{2,3},{3,2},{4,5},{5,4},{6,7},{7,6},{8,9},{9,8},{10,11... | collective-permute-start | bytes 2211848 | tf_op jit(solution)/shard_map/ppermute | solution.py:728
  166.5 41.2 %collective-permute-start.11 = (bf16[192,1920]{1,0:T(8,128)(2,1)}, bf16[192,1920]{1,0:T(8,128)(2,1)S(1)}, u32[]{:S(2)}, u32[]{:S(2)}) collective-permute-start(bf16[192,1920]{1,0:T(8,128)(2,1)} %get-tuple-element.149), channel_id=1, source_target_pairs={{0,2},{1,3},{2,0},{3,1},{4,6},{5,7},{6,4},{7,5},{8,10},{9,11},{10,... | collective-permute-start | bytes 2211848 | tf_op jit(solution)/shard_map/ppermute | solution.py:728
  170.8 36.8 %collective-permute-start.12 = (bf16[96,768]{1,0:T(8,128)(2,1)}, bf16[96,768]{1,0:T(8,128)(2,1)S(1)}, u32[]{:S(2)}, u32[]{:S(2)}) collective-permute-start(bf16[96,768]{1,0:T(8,128)(2,1)} %get-tuple-element.155), channel_id=1, source_target_pairs={{0,8},{1,9},{2,10},{3,11},{4,12},{5,13},{6,14},{7,15},{8,0},{9,1},... | collective-permute-start | bytes 442376 | tf_op jit(solution)/shard_map/ppermute | solution.py:728
  171.2 36.4 %collective-permute-start.13 = (bf16[96,768]{1,0:T(8,128)(2,1)}, bf16[96,768]{1,0:T(8,128)(2,1)S(1)}, u32[]{:S(2)}, u32[]{:S(2)}) collective-permute-start(bf16[96,768]{1,0:T(8,128)(2,1)} %get-tuple-element.156), channel_id=1, source_target_pairs={{0,4},{1,5},{2,6},{3,7},{4,0},{5,1},{6,2},{7,3},{8,12},{9,13},{10,... | collective-permute-start | bytes 442376 | tf_op jit(solution)/shard_map/ppermute | solution.py:728
  173.0 34.7 %collective-permute-start.14 = (bf16[96,768]{1,0:T(8,128)(2,1)}, bf16[96,768]{1,0:T(8,128)(2,1)S(1)}, u32[]{:S(2)}, u32[]{:S(2)}) collective-permute-start(bf16[96,768]{1,0:T(8,128)(2,1)} %get-tuple-element.157), channel_id=1, source_target_pairs={{0,12},{1,13},{2,14},{3,15},{4,8},{5,9},{6,10},{7,11},{8,4},{9,5},... | collective-permute-start | bytes 442376 | tf_op jit(solution)/shard_map/ppermute | solution.py:728
  175.2 32.5 %all-to-all-start.2 = ((bf16[16,16,768]{2,1,0:T(8,128)(2,1)}), bf16[16,16,768]{2,1,0:T(8,128)(2,1)S(1)}, u32[]{:S(2)}, u32[]{:S(2)}) async-start(bf16[16,16,768]{2,1,0:T(8,128)(2,1)} %bitcast.7), calls=%async_computation.2 | async-start | bytes 786432 | tf_op jit(solution)/shard_map/all_to_all | solution.py:998
  207.7 12.0 %copy-start.6 = (bf16[192,1920]{1,0:T(8,128)(2,1)}, bf16[192,1920]{1,0:T(8,128)(2,1)S(1)}, u32[]{:S(2)}) copy-start(bf16[192,1920]{1,0:T(8,128)(2,1)S(1)} %collective-permute-done.10.refs_2_.refs_10_) | copy-start | bytes 2211844
  207.7 15.3 %copy-start.7 = (bf16[192,1920]{1,0:T(8,128)(2,1)}, bf16[192,1920]{1,0:T(8,128)(2,1)S(1)}, u32[]{:S(2)}) copy-start(bf16[192,1920]{1,0:T(8,128)(2,1)S(1)} %collective-permute-done.11.refs_5_.refs_4_.refs_14_) | copy-start | bytes 2211844
  208.5 6.8 %collective-permute-start.15 = (bf16[384,2304]{1,0:T(8,128)(2,1)}, bf16[384,2304]{1,0:T(8,128)(2,1)S(1)}, u32[]{:S(2)}, u32[]{:S(2)}) collective-permute-start(bf16[384,2304]{1,0:T(8,128)(2,1)} %get-tuple-element.165), channel_id=1, source_target_pairs={{0,16},{16,0},{1,17},{17,1},{2,18},{18,2},{3,19},{19,3},{4,20},{20... | collective-permute-start | bytes 5308424 | tf_op jit(solution)/shard_map/ppermute | solution.py:724
  208.5 20.3 %all-to-all-start.3 = ((bf16[16,16,768]{2,1,0:T(8,128)(2,1)}), bf16[16,16,768]{2,1,0:T(8,128)(2,1)}, u32[]{:S(2)}, u32[]{:S(2)}) async-start(bf16[16,16,768]{2,1,0:T(8,128)(2,1)} %bitcast.30), calls=%async_computation.3 | async-start | bytes 786432 | tf_op jit(solution)/shard_map/all_to_all | solution.py:998
  219.7 15.2 %collective-permute-start.16 = (bf16[192,1152]{1,0:T(8,128)(2,1)}, bf16[192,1152]{1,0:T(8,128)(2,1)S(1)}, u32[]{:S(2)}, u32[]{:S(2)}) collective-permute-start(bf16[192,1152]{1,0:T(8,128)(2,1)} %get-tuple-element.168), channel_id=1, source_target_pairs={{0,1},{1,0},{2,3},{3,2},{4,5},{5,4},{6,7},{7,6},{8,9},{9,8},{10,11... | collective-permute-start | bytes 1327112 | tf_op jit(solution)/shard_map/ppermute | solution.py:728
  221.6 14.2 %collective-permute-start.17 = (bf16[192,1152]{1,0:T(8,128)(2,1)}, bf16[192,1152]{1,0:T(8,128)(2,1)S(1)}, u32[]{:S(2)}, u32[]{:S(2)}) collective-permute-start(bf16[192,1152]{1,0:T(8,128)(2,1)} %get-tuple-element.169), channel_id=1, source_target_pairs={{0,2},{1,3},{2,0},{3,1},{4,6},{5,7},{6,4},{7,5},{8,10},{9,11},{10,... | collective-permute-start | bytes 1327112 | tf_op jit(solution)/shard_map/ppermute | solution.py:728
  226.1 19.4 %collective-permute-start.18 = (bf16[96,1920]{1,0:T(8,128)(2,1)}, bf16[96,1920]{1,0:T(8,128)(2,1)S(1)}, u32[]{:S(2)}, u32[]{:S(2)}) collective-permute-start(bf16[96,1920]{1,0:T(8,128)(2,1)} %get-tuple-element.179), channel_id=1, source_target_pairs={{0,2},{1,3},{2,0},{3,1},{4,6},{5,7},{6,4},{7,5},{8,10},{9,11},{10,... | collective-permute-start | bytes 1105928 | tf_op jit(solution)/shard_map/ppermute | solution.py:728
  226.6 20.8 %collective-permute-start.19 = (bf16[96,1920]{1,0:T(8,128)(2,1)}, bf16[96,1920]{1,0:T(8,128)(2,1)S(1)}, u32[]{:S(2)}, u32[]{:S(2)}) collective-permute-start(bf16[96,1920]{1,0:T(8,128)(2,1)} %get-tuple-element.180), channel_id=1, source_target_pairs={{0,1},{1,0},{2,3},{3,2},{4,5},{5,4},{6,7},{7,6},{8,9},{9,8},{10,11... | collective-permute-start | bytes 1105928 | tf_op jit(solution)/shard_map/ppermute | solution.py:728
  239.4 6.1 %copy-start.39 = (bf16[192,256]{1,0:T(8,128)(2,1)S(1)}, bf16[192,256]{1,0:T(8,128)(2,1)}, u32[]{:S(2)}) copy-start(bf16[192,256]{1,0:T(8,128)(2,1)} %get-tuple-element.186) | copy-start | bytes 294916
  239.4 8.1 %copy-start.38 = (bf16[192,256]{1,0:T(8,128)(2,1)S(1)}, bf16[192,256]{1,0:T(8,128)(2,1)}, u32[]{:S(2)}) copy-start(bf16[192,256]{1,0:T(8,128)(2,1)} %get-tuple-element.187) | copy-start | bytes 294916
  241.9 8.6 %collective-permute-start.22 = (bf16[96,1152]{1,0:T(8,128)(2,1)}, bf16[96,1152]{1,0:T(8,128)(2,1)S(1)}, u32[]{:S(2)}, u32[]{:S(2)}) collective-permute-start(bf16[96,1152]{1,0:T(8,128)(2,1)} %get-tuple-element.192), channel_id=1, source_target_pairs={{0,2},{1,3},{2,0},{3,1},{4,6},{5,7},{6,4},{7,5},{8,10},{9,11},{10,... | collective-permute-start | bytes 663560 | tf_op jit(solution)/shard_map/ppermute | solution.py:728
  243.1 7.4 %collective-permute-start.23 = (bf16[96,1152]{1,0:T(8,128)(2,1)}, bf16[96,1152]{1,0:T(8,128)(2,1)S(1)}, u32[]{:S(2)}, u32[]{:S(2)}) collective-permute-start(bf16[96,1152]{1,0:T(8,128)(2,1)} %get-tuple-element.193), channel_id=1, source_target_pairs={{0,1},{1,0},{2,3},{3,2},{4,5},{5,4},{6,7},{7,6},{8,9},{9,8},{10,11... | collective-permute-start | bytes 663560 | tf_op jit(solution)/shard_map/ppermute | solution.py:728
  243.7 6.8 %collective-permute-start.21 = (bf16[192,256]{1,0:T(8,128)(2,1)S(1)}, bf16[192,256]{1,0:T(8,128)(2,1)S(1)}, u32[]{:S(2)}, u32[]{:S(2)}) collective-permute-start(bf16[192,256]{1,0:T(8,128)(2,1)S(1)} %copy-done.40), channel_id=1, source_target_pairs={{0,4},{1,5},{2,6},{3,7},{4,0},{5,1},{6,2},{7,3},{8,12},{9,13},{10,... | collective-permute-start | bytes 294920 | tf_op jit(solution)/shard_map/ppermute | solution.py:728
  245.4 8.7 %collective-permute-start.24 = (bf16[192,256]{1,0:T(8,128)(2,1)S(1)}, bf16[192,256]{1,0:T(8,128)(2,1)S(1)}, u32[]{:S(2)}, u32[]{:S(2)}) collective-permute-start(bf16[192,256]{1,0:T(8,128)(2,1)S(1)} %copy-done.39), channel_id=1, source_target_pairs={{0,8},{1,9},{2,10},{3,11},{4,12},{5,13},{6,14},{7,15},{8,0},{9,1},... | collective-permute-start | bytes 294920 | tf_op jit(solution)/shard_map/ppermute | solution.py:728
  247.5 6.7 %collective-permute-start.25 = (bf16[192,256]{1,0:T(8,128)(2,1)S(1)}, bf16[192,256]{1,0:T(8,128)(2,1)S(1)}, u32[]{:S(2)}, u32[]{:S(2)}) collective-permute-start(bf16[192,256]{1,0:T(8,128)(2,1)S(1)} %copy-done.38), channel_id=1, source_target_pairs={{0,12},{1,13},{2,14},{3,15},{4,8},{5,9},{6,10},{7,11},{8,4},{9,5},... | collective-permute-start | bytes 294920 | tf_op jit(solution)/shard_map/ppermute | solution.py:728
  250.5 9.2 %copy-start.15 = (bf16[96,1152]{1,0:T(8,128)(2,1)}, bf16[96,1152]{1,0:T(8,128)(2,1)S(1)}, u32[]{:S(2)}) copy-start(bf16[96,1152]{1,0:T(8,128)(2,1)S(1)} %collective-permute-done.22.refs_3_) | copy-start | bytes 663556
  250.6 9.1 %copy-start.16 = (bf16[96,1152]{1,0:T(8,128)(2,1)}, bf16[96,1152]{1,0:T(8,128)(2,1)S(1)}, u32[]{:S(2)}) copy-start(bf16[96,1152]{1,0:T(8,128)(2,1)S(1)} %collective-permute-done.23.refs_5_.refs_6_.refs_7_) | copy-start | bytes 663556
  258.7 4.1 %collective-permute-start.26 = (bf16[96,2176]{1,0:T(8,128)(2,1)}, bf16[96,2176]{1,0:T(8,128)(2,1)S(1)}, u32[]{:S(2)}, u32[]{:S(2)}) collective-permute-start(bf16[96,2176]{1,0:T(8,128)(2,1)} %get-tuple-element.198), channel_id=1, source_target_pairs={{0,16},{16,0},{1,17},{17,1},{2,18},{18,2},{3,19},{19,3},{4,20},{20... | collective-permute-start | bytes 1253384 | tf_op jit(solution)/shard_map/ppermute | solution.py:724
  258.7 11.7 %collective-permute-start.20 = (bf16[48,3840]{1,0:T(8,128)(2,1)}, bf16[48,3840]{1,0:T(8,128)(2,1)S(1)}, u32[]{:S(2)}, u32[]{:S(2)}) collective-permute-start(bf16[48,3840]{1,0:T(8,128)(2,1)} %cut.6), channel_id=1, source_target_pairs={{0,4},{1,5},{2,6},{3,7},{4,0},{5,1},{6,2},{7,3},{8,12},{9,13},{10,... | collective-permute-start | bytes 1105928 | tf_op jit(solution)/shard_map/ppermute | solution.py:728
  261.7 17.4 %collective-permute-start.30 = (bf16[48,2304]{1,0:T(8,128)(2,1)}, bf16[48,2304]{1,0:T(8,128)(2,1)}, u32[]{:S(2)}, u32[]{:S(2)}) collective-permute-start(bf16[48,2304]{1,0:T(8,128)(2,1)} %cut.8), channel_id=1, source_target_pairs={{0,4},{1,5},{2,6},{3,7},{4,0},{5,1},{6,2},{7,3},{8,12},{9,13},{10,... | collective-permute-start | bytes 663560 | tf_op jit(solution)/shard_map/ppermute | solution.py:728
  265.5 16.2 %collective-permute-start.27 = (bf16[24,2176]{1,0:T(8,128)(2,1)}, bf16[24,2176]{1,0:T(8,128)(2,1)}, u32[]{:S(2)}, u32[]{:S(2)}) collective-permute-start(bf16[24,2176]{1,0:T(8,128)(2,1)} %get-tuple-element.199), channel_id=1, source_target_pairs={{0,1},{1,0},{2,3},{3,2},{4,5},{5,4},{6,7},{7,6},{8,9},{9,8},{10,11... | collective-permute-start | bytes 313352 | tf_op jit(solution)/shard_map/ppermute | solution.py:728
  266.9 14.8 %collective-permute-start.28 = (bf16[24,2176]{1,0:T(8,128)(2,1)}, bf16[24,2176]{1,0:T(8,128)(2,1)}, u32[]{:S(2)}, u32[]{:S(2)}) collective-permute-start(bf16[24,2176]{1,0:T(8,128)(2,1)} %get-tuple-element.200), channel_id=1, source_target_pairs={{0,3},{1,2},{2,1},{3,0},{4,7},{5,6},{6,5},{7,4},{8,11},{9,10},{10,... | collective-permute-start | bytes 313352 | tf_op jit(solution)/shard_map/ppermute | solution.py:728
  267.9 7.5 %copy-start.5 = (bf16[2048,768]{1,0:T(8,128)(2,1)S(1)}, bf16[2048,768]{1,0:T(8,128)(2,1)}, u32[]{:S(2)}) copy-start(bf16[2048,768]{1,0:T(8,128)(2,1)} %w_ref.1) | copy-start | bytes 9437188
  267.9 13.8 %collective-permute-start.29 = (bf16[24,2176]{1,0:T(8,128)(2,1)}, bf16[24,2176]{1,0:T(8,128)(2,1)}, u32[]{:S(2)}, u32[]{:S(2)}) collective-permute-start(bf16[24,2176]{1,0:T(8,128)(2,1)} %get-tuple-element.201), channel_id=1, source_target_pairs={{0,2},{1,3},{2,0},{3,1},{4,6},{5,7},{6,4},{7,5},{8,10},{9,11},{10,... | collective-permute-start | bytes 313352 | tf_op jit(solution)/shard_map/ppermute | solution.py:728
  273.2 15.6 %collective-permute-start.32 = (bf16[24,3840]{1,0:T(8,128)(2,1)}, bf16[24,3840]{1,0:T(8,128)(2,1)S(1)}, u32[]{:S(2)}, u32[]{:S(2)}) collective-permute-start(bf16[24,3840]{1,0:T(8,128)(2,1)} %cut.7), channel_id=1, source_target_pairs={{0,8},{1,9},{2,10},{3,11},{4,12},{5,13},{6,14},{7,15},{8,0},{9,1},... | collective-permute-start | bytes 552968 | tf_op jit(solution)/shard_map/ppermute | solution.py:728
  280.9 7.8 %collective-permute-start.31 = (bf16[24,2304]{1,0:T(8,128)(2,1)}, bf16[24,2304]{1,0:T(8,128)(2,1)S(1)}, u32[]{:S(2)}, u32[]{:S(2)}) collective-permute-start(bf16[24,2304]{1,0:T(8,128)(2,1)} %cut.9), channel_id=1, source_target_pairs={{0,8},{1,9},{2,10},{3,11},{4,12},{5,13},{6,14},{7,15},{8,0},{9,1},... | collective-permute-start | bytes 331784 | tf_op jit(solution)/shard_map/ppermute | solution.py:728
  (31 other events, 64.2 us)
